TPU v7x, 32 devices: a whole 2x2x4 slice. The times are simulated.
32 devices in a mesh: seq: 16 (over z, y, core), pair: 2 (over x).
Axes of the slice: x: 2, y: 2, z: 4, core: 2. Of those that a mesh axis runs over, the one named last changes fastest.
Arguments:
- inputs: bfloat16 [8192, 1024], P('seq'), may hold values from -6 to 6
- cotangent: bfloat16 [8192, 1024], P('seq'), may hold values from -6 to 6
- doc_lengths: int32 [1, 8], replicated, may hold values from 1 to 4096, 8192 in all within a row
- pad_counts: int32 [1], replicated, may hold values from 0 to 2047
- ln_gain: float32 [1024], replicated, may hold values from 0.5 to 1.5
- ln_bias: float32 [1024], replicated, may hold values from -4 to 4
- w_first: bfloat16 [2, 1024, 4096], P('pair'), may hold values from -1.5 to 1.5
- b_first: float32 [2, 4096], P('pair'), may hold values from -4 to 4
- w_second: bfloat16 [4096, 1024], replicated, may hold values from -0.09375 to 0.09375
- b_second: float32 [1024], replicated, may hold values from -4 to 4
Outputs:
- outputs: bfloat16 [8192, 1024], P('seq')
- d_inputs: bfloat16 [8192, 1024], P('seq')
- d_gain: float32 [1024], replicated
- d_bias: float32 [1024], replicated
- d_w_first: float32 [2, 1024, 4096], P('pair')
- d_b_first: float32 [2, 4096], P('pair')
- d_w_second: float32 [4096, 1024], P('pair')
- d_b_second: float32 [1024], replicated
Inputs may be any that keep to these rules, and one draw needn't show every extreme that they name: `doc_lengths`: each row holds 8 document lengths that sum to 8192; the longest is exactly 4096.
All inputs are finite; a program needn't handle non-finite values.
Results may differ from a plain program's by a relative error of at most 0.0065.
Values may be sent and summed in bfloat16 or wider, within the bound.
No kernel may reach another device: no remote copies, remote signals or barrier semaphores. Data moves between devices by JAX's collectives and lax.ppermute only.
A program may use at most 576 MiB of HBM per device.

v0:
```python
import jax
import jax.numpy as jnp
from jax import lax
from jax.sharding import PartitionSpec as P

HEADS = 16
HEAD_DIM = 64
D = 1024
FF = 4096
ROT = 16
SEQ_LEN = 8192
DOCS = 8


epsilon = 1e-05
masked_fill = -1e30


def from_behind(block, axis, distance):
    devices = range(lax.axis_size(axis))
    route = [((i - distance) % len(devices), i) for i in devices]
    return lax.ppermute(block, axis, route)


def normalize(tok_block, ln_gain, ln_bias):
    centred = tok_block - jnp.mean(tok_block, axis=1, keepdims=True)
    variance = jnp.mean(centred * centred, axis=1, keepdims=True)
    return centred * lax.rsqrt(variance + epsilon) * ln_gain + ln_bias


def exact_gelu(up_proj):
    return jax.nn.gelu(up_proj, approximate=False)


def angles_for(offsets):
    freq_index = jnp.arange(ROT // 2, dtype=jnp.float32)
    inverse = 10000.0 ** (-2.0 * freq_index / ROT)
    angle_tab = offsets.astype(jnp.float32)[:, None] * inverse[None, :]
    return (jnp.cos(angle_tab)[:, None, :], jnp.sin(angle_tab)[:, None, :])


def rotate(tensor, cos_tab, sine_tab):
    lower_part = tensor[..., : ROT // 2]
    upper_part = tensor[..., ROT // 2 : ROT]
    return jnp.concatenate(
        [
            lower_part * cos_tab - upper_part * sine_tab,
            upper_part * cos_tab + lower_part * sine_tab,
            tensor[..., ROT:],
        ],
        axis=-1,
    )


def unrotate(gradient, cos_tab, sine_tab):
    lower_part = gradient[..., : ROT // 2]
    upper_part = gradient[..., ROT // 2 : ROT]
    return jnp.concatenate(
        [
            lower_part * cos_tab + upper_part * sine_tab,
            upper_part * cos_tab - lower_part * sine_tab,
            gradient[..., ROT:],
        ],
        axis=-1,
    )


def segment_ids(positions, bounds, pad_counts):
    seq_of = positions // SEQ_LEN
    offsets = positions % SEQ_LEN
    chooser = (jnp.arange(bounds.shape[0], dtype=jnp.int32)[:, None] == seq_of[None, :]).astype(
        jnp.int32
    )
    row_bounds = jnp.sum(chooser[:, :, None] * bounds[:, None, :], axis=0)
    row_pads = jnp.sum(chooser * pad_counts[:, None], axis=0)
    doc_ids = jnp.sum((offsets[:, None] >= row_bounds).astype(jnp.int32), axis=1)
    padding = offsets >= SEQ_LEN - row_pads
    return (jnp.where(padding, DOCS, doc_ids), seq_of, padding)


def body(
    inputs,
    cotangent,
    doc_lengths,
    pad_counts,
    ln_gain,
    ln_bias,
    w_first,
    b_first,
    w_second,
    b_second,
):
    tok_rows = inputs.shape[0]
    key_span = SEQ_LEN // tok_rows
    half_ff = w_second.shape[0] // 2
    seq_count = lax.axis_size("seq")
    all_tokens = tok_rows * seq_count
    lead_rows = tok_rows * (key_span // 2)
    seq_place = lax.axis_index("seq")
    branch = lax.axis_index("pair")
    score_scale = HEAD_DIM ** (-0.5)
    widened = inputs.astype(jnp.float32)
    normed, ln_backward = jax.vjp(normalize, widened, ln_gain, ln_bias)
    hidden = normed.astype(jnp.bfloat16)
    weights = w_first[0]
    biases = b_first[0]
    row_index = jnp.arange(tok_rows, dtype=jnp.int32)
    query_pos = (seq_place * tok_rows + row_index - lead_rows) % all_tokens
    cos_tab, sine_tab = angles_for(query_pos % SEQ_LEN)

    def attend_front(operand):
        projected = (
            jnp.dot(hidden, weights[:, : 3 * D], preferred_element_type=jnp.float32)
            + biases[: 3 * D]
        )
        per_head = projected.reshape(tok_rows, 3, HEADS, HEAD_DIM)
        queries = rotate(per_head[:, 0], cos_tab, sine_tab).reshape(tok_rows, D)
        keys_rot = rotate(per_head[:, 1], cos_tab, sine_tab).reshape(tok_rows, D)
        values = per_head[:, 2].reshape(tok_rows, D)
        return (
            queries.astype(jnp.bfloat16),
            jnp.concatenate([keys_rot, values], axis=1).astype(jnp.bfloat16),
        )

    def feed_front(operand):
        return (jnp.zeros((tok_rows, D), jnp.bfloat16), jnp.zeros((tok_rows, 2 * D), jnp.bfloat16))

    queries_low, own_pairs = lax.cond(branch == 0, attend_front, feed_front, 0)
    pieces = [own_pairs]
    for number in range(1, key_span):
        pieces.append(from_behind(own_pairs, "seq", number))
    key_value = jnp.concatenate(pieces, axis=0)
    lags = jnp.arange(key_span, dtype=jnp.int32)
    key_device = (seq_place - lags) % seq_count
    key_pos = (
        (key_device[:, None] * tok_rows + row_index[None, :] - lead_rows) % all_tokens
    ).reshape(-1)

    def attend_main(operand):
        bounds = jnp.cumsum(doc_lengths, axis=1)
        query_seg, query_seq, query_pad = segment_ids(query_pos, bounds, pad_counts)
        key_seg, key_seq, key_pad = segment_ids(key_pos, bounds, pad_counts)
        same_place = key_pos[None, :] == query_pos[:, None]
        allowed = (
            (key_seq[None, :] == query_seq[:, None])
            & (key_seg[None, :] == query_seg[:, None])
            & (key_pos[None, :] <= query_pos[:, None])
            & (jnp.logical_not(key_pad)[None, :] | same_place)
        )
        out_weight = weights[:, 3 * D :]
        d_attended = jnp.einsum(
            "td,fd->tf", cotangent, out_weight, preferred_element_type=jnp.float32
        ).astype(jnp.bfloat16)
        total_keys = key_value.shape[0]
        q_heads = jnp.transpose(queries_low.reshape(tok_rows, HEADS, HEAD_DIM), (1, 0, 2))
        k_heads = jnp.transpose(key_value[:, :D].reshape(total_keys, HEADS, HEAD_DIM), (1, 0, 2))
        v_heads = jnp.transpose(key_value[:, D:].reshape(total_keys, HEADS, HEAD_DIM), (1, 0, 2))
        g_heads = jnp.transpose(d_attended.reshape(tok_rows, HEADS, HEAD_DIM), (1, 0, 2))

        def one_head(members):
            head_query, head_keys, head_values, head_grad = members
            scores = (
                jnp.einsum("qd,kd->qk", head_query, head_keys, preferred_element_type=jnp.float32)
                * score_scale
            )
            masked = jnp.where(allowed, scores, masked_fill)
            exponent = jnp.exp(masked - jnp.max(masked, axis=1, keepdims=True))
            probabilities = exponent / jnp.sum(exponent, axis=1, keepdims=True)
            probs_low = probabilities.astype(jnp.bfloat16)
            attended = jnp.dot(probs_low, head_values, preferred_element_type=jnp.float32).astype(
                jnp.bfloat16
            )
            d_probs = jnp.einsum(
                "qd,kd->qk", head_grad, head_values, preferred_element_type=jnp.float32
            )
            row_dot = jnp.sum(probabilities * d_probs, axis=1, keepdims=True)
            d_scores = (probabilities * (d_probs - row_dot) * score_scale).astype(jnp.bfloat16)
            d_query = jnp.dot(d_scores, head_keys, preferred_element_type=jnp.float32)
            d_keys = jnp.einsum(
                "qk,qd->kd", d_scores, head_query, preferred_element_type=jnp.float32
            )
            d_values = jnp.einsum(
                "qk,qd->kd", probs_low, head_grad, preferred_element_type=jnp.float32
            )
            return (attended, d_query, d_keys, d_values)

        attended, d_query, d_keys, d_values = lax.map(
            one_head, (q_heads, k_heads, v_heads, g_heads)
        )
        attended = jnp.transpose(attended, (1, 0, 2)).reshape(tok_rows, D)
        branch_out = (
            jnp.dot(attended, out_weight, preferred_element_type=jnp.float32) + biases[3 * D :]
        )
        g_out = jnp.einsum("tf,td->fd", attended, cotangent, preferred_element_type=jnp.float32)
        grad_first = jnp.concatenate([jnp.zeros((D, 3 * D), jnp.float32), g_out], axis=1)
        grad_bias = jnp.concatenate(
            [jnp.zeros((3 * D,), jnp.float32), jnp.sum(cotangent, axis=0, dtype=jnp.float32)]
        )
        grad_main = jnp.transpose(d_query, (1, 0, 2)).reshape(tok_rows, D)
        key_grads = jnp.transpose(d_keys, (1, 0, 2)).reshape(total_keys, D)
        value_grads = jnp.transpose(d_values, (1, 0, 2)).reshape(total_keys, D)
        pair_grads = jnp.concatenate([key_grads, value_grads], axis=1).reshape(
            key_span, tok_rows, 2 * D
        )
        return (
            branch_out,
            grad_main,
            pair_grads,
            grad_first,
            grad_bias,
            jnp.zeros((FF, D), jnp.float32),
        )

    def feed_main(operand):
        up_proj = jnp.dot(hidden, weights, preferred_element_type=jnp.float32) + biases
        active, gelu_backward = jax.vjp(exact_gelu, up_proj)
        active_low = active.astype(jnp.bfloat16)
        branch_out = jnp.dot(active_low, w_second, preferred_element_type=jnp.float32) + b_second
        d_active = jnp.einsum("td,fd->tf", cotangent, w_second, preferred_element_type=jnp.float32)
        d_up = gelu_backward(d_active)[0].astype(jnp.bfloat16)
        grad_first = jnp.einsum("td,tf->df", hidden, d_up, preferred_element_type=jnp.float32)
        grad_bias = jnp.sum(d_up, axis=0, dtype=jnp.float32)
        d_hidden = jnp.einsum("tf,df->td", d_up, weights, preferred_element_type=jnp.float32)
        grad_second = jnp.einsum(
            "tf,td->fd", active_low, cotangent, preferred_element_type=jnp.float32
        )
        return (
            branch_out,
            d_hidden,
            jnp.zeros((key_span, tok_rows, 2 * D), jnp.float32),
            grad_first,
            grad_bias,
            grad_second,
        )

    branch_out, grad_main, pair_grads, grad_first, grad_bias, grad_second = lax.cond(
        branch == 0, attend_main, feed_main, 0
    )
    returned = pair_grads[0]
    for number in range(1, key_span):
        returned = returned + from_behind(pair_grads[number], "seq", -number)

    def attend_back(operands):
        main_grad, first_grad, bias_grad = operands
        d_q = unrotate(main_grad.reshape(tok_rows, HEADS, HEAD_DIM), cos_tab, sine_tab).reshape(
            tok_rows, D
        )
        d_k = unrotate(
            returned[:, :D].reshape(tok_rows, HEADS, HEAD_DIM), cos_tab, sine_tab
        ).reshape(tok_rows, D)
        d_projected = jnp.concatenate([d_q, d_k, returned[:, D:]], axis=1).astype(jnp.bfloat16)
        proj_weight = weights[:, : 3 * D]
        g_qkv = jnp.einsum("td,tf->df", hidden, d_projected, preferred_element_type=jnp.float32)
        first_grad = jnp.concatenate([g_qkv, first_grad[:, 3 * D :]], axis=1)
        bias_grad = jnp.concatenate(
            [jnp.sum(d_projected, axis=0, dtype=jnp.float32), bias_grad[3 * D :]]
        )
        d_hidden = jnp.einsum(
            "tf,df->td", d_projected, proj_weight, preferred_element_type=jnp.float32
        )
        return (d_hidden, first_grad, bias_grad)

    def feed_back(operands):
        return operands

    d_hidden, grad_first, grad_bias = lax.cond(
        branch == 0, attend_back, feed_back, (grad_main, grad_first, grad_bias)
    )
    total_out, total_grad, lower_rows = lax.psum(
        (branch_out, d_hidden, grad_second[:half_ff]), "pair"
    )
    outputs = (widened + total_out).astype(jnp.bfloat16)
    d_widened, d_gain, d_bias = ln_backward(total_grad)
    d_inputs = (cotangent.astype(jnp.float32) + d_widened).astype(jnp.bfloat16)
    own_rows = jnp.where(branch == 0, lower_rows, grad_second[half_ff:])
    bias_second = jnp.sum(cotangent, axis=0, dtype=jnp.float32)
    summed = (
        lax.psum_scatter(grad_first, "seq", scatter_dimension=1, tiled=True),
        lax.psum_scatter(own_rows, "seq", scatter_dimension=0, tiled=True),
        lax.psum_scatter(grad_bias, "seq", scatter_dimension=0, tiled=True),
        lax.psum_scatter(bias_second, "seq", scatter_dimension=0, tiled=True),
        lax.psum_scatter(d_gain, "seq", scatter_dimension=0, tiled=True),
        lax.psum_scatter(d_bias, "seq", scatter_dimension=0, tiled=True),
    )
    copied = (
        lax.all_gather(summed[0], "seq", axis=1, tiled=True),
        lax.all_gather(summed[1], "seq", axis=0, tiled=True),
        lax.all_gather(summed[2], "seq", axis=0, tiled=True),
        lax.all_gather(summed[3], "seq", axis=0, tiled=True),
        lax.all_gather(summed[4], "seq", axis=0, tiled=True),
        lax.all_gather(summed[5], "seq", axis=0, tiled=True),
    )
    return (
        outputs,
        d_inputs,
        copied[4],
        copied[5],
        copied[0][None],
        copied[2][None],
        copied[1],
        copied[3],
    )


def solution(mesh):
    in_specs = (
        P("seq", None),
        P("seq", None),
        P(),
        P(),
        P(),
        P(),
        P("pair", None, None),
        P("pair", None),
        P(),
        P(),
    )
    out_specs = (
        P("seq", None),
        P("seq", None),
        P(),
        P(),
        P("pair", None, None),
        P("pair", None),
        P("pair", None),
        P(),
    )
    return jax.shard_map(body, mesh=mesh, in_specs=in_specs, out_specs=out_specs, check_vma=False)
```

profile of v0, /device:TPU:0, one launch (start us, length us, event | category | flops | bytes accessed | tf_op | source)
XLA Modules:
  0.0 4667.0 jit_solution(9757026435528249310)
XLA Ops:
  45.1 43.6 collective-permute-done
  90.5 44.1 collective-permute-start.6
  137.6 311.3 %collective-permute-done.4 = bf16[512,2048]{0,1:T(8,128)(2,1)S(1)} collective-permute-done((bf16[512,2048]{0,1:T(8,128)(2,1)S(1)}, bf16[512,2048]{0,1:T(8,128)(2,1)S(1)}, u32[]{:S(2)}, u32[]{:S(2)}) %collective-permute-start.4) | collective-permute-done | bytes 2097184 | tf_op jit(solution)/shard_map/ppermute | solution.py:22
  453.5 46.6 collective-permute-start.10
  501.6 107.0 %collective-permute-start.11 = (bf16[512,2048]{0,1:T(8,128)(2,1)S(1)}, bf16[512,2048]{0,1:T(8,128)(2,1)S(1)}, u32[]{:S(2)}, u32[]{:S(2)}) collective-permute-start(bf16[512,2048]{0,1:T(8,128)(2,1)S(1)} %get-tuple-element.230), channel_id=1, source_target_pairs={{8,0},{10,2},{12,4},{14,6},{16,8},{18,10},{20,12},{22,14},{24,16},... | collective-permute-start | bytes 6291464 | tf_op jit(solution)/shard_map/ppermute | solution.py:22
  611.7 66.5 %collective-permute-start.13 = (bf16[512,2048]{0,1:T(8,128)(2,1)S(1)}, bf16[512,2048]{0,1:T(8,128)(2,1)S(1)}, u32[]{:S(2)}, u32[]{:S(2)}) collective-permute-start(bf16[512,2048]{0,1:T(8,128)(2,1)S(1)} %get-tuple-element.230), channel_id=1, source_target_pairs={{4,0},{6,2},{8,4},{10,6},{12,8},{14,10},{16,12},{18,14},{20,16},{2... | collective-permute-start | bytes 6291464 | tf_op jit(solution)/shard_map/ppermute | solution.py:22
  679.6 65.4 %collective-permute-start.14 = (bf16[512,2048]{0,1:T(8,128)(2,1)S(1)}, bf16[512,2048]{0,1:T(8,128)(2,1)S(1)}, u32[]{:S(2)}, u32[]{:S(2)}) collective-permute-start(bf16[512,2048]{0,1:T(8,128)(2,1)S(1)} %get-tuple-element.230), channel_id=1, source_target_pairs={{2,0},{4,2},{6,4},{8,6},{10,8},{12,10},{14,12},{16,14},{18,16},{20... | collective-permute-start | bytes 6291464 | tf_op jit(solution)/shard_map/ppermute | solution.py:22
  790.6 1193.6 %conditional.4 = (f32[512,1024]{1,0:T(8,128)S(1)}, f32[512,1024]{0,1:T(8,128)}, f32[16,512,2048]{1,0,2:T(8,128)}, f32[1024,4096]{1,0:T(8,128)}, f32[4096]{0:T(1024)S(1)}, /*index=5*/f32[4096,1024]{1,0:T(8,128)}) conditional(s32[]{:T(128)} %convert_element_type.76, (bf16[512,1024]{1,0:T(8,128)(2,1)}, bf16[1024,4096]{1,0:T(8,128)(2,1)}, ...), branch_computations={%region_4.6_spmd, %region_6.16_spmd.clone.clone} | conditional | flops 25935998976 | bytes 729057216 | solution.py:236
  834.0 1011.8 %while.18 = (s32[]{:T(128)}, bf16[16,512,64]{1,2,0:T(8,128)(2,1)}, f32[16,512,64]{1,2,0:T(8,128)}, f32[16,8192,64]{1,2,0:T(8,128)}, f32[16,8192,64]{1,2,0:T(8,12...) while((s32[]{:T(128)}, bf16[16,512,64]{1,2,0:T(8,128)(2,1)}, ...), condition=%wide.region_14.14_spmd.clone, body=%wide.region_10.13_spmd.clone.sunk | while | flops 3342891520 | bytes 218708240 | solution.py:187
  1917.0 44.9 pad_maximum_fusion.10
  1984.2 57.2 %copy.113 = f32[16,512,2048]{1,2,0:T(8,128)} copy(f32[16,512,2048]{1,0,2:T(8,128)} %get-tuple-element.235) | data formatting | bytes 134217728 | tf_op jit(solution)/shard_map/cond | solution.py:236
  2041.4 40.6 slice_bitcast_fusion.3
  2128.1 49.9 %collective-permute-done.15 = f32[512,2048]{0,1:T(8,128)} collective-permute-done((f32[512,2048]{0,1:T(8,128)}, f32[512,2048]{0,1:T(8,128)}, u32[]{:S(2)}, u32[]{:S(2)}) %collective-permute-start.15) | collective-permute-done | bytes 4194336 | tf_op jit(solution)/shard_map/ppermute | solution.py:22
  2178.0 89.9 %collective-permute-done.16 = f32[512,2048]{0,1:T(8,128)} collective-permute-done((f32[512,2048]{0,1:T(8,128)}, f32[512,2048]{0,1:T(8,128)}, u32[]{:S(2)}, u32[]{:S(2)}) %collective-permute-start.16) | collective-permute-done | bytes 4194336 | tf_op jit(solution)/shard_map/ppermute | solution.py:22
  2267.9 89.9 %collective-permute-done.17 = f32[512,2048]{0,1:T(8,128)} collective-permute-done((f32[512,2048]{0,1:T(8,128)}, f32[512,2048]{0,1:T(8,128)}, u32[]{:S(2)}, u32[]{:S(2)}) %collective-permute-start.17) | collective-permute-done | bytes 4194336 | tf_op jit(solution)/shard_map/ppermute | solution.py:22
  2357.8 38.0 collective-permute-start.22
  2395.8 51.8 %collective-permute-done.18 = f32[512,2048]{0,1:T(8,128)} collective-permute-done((f32[512,2048]{0,1:T(8,128)}, f32[512,2048]{0,1:T(8,128)}, u32[]{:S(2)}, u32[]{:S(2)}) %collective-permute-start.18) | collective-permute-done | bytes 4194336 | tf_op jit(solution)/shard_map/ppermute | solution.py:22
  2447.6 89.9 %collective-permute-done.19 = f32[512,2048]{0,1:T(8,128)} collective-permute-done((f32[512,2048]{0,1:T(8,128)}, f32[512,2048]{0,1:T(8,128)}, u32[]{:S(2)}, u32[]{:S(2)}) %collective-permute-start.19) | collective-permute-done | bytes 4194336 | tf_op jit(solution)/shard_map/ppermute | solution.py:22
  2537.5 89.9 %collective-permute-done.20 = f32[512,2048]{0,1:T(8,128)} collective-permute-done((f32[512,2048]{0,1:T(8,128)}, f32[512,2048]{0,1:T(8,128)}, u32[]{:S(2)}, u32[]{:S(2)}) %collective-permute-start.20) | collective-permute-done | bytes 4194336 | tf_op jit(solution)/shard_map/ppermute | solution.py:22
  2627.4 225.4 %collective-permute-start.25 = (f32[512,2048]{0,1:T(8,128)}, f32[512,2048]{0,1:T(8,128)}, u32[]{:S(2)}, u32[]{:S(2)}) collective-permute-start(f32[512,2048]{0,1:T(8,128)} %get-tuple-element.669), channel_id=1, source_target_pairs={{22,0},{24,2},{26,4},{28,6},{30,8},{0,10},{2,12},{4,14},{6,16},{8,... | collective-permute-start | bytes 12582920 | tf_op jit(solution)/shard_map/ppermute | solution.py:22
  2852.9 261.4 %collective-permute-start.26 = (f32[512,2048]{0,1:T(8,128)}, f32[512,2048]{0,1:T(8,128)}, u32[]{:S(2)}, u32[]{:S(2)}) collective-permute-start(f32[512,2048]{0,1:T(8,128)} %get-tuple-element.668), channel_id=1, source_target_pairs={{24,0},{26,2},{28,4},{30,6},{0,8},{2,10},{4,12},{6,14},{8,16},{10,... | collective-permute-start | bytes 12582920 | tf_op jit(solution)/shard_map/ppermute | solution.py:22
  3114.2 405.1 %collective-permute-done.22 = f32[512,2048]{0,1:T(8,128)} collective-permute-done((f32[512,2048]{0,1:T(8,128)}, f32[512,2048]{0,1:T(8,128)}, u32[]{:S(2)}, u32[]{:S(2)}) %collective-permute-start.22) | collective-permute-done | bytes 4194336 | tf_op jit(solution)/shard_map/ppermute | solution.py:22
  3527.9 41.5 collective-permute-done.27
  3569.4 45.9 collective-permute-done.28
  3615.3 151.4 %conditional.5 = (f32[512,1024]{1,0:T(8,128)S(1)}, f32[4096]{0:T(1024)S(1)}, f32[1024,4096]{1,0:T(8,128)}) conditional(s32[]{:T(128)} %convert_element_type.76, (f32[512,1024]{0,1:T(8,128)}, f32[1024,4096]{1,0:T(8,128)}, f32[4096]{0:T(1024)S(1)}) %tuple.39, (f32[512,1024]{0,1:T(8,128)}, f32[512,1,8]{0,2,1:T(8,128)}, f32[512,1,8]{0,2,1:T(8,128)}, ...), branch_computations={%region_17.18_spmd, %region_18.20_spmd} | conditional | flops 6499599360 | bytes 373903488 | solution.py:266
  3615.5 56.4 %copy.130 = f32[16,512,2048]{1,2,0:T(8,128)} copy(f32[16,512,2048]{1,0,2:T(8,128)} %get-tuple-element.515) | data formatting | bytes 134217728 | tf_op jit(solution)/shard_map
  3768.1 369.6 %all-reduce.14.cloned.1.call-done = (f32[512,1024]{1,0:T(8,128)}, f32[512,1024]{1,0:T(8,128)}, f32[2048,1024]{1,0:T(8,128)}) async-done(((f32[512,1024]{1,0:T(8,128)}, f32[512,1024]{1,0:T(8,128)}, f32[2048,1024]{1,0:T(8,128)}), (f32[512,1024]{1,0:T(8,128)}, f32[512,1024]{1,0:T(8,128)}, f32[2048,1024]{1,0:T(8,128)})) %all-reduce.14.cloned.1.call-update) | async-done | bytes 12582928 | tf_op jit(solution)/shard_map/psum | solution.py:269
  4150.7 102.8 %reduce-scatter.5.cloned.1.call-done = f32[128,1024]{1,0:T(8,128)} async-done(((f32[2048,1024]{1,0:T(8,128)}), f32[128,1024]{1,0:T(8,128)}) %reduce-scatter.5.cloned.1.call-update) | async-done | bytes 524304 | tf_op jit(solution)/shard_map/reduce_scatter | solution.py:279
  4253.5 181.4 %reduce-scatter.3.cloned.1.call-done = f32[1024,256]{1,0:T(8,128)} async-done(((f32[1024,4096]{1,0:T(8,128)}), f32[1024,256]{1,0:T(8,128)}) %reduce-scatter.3.cloned.1.call-update) | async-done | bytes 1048592 | tf_op jit(solution)/shard_map/reduce_scatter | solution.py:278
  4443.3 62.4 %all-reduce.10 = (f32[1024]{0:T(1024)S(1)}, f32[1024]{0:T(1024)S(1)}, f32[1024]{0:T(1024)S(1)}) all-reduce(f32[1024]{0:T(1024)S(1)} %get-tuple-element.584, f32[1024]{0:T(1024)S(1)} %get-tuple-element.586, f32[1024]{0:T(1024)S(1)} %get-tuple-element.680), channel_id=2, replica_groups=mesh['seq'=16,'pair'=2] {'seq'}, use_global_device_ids=true, to_apply=%region_24.25.clone | all-reduce | flops 3072 | bytes 24576
  4506.2 59.8 %all-reduce.9 = (f32[1024]{0:T(1024)}, f32[1024]{0:T(1024)}, f32[4096]{0:T(1024)S(1)}, f32[1024]{0:T(1024)}) all-reduce(f32[1024]{0:T(1024)S(1)} %dynamic-slice_dynamic-update-slice_fusion.2, f32[1024]{0:T(1024)S(1)} %dynamic-slice_dynamic-update-slice_fusion.1, f32[4096]{0:T(1024)S(1)} %copy-done.20, ...), channel_id=1, replica_groups=mesh['seq'=16,'pair'=2] {'seq'}, use_global_device_ids=true, to_apply=%add.2 | all-reduce | flops 7168 | bytes 57344
  4584.2 58.3 %all-gather.4.cloned.1.call-done = f32[1024,4096]{1,0:T(8,128)} async-done(((f32[1024,256]{1,0:T(8,128)}), f32[1024,4096]{1,0:T(8,128)}) %all-gather.4.cloned.1.call-update) | async-done | bytes 16777232 | tf_op jit(solution)/shard_map/all_gather | solution.py:286
  (503 shorter events, 1460.8 us)
Async XLA Ops:
  7.2 4130.5 %all-reduce.14.cloned.1.call-start = ((), (), s32[]{:S(2)}) async-start(), calls=%async_computation.6 | async-start | bytes 25165824 | tf_op jit(solution)/shard_map/psum | solution.py:269
  40.9 93.8 %collective-permute-start.2 = (bf16[512,2048]{0,1:T(8,128)(2,1)S(1)}, bf16[512,2048]{0,1:T(8,128)(2,1)S(1)}, u32[]{:S(2)}, u32[]{:S(2)}) collective-permute-start(bf16[512,2048]{0,1:T(8,128)(2,1)S(1)} %get-tuple-element.230), channel_id=1, source_target_pairs={{26,0},{28,2},{30,4},{0,6},{2,8},{4,10},{6,12},{8,14},{10,16},{12,... | collective-permute-start | bytes 6291464 | tf_op jit(solution)/shard_map/ppermute | solution.py:22
  43.3 93.2 %collective-permute-start.3 = (bf16[512,2048]{0,1:T(8,128)(2,1)S(1)}, bf16[512,2048]{0,1:T(8,128)(2,1)S(1)}, u32[]{:S(2)}, u32[]{:S(2)}) collective-permute-start(bf16[512,2048]{0,1:T(8,128)(2,1)S(1)} %get-tuple-element.230), channel_id=1, source_target_pairs={{24,0},{26,2},{28,4},{30,6},{0,8},{2,10},{4,12},{6,14},{8,16},{10,... | collective-permute-start | bytes 6291464 | tf_op jit(solution)/shard_map/ppermute | solution.py:22
  44.9 404.0 %collective-permute-start.4 = (bf16[512,2048]{0,1:T(8,128)(2,1)S(1)}, bf16[512,2048]{0,1:T(8,128)(2,1)S(1)}, u32[]{:S(2)}, u32[]{:S(2)}) collective-permute-start(bf16[512,2048]{0,1:T(8,128)(2,1)S(1)} %get-tuple-element.230), channel_id=1, source_target_pairs={{22,0},{24,2},{26,4},{28,6},{30,8},{0,10},{2,12},{4,14},{6,16},{8,... | collective-permute-start | bytes 6291464 | tf_op jit(solution)/shard_map/ppermute | solution.py:22
  88.7 364.8 %collective-permute-start.5 = (bf16[512,2048]{0,1:T(8,128)(2,1)S(1)}, bf16[512,2048]{0,1:T(8,128)(2,1)S(1)}, u32[]{:S(2)}, u32[]{:S(2)}) collective-permute-start(bf16[512,2048]{0,1:T(8,128)(2,1)S(1)} %get-tuple-element.230), channel_id=1, source_target_pairs={{20,0},{22,2},{24,4},{26,6},{28,8},{30,10},{0,12},{2,14},{4,16},{6... | collective-permute-start | bytes 6291464 | tf_op jit(solution)/shard_map/ppermute | solution.py:22
  90.5 411.1 %collective-permute-start.6 = (bf16[512,2048]{0,1:T(8,128)(2,1)S(1)}, bf16[512,2048]{0,1:T(8,128)(2,1)S(1)}, u32[]{:S(2)}, u32[]{:S(2)}) collective-permute-start(bf16[512,2048]{0,1:T(8,128)(2,1)S(1)} %get-tuple-element.230), channel_id=1, source_target_pairs={{18,0},{20,2},{22,4},{24,6},{26,8},{28,10},{30,12},{0,14},{2,16},{... | collective-permute-start | bytes 6291464 | tf_op jit(solution)/shard_map/ppermute | solution.py:22
  134.7 475.3 %collective-permute-start.7 = (bf16[512,2048]{0,1:T(8,128)(2,1)S(1)}, bf16[512,2048]{0,1:T(8,128)(2,1)S(1)}, u32[]{:S(2)}, u32[]{:S(2)}) collective-permute-start(bf16[512,2048]{0,1:T(8,128)(2,1)S(1)} %get-tuple-element.230), channel_id=1, source_target_pairs={{16,0},{18,2},{20,4},{22,6},{24,8},{26,10},{28,12},{30,14},{0,16},... | collective-permute-start | bytes 6291464 | tf_op jit(solution)/shard_map/ppermute | solution.py:22
  136.6 475.1 %collective-permute-start.8 = (bf16[512,2048]{0,1:T(8,128)(2,1)S(1)}, bf16[512,2048]{0,1:T(8,128)(2,1)S(1)}, u32[]{:S(2)}, u32[]{:S(2)}) collective-permute-start(bf16[512,2048]{0,1:T(8,128)(2,1)S(1)} %get-tuple-element.230), channel_id=1, source_target_pairs={{14,0},{16,2},{18,4},{20,6},{22,8},{24,10},{26,12},{28,14},{30,16}... | collective-permute-start | bytes 6291464 | tf_op jit(solution)/shard_map/ppermute | solution.py:22
  449.0 230.7 %collective-permute-start.9 = (bf16[512,2048]{0,1:T(8,128)(2,1)S(1)}, bf16[512,2048]{0,1:T(8,128)(2,1)S(1)}, u32[]{:S(2)}, u32[]{:S(2)}) collective-permute-start(bf16[512,2048]{0,1:T(8,128)(2,1)S(1)} %get-tuple-element.230), channel_id=1, source_target_pairs={{12,0},{14,2},{16,4},{18,6},{20,8},{22,10},{24,12},{26,14},{28,16}... | collective-permute-start | bytes 6291464 | tf_op jit(solution)/shard_map/ppermute | solution.py:22
  453.5 297.3 %collective-permute-start.10 = (bf16[512,2048]{0,1:T(8,128)(2,1)S(1)}, bf16[512,2048]{0,1:T(8,128)(2,1)S(1)}, u32[]{:S(2)}, u32[]{:S(2)}) collective-permute-start(bf16[512,2048]{0,1:T(8,128)(2,1)S(1)} %get-tuple-element.230), channel_id=1, source_target_pairs={{10,0},{12,2},{14,4},{16,6},{18,8},{20,10},{22,12},{24,14},{26,16}... | collective-permute-start | bytes 6291464 | tf_op jit(solution)/shard_map/ppermute | solution.py:22
  501.6 250.7 %collective-permute-start.11 = (bf16[512,2048]{0,1:T(8,128)(2,1)S(1)}, bf16[512,2048]{0,1:T(8,128)(2,1)S(1)}, u32[]{:S(2)}, u32[]{:S(2)}) collective-permute-start(bf16[512,2048]{0,1:T(8,128)(2,1)S(1)} %get-tuple-element.230), channel_id=1, source_target_pairs={{8,0},{10,2},{12,4},{14,6},{16,8},{18,10},{20,12},{22,14},{24,16},... | collective-permute-start | bytes 6291464 | tf_op jit(solution)/shard_map/ppermute | solution.py:22
  610.0 143.7 %collective-permute-start.12 = (bf16[512,2048]{0,1:T(8,128)(2,1)S(1)}, bf16[512,2048]{0,1:T(8,128)(2,1)S(1)}, u32[]{:S(2)}, u32[]{:S(2)}) collective-permute-start(bf16[512,2048]{0,1:T(8,128)(2,1)S(1)} %get-tuple-element.230), channel_id=1, source_target_pairs={{6,0},{8,2},{10,4},{12,6},{14,8},{16,10},{18,12},{20,14},{22,16},{... | collective-permute-start | bytes 6291464 | tf_op jit(solution)/shard_map/ppermute | solution.py:22
  611.7 156.4 %collective-permute-start.13 = (bf16[512,2048]{0,1:T(8,128)(2,1)S(1)}, bf16[512,2048]{0,1:T(8,128)(2,1)S(1)}, u32[]{:S(2)}, u32[]{:S(2)}) collective-permute-start(bf16[512,2048]{0,1:T(8,128)(2,1)S(1)} %get-tuple-element.230), channel_id=1, source_target_pairs={{4,0},{6,2},{8,4},{10,6},{12,8},{14,10},{16,12},{18,14},{20,16},{2... | collective-permute-start | bytes 6291464 | tf_op jit(solution)/shard_map/ppermute | solution.py:22
  679.6 109.4 %collective-permute-start.14 = (bf16[512,2048]{0,1:T(8,128)(2,1)S(1)}, bf16[512,2048]{0,1:T(8,128)(2,1)S(1)}, u32[]{:S(2)}, u32[]{:S(2)}) collective-permute-start(bf16[512,2048]{0,1:T(8,128)(2,1)S(1)} %get-tuple-element.230), channel_id=1, source_target_pairs={{2,0},{4,2},{6,4},{8,6},{10,8},{12,10},{14,12},{16,14},{18,16},{20... | collective-permute-start | bytes 6291464 | tf_op jit(solution)/shard_map/ppermute | solution.py:22
  2082.0 96.0 %collective-permute-start.15 = (f32[512,2048]{0,1:T(8,128)}, f32[512,2048]{0,1:T(8,128)}, u32[]{:S(2)}, u32[]{:S(2)}) collective-permute-start(f32[512,2048]{0,1:T(8,128)} %get-tuple-element.679), channel_id=1, source_target_pairs={{2,0},{4,2},{6,4},{8,6},{10,8},{12,10},{14,12},{16,14},{18,16},{20... | collective-permute-start | bytes 12582920 | tf_op jit(solution)/shard_map/ppermute | solution.py:22
  2086.7 181.2 %collective-permute-start.16 = (f32[512,2048]{0,1:T(8,128)}, f32[512,2048]{0,1:T(8,128)}, u32[]{:S(2)}, u32[]{:S(2)}) collective-permute-start(f32[512,2048]{0,1:T(8,128)} %get-tuple-element.678), channel_id=1, source_target_pairs={{4,0},{6,2},{8,4},{10,6},{12,8},{14,10},{16,12},{18,14},{20,16},{2... | collective-permute-start | bytes 12582920 | tf_op jit(solution)/shard_map/ppermute | solution.py:22
  2086.7 271.1 %collective-permute-start.17 = (f32[512,2048]{0,1:T(8,128)}, f32[512,2048]{0,1:T(8,128)}, u32[]{:S(2)}, u32[]{:S(2)}) collective-permute-start(f32[512,2048]{0,1:T(8,128)} %get-tuple-element.677), channel_id=1, source_target_pairs={{6,0},{8,2},{10,4},{12,6},{14,8},{16,10},{18,12},{20,14},{22,16},{... | collective-permute-start | bytes 12582920 | tf_op jit(solution)/shard_map/ppermute | solution.py:22
  2105.9 341.7 %collective-permute-start.18 = (f32[512,2048]{0,1:T(8,128)}, f32[512,2048]{0,1:T(8,128)}, u32[]{:S(2)}, u32[]{:S(2)}) collective-permute-start(f32[512,2048]{0,1:T(8,128)} %get-tuple-element.676), channel_id=1, source_target_pairs={{8,0},{10,2},{12,4},{14,6},{16,8},{18,10},{20,12},{22,14},{24,16},... | collective-permute-start | bytes 12582920 | tf_op jit(solution)/shard_map/ppermute | solution.py:22
  2126.1 411.5 %collective-permute-start.19 = (f32[512,2048]{0,1:T(8,128)}, f32[512,2048]{0,1:T(8,128)}, u32[]{:S(2)}, u32[]{:S(2)}) collective-permute-start(f32[512,2048]{0,1:T(8,128)} %get-tuple-element.675), channel_id=1, source_target_pairs={{10,0},{12,2},{14,4},{16,6},{18,8},{20,10},{22,12},{24,14},{26,16}... | collective-permute-start | bytes 12582920 | tf_op jit(solution)/shard_map/ppermute | solution.py:22
  2178.0 449.4 %collective-permute-start.20 = (f32[512,2048]{0,1:T(8,128)}, f32[512,2048]{0,1:T(8,128)}, u32[]{:S(2)}, u32[]{:S(2)}) collective-permute-start(f32[512,2048]{0,1:T(8,128)} %get-tuple-element.674), channel_id=1, source_target_pairs={{12,0},{14,2},{16,4},{18,6},{20,8},{22,10},{24,12},{26,14},{28,16}... | collective-permute-start | bytes 12582920 | tf_op jit(solution)/shard_map/ppermute | solution.py:22
  2267.9 585.0 %collective-permute-start.21 = (f32[512,2048]{0,1:T(8,128)}, f32[512,2048]{0,1:T(8,128)}, u32[]{:S(2)}, u32[]{:S(2)}) collective-permute-start(f32[512,2048]{0,1:T(8,128)} %get-tuple-element.673), channel_id=1, source_target_pairs={{14,0},{16,2},{18,4},{20,6},{22,8},{24,10},{26,12},{28,14},{30,16}... | collective-permute-start | bytes 12582920 | tf_op jit(solution)/shard_map/ppermute | solution.py:22
  2357.8 1161.6 %collective-permute-start.22 = (f32[512,2048]{0,1:T(8,128)}, f32[512,2048]{0,1:T(8,128)}, u32[]{:S(2)}, u32[]{:S(2)}) collective-permute-start(f32[512,2048]{0,1:T(8,128)} %get-tuple-element.672), channel_id=1, source_target_pairs={{16,0},{18,2},{20,4},{22,6},{24,8},{26,10},{28,12},{30,14},{0,16},... | collective-permute-start | bytes 12582920 | tf_op jit(solution)/shard_map/ppermute | solution.py:22
  2447.6 1071.7 %collective-permute-start.23 = (f32[512,2048]{0,1:T(8,128)}, f32[512,2048]{0,1:T(8,128)}, u32[]{:S(2)}, u32[]{:S(2)}) collective-permute-start(f32[512,2048]{0,1:T(8,128)} %get-tuple-element.671), channel_id=1, source_target_pairs={{18,0},{20,2},{22,4},{24,6},{26,8},{28,10},{30,12},{0,14},{2,16},{... | collective-permute-start | bytes 12582920 | tf_op jit(solution)/shard_map/ppermute | solution.py:22
  2537.5 981.8 %collective-permute-start.24 = (f32[512,2048]{0,1:T(8,128)}, f32[512,2048]{0,1:T(8,128)}, u32[]{:S(2)}, u32[]{:S(2)}) collective-permute-start(f32[512,2048]{0,1:T(8,128)} %get-tuple-element.670), channel_id=1, source_target_pairs={{20,0},{22,2},{24,4},{26,6},{28,8},{30,10},{0,12},{2,14},{4,16},{6... | collective-permute-start | bytes 12582920 | tf_op jit(solution)/shard_map/ppermute | solution.py:22
  2627.4 900.5 %collective-permute-start.25 = (f32[512,2048]{0,1:T(8,128)}, f32[512,2048]{0,1:T(8,128)}, u32[]{:S(2)}, u32[]{:S(2)}) collective-permute-start(f32[512,2048]{0,1:T(8,128)} %get-tuple-element.669), channel_id=1, source_target_pairs={{22,0},{24,2},{26,4},{28,6},{30,8},{0,10},{2,12},{4,14},{6,16},{8,... | collective-permute-start | bytes 12582920 | tf_op jit(solution)/shard_map/ppermute | solution.py:22
  2852.9 675.0 %collective-permute-start.26 = (f32[512,2048]{0,1:T(8,128)}, f32[512,2048]{0,1:T(8,128)}, u32[]{:S(2)}, u32[]{:S(2)}) collective-permute-start(f32[512,2048]{0,1:T(8,128)} %get-tuple-element.668), channel_id=1, source_target_pairs={{24,0},{26,2},{28,4},{30,6},{0,8},{2,10},{4,12},{6,14},{8,16},{10,... | collective-permute-start | bytes 12582920 | tf_op jit(solution)/shard_map/ppermute | solution.py:22
  3519.3 96.0 %collective-permute-start.28 = (f32[512,2048]{0,1:T(8,128)}, f32[512,2048]{0,1:T(8,128)}, u32[]{:S(2)}, u32[]{:S(2)}) collective-permute-start(f32[512,2048]{0,1:T(8,128)} %get-tuple-element.666), channel_id=1, source_target_pairs={{28,0},{30,2},{0,4},{2,6},{4,8},{6,10},{8,12},{10,14},{12,16},{14,... | collective-permute-start | bytes 12582920 | tf_op jit(solution)/shard_map/ppermute | solution.py:22
  3519.4 95.9 %collective-permute-start.29 = (f32[512,2048]{0,1:T(8,128)}, f32[512,2048]{0,1:T(8,128)}, u32[]{:S(2)}, u32[]{:S(2)}) collective-permute-start(f32[512,2048]{0,1:T(8,128)} %get-tuple-element.665), channel_id=1, source_target_pairs={{30,0},{0,2},{2,4},{4,6},{6,8},{8,10},{10,12},{12,14},{14,16},{16,... | collective-permute-start | bytes 12582920 | tf_op jit(solution)/shard_map/ppermute | solution.py:22
  3768.0 485.4 %reduce-scatter.5.cloned.1.call-start = ((), (), s32[]{:S(2)}) async-start(), calls=%async_computation.4 | async-start | bytes 8912896 | tf_op jit(solution)/shard_map/reduce_scatter | solution.py:279
  4149.9 285.1 %reduce-scatter.3.cloned.1.call-start = ((), (), s32[]{:S(2)}) async-start(), calls=%async_computation.2 | async-start | bytes 17825792 | tf_op jit(solution)/shard_map/reduce_scatter | solution.py:278
  4150.6 433.5 %all-gather.6.cloned.1.call-start = ((), (), s32[]{:S(2)}) async-start(), calls=%async_computation.5 | async-start | bytes 8912896 | tf_op jit(solution)/shard_map/all_gather | solution.py:287
  4253.5 389.0 %all-gather.4.cloned.1.call-start = ((), (), s32[]{:S(2)}) async-start(), calls=%async_computation.3 | async-start | bytes 17825792 | tf_op jit(solution)/shard_map/all_gather | solution.py:286
  (103 other events, 4540.8 us)
Sparse Core Ops, SparseCore 0:
  3768.2 369.4 all-reduce.13
  4150.0 103.4 reduce-scatter.4
  4258.1 176.7 reduce-scatter.2
  4437.0 74.3 all-gather.5
  4513.4 129.0 all-gather.3
where the time goes:
time: 4680 us; the launch traced here: 4670 us
  waiting for transfers between devices  2060 us (44%)
  starting transfers between devices  912 us (19%)
  matrix products  782 us (17%)
  other arithmetic  376 us (8%)
  local copies, waits for them, and re-layouts  369 us (8%)
  blocking collectives  140 us (3%)
    ppermute x30, waiting for transfers between devices, from_behind(): return lax.ppermute(block, axis, route)  1340 us
    ppermute x30, starting transfers between devices, from_behind(): return lax.ppermute(block, axis, route)  911 us
    psum x1, waiting for transfers between devices, body(): lax.psum((branch_out, d_hidden, grad_second[:half_ff]), 'pair')  370 us
    dot_general x16, matrix products, one_head(): jnp.einsum('qd,kd->qk', head_query, head_keys, preferred_element_type=jnp...  213 us
    reduce_scatter x1, waiting for transfers between devices, body(): lax.psum_scatter(grad_first, 'seq', scatter_dimension=1, tiled=True)  181 us
    dot_general x16, matrix products, one_head(): jnp.einsum('qk,qd->kd', probs_low, head_grad, preferred_element_type=jnp....  165 us
    dot_general x16, matrix products, one_head(): jnp.einsum('qd,kd->qk', head_grad, head_values, preferred_element_type=jn...  150 us
    convert_element_type x16, other arithmetic, one_head(): (probabilities * (d_probs - row_dot) * score_scale).astype(jnp.bfloat16)  134 us
  transfers between devices with their start and end apart: 35, of which 18 were waited for; matrix products, arithmetic and copies ran while one was open for 1% of the time, Pallas kernels for 0%

commit v1 on v0

v1 whole, which is shorter than its diff:
```python
import functools

import jax
import jax.numpy as jnp
from jax import lax
from jax.experimental import pallas as pl
from jax.experimental.pallas import tpu as pltpu
from jax.sharding import PartitionSpec as P

HEADS = 16
HEAD_DIM = 64
D = 1024
FF = 4096
ROT = 16
SEQ_LEN = 8192
DOCS = 8

BQ = 256
BK = 512
epsilon = 1e-05
masked_fill = -1e30
bf16 = jnp.bfloat16
f32 = jnp.float32
VMEM_LIMIT = 60 * 1024 * 1024


def mm(left, right, dims):
    return lax.dot_general(left, right, (dims, ((), ())), preferred_element_type=f32)


def rotation_tables(positions, period):
    lane = lax.broadcasted_iota(jnp.int32, (positions.shape[0], 128), 1) % period
    inverse = 10000.0 ** (-2.0 * (lane % (ROT // 2)).astype(f32) / ROT)
    angle = positions.astype(f32)[:, None] * inverse
    cos_tab = jnp.where(lane < ROT, jnp.cos(angle), 1.0)
    sine = jnp.sin(angle)
    sine_tab = jnp.where(lane < ROT // 2, -sine, jnp.where(lane < ROT, sine, 0.0))
    return cos_tab, sine_tab


def turn(block, cos_tab, sine_tab, lane):
    from_left = pltpu.roll(block, 8, 1)
    from_right = pltpu.roll(block, 120, 1)
    return block * cos_tab + jnp.where(lane % 64 < 8, from_right, from_left) * sine_tab


def project_kernel(h_ref, g_ref, wq, wk, wv, wo, bq, bk, bv, c_ref, s_ref, out):
    rows = h_ref.shape[0]
    lane = lax.broadcasted_iota(jnp.int32, (rows, 128), 1)
    low = lane < 64
    hidden = h_ref[...]
    q_all = mm(hidden, wq[...], ((1,), (0,))) + bq[...]
    k_all = mm(hidden, wk[...], ((1,), (0,))) + bk[...]
    v_all = mm(hidden, wv[...], ((1,), (0,))) + bv[...]
    g_all = mm(g_ref[...], wo[...], ((1,), (1,)))
    cos_tab = c_ref[...]
    sine_tab = s_ref[...]
    for pair in range(2):
        cut = slice(128 * pair, 128 * pair + 128)
        q = turn(q_all[:, cut], cos_tab, sine_tab, lane)
        k = turn(k_all[:, cut], cos_tab, sine_tab, lane)
        v = v_all[:, cut]
        g = g_all[:, cut]
        out[2 * pair, 0] = jnp.where(low, q, pltpu.roll(g, 64, 1)).astype(bf16)
        out[2 * pair, 1] = jnp.where(low, k, pltpu.roll(v, 64, 1)).astype(bf16)
        out[2 * pair + 1, 0] = jnp.where(low, pltpu.roll(q, 64, 1), g).astype(bf16)
        out[2 * pair + 1, 1] = jnp.where(low, pltpu.roll(k, 64, 1), v).astype(bf16)


def project(hidden, cotangent, weights, biases, cos_tab, sine_tab):
    rows = hidden.shape[0]
    whole = lambda i: (0, 0)
    steps = HEADS // 4
    return pl.pallas_call(
        project_kernel,
        grid=(steps,),
        in_specs=[
            pl.BlockSpec((rows, D), whole),
            pl.BlockSpec((rows, D), whole),
            pl.BlockSpec((D, 256), lambda i: (0, i)),
            pl.BlockSpec((D, 256), lambda i: (0, i + steps)),
            pl.BlockSpec((D, 256), lambda i: (0, i + 2 * steps)),
            pl.BlockSpec((256, D), lambda i: (i, 3)),
            pl.BlockSpec((1, 256), lambda i: (0, i)),
            pl.BlockSpec((1, 256), lambda i: (0, i + steps)),
            pl.BlockSpec((1, 256), lambda i: (0, i + 2 * steps)),
            pl.BlockSpec((rows, 128), whole),
            pl.BlockSpec((rows, 128), whole),
        ],
        out_specs=pl.BlockSpec((4, 2, rows, 128), lambda i: (i, 0, 0, 0)),
        out_shape=jax.ShapeDtypeStruct((HEADS, 2, rows, 128), bf16),
        compiler_params=pltpu.CompilerParams(vmem_limit_bytes=VMEM_LIMIT),
        name="project",
    )(hidden, cotangent, weights, weights, weights, weights, biases, biases, biases,
      cos_tab, sine_tab)


def attend_kernel(scal, lo_ref, x_ref, kvp_ref, dq_ref, own_ref, send_ref,
                  kv_s, kvt_s, s_buf, p_buf, acc_s):
    members, _, rows, _ = x_ref.shape
    place = scal[0]
    parity = scal[1]
    scale = HEAD_DIM ** (-0.5)
    to_two = scale * 1.4426950408889634

    for m in range(members):
        d = (place - m + members) % members
        at_own = pl.multiple_of((2 * m + parity) * rows, rows)
        at_other = pl.multiple_of((2 * m + 1 - parity) * rows, rows)
        kv_s[pl.ds(at_own, rows), :] = x_ref[d, 1]
        kv_s[pl.ds(at_other, rows), :] = kvp_ref[d]
    acc_s[...] = jnp.zeros_like(acc_s)

    def transpose_step(b, carry):
        at = pl.multiple_of(b * 256, 256)
        kvt_s[:, pl.ds(at, 256)] = kv_s[pl.ds(at, 256), :].astype(f32).T.astype(bf16)
        return carry

    lax.fori_loop(0, kv_s.shape[0] // 256, transpose_step, 0)

    per = rows // BQ
    lane = lax.broadcasted_iota(jnp.int32, (BQ, 128), 1)
    key_iota = lax.broadcasted_iota(jnp.int32, (BK, BQ), 0)
    query_iota = lax.broadcasted_iota(jnp.int32, (1, BQ), 1)

    def query_block(i, carry):
        m = i // per
        part = i % per
        d = (place - m + members) % members
        off = pl.multiple_of(part * BQ, BQ)
        first = (2 * m + parity) * rows + off
        qd = x_ref[d, 0, pl.ds(off, BQ), :]
        zero = jnp.zeros_like(qd)
        qz = jnp.where(lane < 64, qd, zero)
        dz = jnp.where(lane < 64, zero, qd)
        both = jnp.concatenate([qz, dz], axis=0)
        kb0 = scal[2 + i] // BK
        kb1 = (first + BQ - 1) // BK + 1
        qpos = first + query_iota
        lo = lo_ref[pl.ds(i, 1), :]

        def scores_step(kb, mx):
            at = pl.multiple_of(kb * BK, BK)
            r = mm(kv_s[pl.ds(at, BK), :], both, ((1,), (1,)))
            kpos = at + key_iota
            s = jnp.where((kpos <= qpos) & (kpos >= lo), r[:, :BQ], masked_fill)
            s_buf[pl.ds(at, BK), :] = s
            p_buf[pl.ds(at, BK), :] = r[:, BQ:]
            return jnp.maximum(mx, jnp.max(s.reshape(BK // 8, 8, BQ), axis=0))

        mx = lax.fori_loop(kb0, kb1, scores_step, jnp.full((8, BQ), masked_fill, f32))
        top = jnp.max(mx, axis=0, keepdims=True)

        def exp_step(kb, sums):
            total, dots = sums
            at = pl.multiple_of(kb * BK, BK)
            e = jnp.exp2((s_buf[pl.ds(at, BK), :] - top) * to_two)
            s_buf[pl.ds(at, BK), :] = e
            w = e * p_buf[pl.ds(at, BK), :]
            return (total + jnp.sum(e.reshape(BK // 8, 8, BQ), axis=0),
                    dots + jnp.sum(w.reshape(BK // 8, 8, BQ), axis=0))

        zeros = jnp.zeros((8, BQ), f32)
        total, dots = lax.fori_loop(kb0, kb1, exp_step, (zeros, zeros))
        inv = 1.0 / jnp.sum(total, axis=0, keepdims=True)
        row_dot = jnp.sum(dots, axis=0, keepdims=True) * inv

        def grad_step(kb, outs):
            dq_t, at_t = outs
            at = pl.multiple_of(kb * BK, BK)
            p = s_buf[pl.ds(at, BK), :] * inv
            ds = p * (p_buf[pl.ds(at, BK), :] - row_dot)
            p_low = p.astype(bf16)
            ds_low = ds.astype(bf16)
            joined = jnp.concatenate([ds_low, p_low], axis=1)
            acc_s[pl.ds(at, BK), :] += mm(joined, both, ((1,), (0,)))
            dq_t = dq_t + mm(kvt_s[0:64, pl.ds(at, BK)], ds_low, ((1,), (0,)))
            at_t = at_t + mm(kvt_s[64:128, pl.ds(at, BK)], p_low, ((1,), (0,)))
            return dq_t, at_t

        wide = jnp.zeros((64, BQ), f32)
        dq_t, at_t = lax.fori_loop(kb0, kb1, grad_step, (wide, wide))
        dq_ref[m, pl.ds(off, BQ), :] = jnp.concatenate([dq_t, at_t], axis=0).T
        return carry

    lax.fori_loop(0, members * per, query_block, 0)

    for m in range(members):
        at_own = pl.multiple_of((2 * m + parity) * rows, rows)
        at_other = pl.multiple_of((2 * m + 1 - parity) * rows, rows)
        own_ref[m] = acc_s[pl.ds(at_own, rows), :]
        send_ref[m] = acc_s[pl.ds(at_other, rows), :]


def attend(scal, lo, x, kv_other):
    members, _, rows, _ = x.shape
    total = 2 * members * rows
    piece = jax.ShapeDtypeStruct((members, rows, 128), f32)
    vmem = pl.BlockSpec(memory_space=pltpu.VMEM)
    return pl.pallas_call(
        attend_kernel,
        in_specs=[pl.BlockSpec(memory_space=pltpu.SMEM), vmem, vmem, vmem],
        out_specs=[vmem, vmem, vmem],
        out_shape=[piece, piece, piece],
        scratch_shapes=[
            pltpu.VMEM((total, 128), bf16),
            pltpu.VMEM((128, total), bf16),
            pltpu.VMEM((total, BQ), f32),
            pltpu.VMEM((total, BQ), f32),
            pltpu.VMEM((total, 128), f32),
        ],
        compiler_params=pltpu.CompilerParams(vmem_limit_bytes=VMEM_LIMIT),
        name="attend",
    )(scal, lo, x, kv_other)


def join_kernel(dq_ref, own_ref, got_ref, c_ref, s_ref, out):
    rows = dq_ref.shape[1]
    lane = lax.broadcasted_iota(jnp.int32, (rows, 128), 1)
    scale = jnp.where(lane < 64, HEAD_DIM ** (-0.5), 1.0)
    cos_tab = c_ref[0]
    sine_tab = -s_ref[0]
    out[0, 0] = turn(dq_ref[0] * scale, cos_tab, sine_tab, lane).astype(bf16)
    out[0, 1] = turn((own_ref[0] + got_ref[0]) * scale, cos_tab, sine_tab, lane).astype(bf16)


def join(dq, own, got, cos_tab, sine_tab):
    members, rows, _ = dq.shape
    one = pl.BlockSpec((1, rows, 128), lambda m: (m, 0, 0))
    return pl.pallas_call(
        join_kernel,
        grid=(members,),
        in_specs=[one] * 5,
        out_specs=pl.BlockSpec((1, 2, rows, 128), lambda m: (m, 0, 0, 0)),
        out_shape=jax.ShapeDtypeStruct((members, 2, rows, 128), bf16),
        name="join",
    )(dq, own, got, cos_tab, sine_tab)


def gather_kernel(scal, x_ref, proj_ref, att_ref):
    members, _, rows, _ = x_ref.shape
    place = scal[0]
    low = lax.broadcasted_iota(jnp.int32, (rows, 128), 1) < 64
    half = members * 64
    for pair in range(members // 2):
        d0 = (place - 2 * pair + members) % members
        d1 = (place - 2 * pair - 1 + members) % members
        for side in range(2):
            a = x_ref[d0, side].astype(f32)
            b = x_ref[d1, side].astype(f32)
            front = jnp.where(low, a, pltpu.roll(b, 64, 1)).astype(bf16)
            back = jnp.where(low, pltpu.roll(a, 64, 1), b).astype(bf16)
            cut = slice(128 * pair, 128 * pair + 128)
            if side == 0:
                proj_ref[:, cut] = front
                att_ref[:, cut] = back
            else:
                proj_ref[:, half + 128 * pair : half + 128 * pair + 128] = front
                proj_ref[:, 2 * half + 128 * pair : 2 * half + 128 * pair + 128] = back


def gather_heads(scal, x):
    members, _, rows, _ = x.shape
    vmem = pl.BlockSpec(memory_space=pltpu.VMEM)
    return pl.pallas_call(
        gather_kernel,
        in_specs=[pl.BlockSpec(memory_space=pltpu.SMEM), vmem],
        out_specs=[vmem, vmem],
        out_shape=[
            jax.ShapeDtypeStruct((rows, 3 * members * 64), bf16),
            jax.ShapeDtypeStruct((rows, members * 64), bf16),
        ],
        compiler_params=pltpu.CompilerParams(vmem_limit_bytes=VMEM_LIMIT),
        name="gather_heads",
    )(scal, x)


def body(inputs, cotangent, doc_lengths, pad_counts, ln_gain, ln_bias,
         w_first, b_first, w_second, b_second):
    rows = inputs.shape[0]
    count = lax.axis_size("seq")
    span = SEQ_LEN // rows
    lead = span // 2
    members = span // 2
    half = members * HEAD_DIM
    half_ff = FF // 2
    seq_at = lax.axis_index("seq")
    branch = lax.axis_index("pair")
    on_first = branch == 0
    block_at = (seq_at - lead) % count
    seq_no = block_at // span
    block_in = block_at % span
    place = block_in // 2
    parity = block_in % 2

    def device_of(block):
        return (block + lead) % count

    def seq_swap(bit):
        return [(i, i ^ bit) for i in range(count)]

    core_swap = [(device_of(b), device_of(b ^ 1)) for b in range(count)]

    weights = w_first[0]
    ids = jnp.arange(rows, dtype=jnp.int32)

    widened = inputs.astype(f32)
    centred = widened - jnp.mean(widened, axis=1, keepdims=True)
    rstd = lax.rsqrt(jnp.mean(centred * centred, axis=1, keepdims=True) + epsilon)
    hidden = (centred * rstd * ln_gain + ln_bias).astype(bf16)

    core = parity
    wu_send = lax.dynamic_slice(weights[:, :half_ff], (core * (D // 2), 0), (D // 2, half_ff))
    wu_got = lax.ppermute(wu_send, ("seq", "pair"), [(2 * i + 1, 2 * i) for i in range(count)])
    b_other = lax.ppermute(b_first, "pair", [(0, 1), (1, 0)])

    cos_q, sine_q = rotation_tables(block_in * rows + ids, 64)
    heads = project(hidden, cotangent, weights, b_first, cos_q, sine_q)
    received = []
    for step in range(members):
        target = (place + step) % members
        got = []
        for side in range(2):
            chunk = lax.dynamic_index_in_dim(heads, side * members + target, 0, keepdims=False)
            route = []
            for b in range(count):
                base, j = b // span * span, b % span
                to = base + (j + 2 * step) % span
                route.append((2 * device_of(b), 2 * device_of(to) + side))
            if step == 0 and side == 0:
                got.append(chunk)
            else:
                got.append(lax.ppermute(chunk, ("seq", "pair"), route))
        received.append(jnp.where(on_first, got[0], got[1]))
    own = jnp.stack(received)
    kv_other = lax.ppermute(own[:, 1], "seq", core_swap)

    def attn_half(matrix, index):
        parts = [matrix[:, j * D + index * half : j * D + index * half + half] for j in range(3)]
        return jnp.concatenate(parts, axis=1)

    held, tied = lax.optimization_barrier((weights, own[0, 0, :8]))
    qkv_second = attn_half(held, 1)
    out_second = held[half : 2 * half, 3 * D :]
    wa_send = jnp.concatenate(
        [
            lax.dynamic_slice(qkv_second, (core * (D // 2), 0), (D // 2, 3 * half)),
            lax.dynamic_slice(out_second, (0, core * (D // 2)), (half, D // 2)),
        ],
        axis=1,
    )
    wa_got = lax.ppermute(wa_send, ("seq", "pair"), [(2 * i, 2 * i + 1) for i in range(count)])

    def both_cores(got):
        other = lax.ppermute(got, "seq", core_swap)
        return (jnp.where(core == 0, got, other), jnp.where(core == 0, other, got))

    wu_low, wu_high = both_cores(wu_got)
    w_up = jnp.where(on_first, jnp.concatenate([wu_low, wu_high], axis=0), weights[:, half_ff:])
    b_up = jnp.where(on_first, b_other[0, :half_ff], b_first[0, half_ff:])
    w_down = lax.dynamic_slice(w_second, (branch * half_ff, 0), (half_ff, D))

    root_half = 0.7071067811865476
    up_proj = mm(hidden, w_up, ((1,), (0,))) + b_up
    cdf = 0.5 * (1.0 + lax.erf(up_proj * root_half))
    active = (up_proj * cdf).astype(bf16)
    slope = cdf + up_proj * jnp.exp(up_proj * up_proj * -0.5) * 0.3989422804014327
    d_active = mm(cotangent, w_down, ((1,), (1,)))
    d_up = (d_active * slope).astype(bf16)
    feed_out = mm(active, w_down, ((1,), (0,)))
    d_hidden_feed = mm(d_up, w_up, ((1,), (1,)))
    g_up = mm(hidden, d_up, ((0,), (0,))).astype(bf16)
    g_down = mm(active, cotangent, ((0,), (0,))).astype(bf16)
    up_bias = jnp.sum(d_up, axis=0, dtype=f32)

    bits = [b for b in range(count.bit_length() - 1)]
    path_one = [bits[0]] + bits[1:]
    path_two = [bits[0]] + bits[2:] + [bits[1]]

    def reduce_scatter(array, path):
        for b in path:
            n, size, cols = array.shape
            bit = (seq_at >> b) & 1
            split = array.reshape(n, 2, size // 2, cols)
            keep = lax.dynamic_index_in_dim(split, bit, 1, keepdims=False)
            send = lax.dynamic_index_in_dim(split, 1 - bit, 1, keepdims=False)
            got = lax.ppermute(send, "seq", seq_swap(1 << b))
            array = (keep.astype(f32) + got.astype(f32)).astype(bf16)
        return array

    def all_gather(array, path):
        for b in reversed(path):
            bit = (seq_at >> b) & 1
            got = lax.ppermute(array, "seq", seq_swap(1 << b))
            array = jnp.where(
                bit == 0,
                jnp.concatenate([array, got], axis=1),
                jnp.concatenate([got, array], axis=1),
            )
        return array

    feed_one = reduce_scatter(jnp.stack([g_up[:, :D], g_down[:D]]), path_one)
    feed_two = reduce_scatter(jnp.stack([g_up[:, D:], g_down[D:]]), path_two)
    down_one = all_gather(feed_one[1:], path_one)
    down_two = all_gather(feed_two[1:], path_two)
    d_w_second = jnp.concatenate([down_one[0], down_two[0]], axis=0).astype(f32)

    doc_row = lax.dynamic_index_in_dim(doc_lengths, seq_no, 0, keepdims=False)
    pads = lax.dynamic_index_in_dim(pad_counts, seq_no, 0, keepdims=False)
    bounds = jnp.cumsum(doc_row)
    own_blocks = 2 * jnp.arange(members, dtype=jnp.int32) + parity
    own_pos = (own_blocks[:, None] * rows + ids[None, :]).reshape(-1)
    start = jnp.max(jnp.where(bounds[:, None] <= own_pos[None, :], bounds[:, None], 0), axis=0)
    lo = jnp.where(own_pos >= SEQ_LEN - pads, own_pos, start)
    lo = lo.reshape(-1, BQ)
    scal = jnp.concatenate([jnp.stack([place, parity]), lo[:, 0]]).astype(jnp.int32)
    dq, dkv_own, dkv_send = attend(scal, lo, own, kv_other)
    dkv_got = lax.ppermute(dkv_send, "seq", core_swap)
    cos_k, sine_k = rotation_tables(own_pos, 128)
    shape_tab = (members, rows, 128)
    back = join(dq, dkv_own, dkv_got, cos_k.reshape(shape_tab), sine_k.reshape(shape_tab))
    returned = []
    for step in range(members):
        target = (place + step) % members
        chunk = lax.dynamic_index_in_dim(back, target, 0, keepdims=False)
        route = []
        for b in range(count):
            base, j = b // span * span, b % span
            route.append((device_of(b), device_of(base + (j + 2 * step) % span)))
        returned.append(chunk if step == 0 else lax.ppermute(chunk, "seq", route))
    d_proj, attended = gather_heads(scal, jnp.stack(returned))

    wa_low, wa_high = both_cores(wa_got)
    w_qkv = jnp.where(
        on_first,
        attn_half(weights, 0),
        jnp.concatenate([wa_low[:, : 3 * half], wa_high[:, : 3 * half]], axis=0),
    )
    w_out = jnp.where(
        on_first,
        weights[:half, 3 * D :],
        jnp.concatenate([wa_low[:, 3 * half :], wa_high[:, 3 * half :]], axis=1),
    )

    g_qkv = mm(hidden, d_proj, ((0,), (0,))).astype(bf16)
    g_out = mm(attended, cotangent, ((0,), (0,))).astype(bf16)
    d_hidden = mm(d_proj, w_qkv, ((1,), (1,))) + d_hidden_feed
    out_part = mm(attended, w_out, ((1,), (0,))) + feed_out
    out_part = out_part + jnp.where(on_first, b_first[0, 3 * D :], 0.0)
    d_hidden_low = d_hidden.astype(bf16)
    out_low = out_part.astype(bf16)
    crossed = lax.ppermute(jnp.stack([out_low, d_hidden_low]), "pair", [(0, 1), (1, 0)])

    packed = g_out.reshape(count, half // count, 2, D // 2)
    packed = packed.transpose(0, 2, 1, 3).reshape(D, D // 2)
    attn_one = reduce_scatter(g_qkv[None, :, :D], path_one)
    attn_two = reduce_scatter(jnp.concatenate([g_qkv[:, D:], packed], axis=1)[None], path_two)

    def slot_shards(attn, feed):
        mine = jnp.where(on_first, attn[0], feed[0])
        other = lax.ppermute(jnp.where(on_first, feed[0], attn[0]), "pair", [(0, 1), (1, 0)])
        return jnp.stack([jnp.where(on_first, mine, other), jnp.where(on_first, other, mine)])

    full_one = all_gather(slot_shards(attn_one, feed_one), path_one)
    full_two = all_gather(slot_shards(attn_two, feed_two), path_two)
    unpacked = full_two[:, :, D // 2 :].reshape(2, count, 2, half // count, D // 2)
    unpacked = unpacked.transpose(0, 1, 3, 2, 4).reshape(D, D)
    as_attn = jnp.concatenate(
        [
            full_one[0, :, :half], full_one[1, :, :half],
            full_one[0, :, half:], full_one[1, :, half:],
            full_two[0, :, :half], full_two[1, :, :half],
            unpacked,
        ],
        axis=1,
    )
    as_feed = jnp.concatenate([full_one[0], full_two[0], full_one[1], full_two[1]], axis=1)
    d_w_first = jnp.where(on_first, as_attn, as_feed).astype(f32)

    outputs = (widened + b_second + (out_low.astype(f32) + crossed[0].astype(f32))).astype(bf16)
    normal = centred * rstd
    e = (d_hidden_low.astype(f32) + crossed[1].astype(f32)) * ln_gain
    d_norm = rstd * (
        e
        - jnp.mean(e, axis=1, keepdims=True)
        - normal * jnp.mean(e * normal, axis=1, keepdims=True)
    )
    d_inputs = (cotangent.astype(f32) + d_norm).astype(bf16)

    def in_half(vector):
        zero = jnp.zeros_like(vector)
        return jnp.stack([jnp.where(on_first, vector, zero), jnp.where(on_first, zero, vector)])

    qkv_bias = jnp.sum(d_proj, axis=0, dtype=f32).reshape(3, half)
    cot_sum = jnp.where(on_first, jnp.sum(cotangent, axis=0, dtype=f32), 0.0)
    small = jnp.concatenate(
        [
            in_half(qkv_bias).transpose(1, 0, 2).reshape(-1),
            in_half(up_bias).reshape(-1),
            cot_sum,
            jnp.sum(d_hidden * normal, axis=0),
            jnp.sum(d_hidden, axis=0),
        ]
    ).reshape(-1, 128)
    for b in bits:
        small = small + lax.ppermute(small, "seq", seq_swap(1 << b))
    small = (small + lax.ppermute(small, "pair", [(0, 1), (1, 0)])).reshape(-1)
    cot_total = small[3 * D + FF : 4 * D + FF]
    d_b_first = jnp.where(
        on_first, jnp.concatenate([small[: 3 * D], cot_total]), small[3 * D : 3 * D + FF]
    )
    return (
        outputs,
        d_inputs,
        small[4 * D + FF : 5 * D + FF],
        small[5 * D + FF :],
        d_w_first[None],
        d_b_first[None],
        d_w_second,
        cot_total,
    )


def solution(mesh):
    in_specs = (
        P("seq", None),
        P("seq", None),
        P(),
        P(),
        P(),
        P(),
        P("pair", None, None),
        P("pair", None),
        P(),
        P(),
    )
    out_specs = (
        P("seq", None),
        P("seq", None),
        P(),
        P(),
        P("pair", None, None),
        P("pair", None),
        P("pair", None),
        P(),
    )
    return jax.shard_map(body, mesh=mesh, in_specs=in_specs, out_specs=out_specs, check_vma=False)
```

time: 4680 us -> 659 us (0.14)
  waiting for transfers between devices: 2060 us -> 246 us
  starting transfers between devices: 912 us -> 149 us
  matrix products: 782 us -> 38.5 us
  other arithmetic: 376 us -> 67.3 us
  local copies, waits for them, and re-layouts: 369 us -> 69.2 us
  blocking collectives: 140 us -> 0 us
  Pallas kernels: 0 us -> 73.1 us
    ppermute x30 -> x69, waiting for transfers between devices: 1340 us -> 246 us  [the longest x16 93.7 us: all_gather(): got = lax.ppermute(array, 'seq', seq_swap(1 << b))]
    ppermute x30 -> x69, starting transfers between devices: 911 us -> 149 us  [the longest x15 70.1 us: body(): got.append(lax.ppermute(chunk, ('seq', 'pair'), route))]
    dot_general x102 -> x10, matrix products: 782 us -> 38.5 us  [mm(): lax.dot_general(left, right, (dims, ((), ())), preferred_element_type=f32)]
    psum x1 -> x0, waiting for transfers between devices: 370 us -> none  [body(): lax.psum((branch_out, d_hidden, grad_second[:half_ff]), 'pair')]
    reduce_scatter x2 -> x0, waiting for transfers between devices: 284 us -> none  [the longest x1 181 us: body(): lax.psum_scatter(grad_first, 'seq', scatter_dimension=1, tiled=True)]
    cond x33 -> x0, local copies, waits for them, and re-layouts: 146 us -> none
    reduce_sum x25 -> x4, other arithmetic: 142 us -> 3.04 us  [the longest x1 1.51 us: body(): centred = widened - jnp.mean(widened, axis=1, keepdims=True)]
    unnamed x2 -> x0, blocking collectives: 122 us -> none
  transfers between devices with their start and end apart: 35 -> 69, of which waited for: 18 -> 24; matrix products, arithmetic and copies ran while one was open for 1% -> 20% of each run, Pallas kernels for 0% -> 10%
where the time goes in v1:
time: 659 us; the launch traced here: 646 us
  waiting for transfers between devices  246 us (37%)
  starting transfers between devices  149 us (23%)
  Pallas kernels  73.1 us (11%)
  local copies, waits for them, and re-layouts  69.2 us (11%)
  other arithmetic  67.3 us (10%)
  matrix products  38.5 us (6%)
    ppermute x16, waiting for transfers between devices, all_gather(): got = lax.ppermute(array, 'seq', seq_swap(1 << b))  93.7 us
    ppermute x15, starting transfers between devices, body(): got.append(lax.ppermute(chunk, ('seq', 'pair'), route))  70.1 us
    pallas_call x1, Pallas kernels, attend(): pl.pallas_call(attend_kernel, in_specs=[pl.BlockSpec(memory_space=pltpu.S...  50.6 us
    ppermute x4, waiting for transfers between devices, body(): small = small + lax.ppermute(small, 'seq', seq_swap(1 << b))  41.1 us
    dot_general x10, matrix products, mm(): lax.dot_general(left, right, (dims, ((), ())), preferred_element_type=f32)  38.5 us
    ppermute x7, starting transfers between devices, body(): returned.append(chunk if step == 0 else lax.ppermute(chunk, 'seq', route))  34.8 us
    ppermute x15, waiting for transfers between devices, body(): got.append(lax.ppermute(chunk, ('seq', 'pair'), route))  34 us
    ppermute x1, waiting for transfers between devices, body(): lax.ppermute(jnp.stack([out_low, d_hidden_low]), 'pair', [(0, 1), (1, 0)])  23.5 us
  transfers between devices with their start and end apart: 69, of which 24 were waited for; matrix products, arithmetic and copies ran while one was open for 20% of the time, Pallas kernels for 10%

profile of v1, /device:TPU:0, one launch (start us, length us, event | category | flops | bytes accessed | tf_op | source)
XLA Modules:
  0.0 645.9 jit_solution(11935474312115596657)
XLA Ops:
  6.2 10.3 %project.1 = bf16[16,2,512,128]{3,2,1,0:T(8,128)(2,1)} custom-call(bf16[512,1024]{1,0:T(8,128)(2,1)} %fusion.29.h_ref, bf16[512,1024]{1,0:T(8,128)(2,1)} %g_ref.1, bf16[1024,4096]{1,0:T(8,128)(2,1)} %bitcast.327, bf16[1024,4096]{1,0:T(8,128)(2,1)} %bitcast.328, bf16[1024,4096]{1,0:T(8,128)(2,1)} %bitcast.329, bf16[1024,4096]{1,0:T(8,128)(2,1)} %bitcast.330, ...), custom_call_target="tpu_custom_call" | custom-call | tf_op jit(solution)/shard_map/project/pallas_call | solution.py:74
  20.6 4.9 collective-permute-start
  38.2 5.5 collective-permute-start.2
  60.2 5.7 collective-permute-start.8
  67.0 25.5 %collective-permute-done.5 = bf16[2,512,128]{2,1,0:T(8,128)(2,1)S(1)} collective-permute-done((bf16[2,512,128]{2,1,0:T(8,128)(2,1)}, bf16[2,512,128]{2,1,0:T(8,128)(2,1)S(1)}, u32[]{:S(2)}, u32[]{:S(2)}) %collective-permute-start.5) | collective-permute-done | bytes 262176 | tf_op jit(solution)/shard_map/ppermute | solution.py:333
  97.8 13.5 %collective-permute-start.12 = (bf16[2,512,128]{2,1,0:T(8,128)(2,1)}, bf16[2,512,128]{2,1,0:T(8,128)(2,1)S(1)}, u32[]{:S(2)}, u32[]{:S(2)}) collective-permute-start(bf16[2,512,128]{2,1,0:T(8,128)(2,1)} %get-tuple-element.44), channel_id=1, source_target_pairs={{16,9},{18,11},{20,13},{22,15},{24,17},{26,19},{28,21},{30,23},{0,... | collective-permute-start | bytes 786440 | tf_op jit(solution)/shard_map/ppermute | solution.py:333
  115.0 13.7 %collective-permute-start.13 = (bf16[2,512,128]{2,1,0:T(8,128)(2,1)}, bf16[2,512,128]{2,1,0:T(8,128)(2,1)S(1)}, u32[]{:S(2)}, u32[]{:S(2)}) collective-permute-start(bf16[2,512,128]{2,1,0:T(8,128)(2,1)} %get-tuple-element.43), channel_id=1, source_target_pairs={{16,12},{18,14},{20,16},{22,18},{24,20},{26,22},{28,24},{30,26},{0... | collective-permute-start | bytes 786440 | tf_op jit(solution)/shard_map/ppermute | solution.py:333
  133.5 4.9 collective-permute-done.13
  148.9 50.6 %attend.1 = (f32[8,512,128]{2,1,0:T(8,128)}, f32[8,512,128]{2,1,0:T(8,128)}, f32[8,512,128]{2,1,0:T(8,128)}) custom-call(s32[18]{0:T(128)} %pad_add_fusion.scal, s32[16,256]{1,0:T(8,128)} %copy-done.17, bf16[8,2,512,128]{3,2,1,0:T(8,128)(2,1)} %copy.75.x_ref, bf16[8,512,128]{2,1,0:T(8,128)(2,1)} %collective-permute-done.15.kvp_ref), custom_call_target="tpu_custom_call" | custom-call | tf_op jit(solution)/shard_map/attend/pallas_call | solution.py:200
  202.1 5.8 collective-permute-start.24
  211.5 9.1 %fusion.27 = (f32[8,512,128]{2,1,0:T(8,128)}, f32[8,512,128]{2,1,0:T(8,128)}) fusion(s32[128]{0:T(128)S(1)} %get-tuple-element.102, s32[128]{0:T(128)S(1)} %get-tuple-element.103, pred[128]{0:T(512)(128)(4,1)S(1)} %get-tuple-element.98, f32[8,512]{1,0:T(8,128)S(1)} %get-tuple-element.91), kind=kLoop, calls=%fused_computation.68 | loop fusion | flops 11010048 | bytes 4211840 | tf_op jit(solution)/shard_map/jit(_where)/select_n | solution.py:37
  220.6 8.4 %join.1 = bf16[8,2,512,128]{3,2,1,0:T(8,128)(2,1)} custom-call(f32[8,512,128]{2,1,0:T(8,128)} %get-tuple-element.13.dq_ref, f32[8,512,128]{2,1,0:T(8,128)} %get-tuple-element.14.own_ref, f32[8,512,128]{2,1,0:T(8,128)} %collective-permute-done.16.got_ref, f32[8,512,128]{2,1,0:T(8,128)} %get-tuple-element.84.c_ref, f32[8,512,128]{2,1,0:T(8,128)} %get-tuple-element.83.s_ref), custom_call_target="tpu_custom_call" | custom-call | tf_op jit(solution)/shard_map/join/pallas_call | solution.py:230
  231.3 7.1 %collective-permute-start.17 = (bf16[2,512,128]{2,1,0:T(8,128)(2,1)S(1)}, bf16[2,512,128]{2,1,0:T(8,128)(2,1)S(1)}, u32[]{:S(2)}, u32[]{:S(2)}) collective-permute-start(bf16[2,512,128]{2,1,0:T(8,128)(2,1)S(1)} %get-tuple-element.68), channel_id=1, source_target_pairs={{16,20},{18,22},{20,24},{22,26},{24,28},{26,30},{28,0},{30,2},{0,4... | collective-permute-start | bytes 786440 | tf_op jit(solution)/shard_map/ppermute | solution.py:430
  238.5 14.0 %collective-permute-done.28 = f32[1,4096]{1,0:T(1,128)S(1)} collective-permute-done((f32[1,4096]{1,0:T(1,128)S(1)}, f32[1,4096]{1,0:T(1,128)S(1)}, u32[]{:S(2)}, u32[]{:S(2)}) %collective-permute-start.28) | collective-permute-done | bytes 16416 | tf_op jit(solution)/shard_map/ppermute | solution.py:315
  258.6 8.5 %collective-permute-start.21 = (bf16[2,512,128]{2,1,0:T(8,128)(2,1)S(1)}, bf16[2,512,128]{2,1,0:T(8,128)(2,1)S(1)}, u32[]{:S(2)}, u32[]{:S(2)}) collective-permute-start(bf16[2,512,128]{2,1,0:T(8,128)(2,1)S(1)} %get-tuple-element.64), channel_id=1, source_target_pairs={{16,4},{18,6},{20,8},{22,10},{24,12},{26,14},{28,16},{30,18},{0,20... | collective-permute-start | bytes 786440 | tf_op jit(solution)/shard_map/ppermute | solution.py:430
  267.8 7.8 %collective-permute-done.19 = bf16[2,512,128]{2,1,0:T(8,128)(2,1)S(1)} collective-permute-done((bf16[2,512,128]{2,1,0:T(8,128)(2,1)S(1)}, bf16[2,512,128]{2,1,0:T(8,128)(2,1)S(1)}, u32[]{:S(2)}, u32[]{:S(2)}) %collective-permute-start.19) | collective-permute-done | bytes 262176 | tf_op jit(solution)/shard_map/ppermute | solution.py:430
  275.6 8.7 %collective-permute-start.22 = (bf16[2,512,128]{2,1,0:T(8,128)(2,1)S(1)}, bf16[2,512,128]{2,1,0:T(8,128)(2,1)S(1)}, u32[]{:S(2)}, u32[]{:S(2)}) collective-permute-start(bf16[2,512,128]{2,1,0:T(8,128)(2,1)S(1)} %get-tuple-element.63), channel_id=1, source_target_pairs={{16,8},{18,10},{20,12},{22,14},{24,16},{26,18},{28,20},{30,22},{0,... | collective-permute-start | bytes 786440 | tf_op jit(solution)/shard_map/ppermute | solution.py:430
  285.1 5.7 collective-permute-start.23
  293.7 5.6 collective-permute-done.23
  331.7 6.5 %convert_reduce_fusion = (f32[2048]{0:T(1024)S(1)}, bf16[512,2048]{1,0:T(8,128)(2,1)}) fusion(f32[512,2048]{1,0:T(8,128)} %get-tuple-element.95, f32[2048]{0:T(1024)S(1)} %bitcast.406, bf16[512,1024]{1,0:T(8,128)(2,1)S(1)} %copy-done.9, bf16[4096,1024]{1,0:T(8,128)(2,1)S(1)} %bitcast.410, s32[]{:T(128)S(6)} %select_n.829), kind=kOutput, calls=%fused_computation.25 | convolution fusion | flops 2161113088 | bytes 11550724 | tf_op jit(solution)/shard_map/dot_general | solution.py:28
  338.1 7.9 %fusion.96 = f32[512,1024]{1,0:T(8,128)} fusion(bf16[512,2048]{1,0:T(8,128)(2,1)} %get-tuple-element.97, bf16[1024,4096]{1,0:T(8,128)(2,1)S(1)} %bitcast.338, bf16[512,2048]{1,0:T(8,128)(2,1)S(1)} %get-tuple-element.58, bf16[512,2048]{1,0:T(8,128)(2,1)S(1)} %get-tuple-element.57, pred[]{:T(512)S(6)} %eq.59), kind=kOutput, calls=%fused_computation.303 | convolution fusion | flops 2157969408 | bytes 12582913 | tf_op jit(solution)/shard_map/dot_general | solution.py:28
  371.2 9.9 %collective-permute-done.36 = bf16[1,256,1024]{2,1,0:T(8,128)(2,1)S(1)} collective-permute-done((bf16[1,256,1024]{2,1,0:T(8,128)(2,1)S(1)}, bf16[1,256,1024]{2,1,0:T(8,128)(2,1)S(1)}, u32[]{:S(2)}, u32[]{:S(2)}) %collective-permute-start.36) | collective-permute-done | bytes 524320 | tf_op jit(solution)/shard_map/ppermute | solution.py:387
  385.9 23.5 %collective-permute-done.29 = bf16[2,512,1024]{2,1,0:T(8,128)(2,1)S(1)} collective-permute-done((bf16[2,512,1024]{2,1,0:T(8,128)(2,1)S(1)}, bf16[2,512,1024]{2,1,0:T(8,128)(2,1)S(1)}, u32[]{:S(2)}, u32[]{:S(2)}) %collective-permute-start.29) | collective-permute-done | bytes 2097184 | tf_op jit(solution)/shard_map/ppermute | solution.py:452
  421.4 21.4 %collective-permute-done.31 = f32[80,128]{1,0:T(8,128)S(1)} collective-permute-done((f32[80,128]{1,0:T(8,128)S(1)}, f32[80,128]{1,0:T(8,128)S(1)}, u32[]{:S(2)}, u32[]{:S(2)}) %collective-permute-start.31) | collective-permute-done | bytes 40992 | tf_op jit(solution)/shard_map/ppermute | solution.py:506
  450.6 19.7 %collective-permute-done.33 = f32[80,128]{1,0:T(8,128)S(1)} collective-permute-done((f32[80,128]{1,0:T(8,128)S(1)}, f32[80,128]{1,0:T(8,128)S(1)}, u32[]{:S(2)}, u32[]{:S(2)}) %collective-permute-start.33) | collective-permute-done | bytes 40992 | tf_op jit(solution)/shard_map/ppermute | solution.py:506
  479.6 7.7 %collective-permute-done.42 = bf16[2,64,1024]{2,1,0:T(8,128)(2,1)S(1)} collective-permute-done((bf16[2,64,1024]{2,1,0:T(8,128)(2,1)S(1)}, bf16[2,64,1024]{2,1,0:T(8,128)(2,1)S(1)}, u32[]{:S(2)}, u32[]{:S(2)}) %collective-permute-start.42) | collective-permute-done | bytes 262176 | tf_op jit(solution)/shard_map/ppermute | solution.py:387
  500.6 24.8 %collective-permute-done.44 = bf16[2,64,1024]{2,1,0:T(8,128)(2,1)S(1)} collective-permute-done((bf16[2,64,1024]{2,1,0:T(8,128)(2,1)S(1)}, bf16[2,64,1024]{2,1,0:T(8,128)(2,1)S(1)}, u32[]{:S(2)}, u32[]{:S(2)}) %collective-permute-start.44) | collective-permute-done | bytes 262176 | tf_op jit(solution)/shard_map/ppermute | solution.py:394
  528.5 11.0 %collective-permute-done.58 = bf16[2,128,1024]{2,1,0:T(8,128)(2,1)S(1)} collective-permute-done((bf16[2,128,1024]{2,1,0:T(8,128)(2,1)S(1)}, bf16[2,128,1024]{2,1,0:T(8,128)(2,1)S(1)}, u32[]{:S(2)}, u32[]{:S(2)}) %collective-permute-start.58) | collective-permute-done | bytes 524320 | tf_op jit(solution)/shard_map/ppermute | solution.py:394
  545.1 11.0 %collective-permute-done.45 = bf16[2,128,1024]{2,1,0:T(8,128)(2,1)S(1)} collective-permute-done((bf16[2,128,1024]{2,1,0:T(8,128)(2,1)S(1)}, bf16[2,128,1024]{2,1,0:T(8,128)(2,1)S(1)}, u32[]{:S(2)}, u32[]{:S(2)}) %collective-permute-start.45) | collective-permute-done | bytes 524320 | tf_op jit(solution)/shard_map/ppermute | solution.py:394
  556.7 5.1 collective-permute-done.62
  562.9 32.5 %collective-permute-done.67 = bf16[1,256,1024]{2,1,0:T(8,128)(2,1)S(1)} collective-permute-done((bf16[1,256,1024]{2,1,0:T(8,128)(2,1)S(1)}, bf16[1,256,1024]{2,1,0:T(8,128)(2,1)S(1)}, u32[]{:S(2)}, u32[]{:S(2)}) %collective-permute-start.67) | collective-permute-done | bytes 524320 | tf_op jit(solution)/shard_map/ppermute | solution.py:394
  632.2 13.3 %fusion = f32[1,1024,4096]{2,1,0:T(8,128)} fusion(bf16[1,1024,4096]{2,1,0:T(8,128)(2,1)} %constant_dynamic-update-slice_fusion.1, bf16[1,1024,1024]{2,1,0:T(8,128)(2,1)S(1)} %copy-done.3, bf16[1,1024,1024]{2,1,0:T(8,128)(2,1)} %get-tuple-element.33, bf16[1,1024,1024]{2,1,0:T(8,128)(2,1)S(1)} %get-tuple-element.34, bf16[1,1024,1024]{2,1,0:T(8,128)(2,1)S(1)} %copy-done.4, ...), kind=kLoop, calls=%fused_computation.1 | loop fusion | flops 41943040 | bytes 33554432 | tf_op jit(solution)/shard_map/convert_element_type | solution.py:478
  (351 shorter events, 232.9 us)
Async XLA Ops:
  33.5 219.0 %collective-permute-start.26 = (bf16[512,2048]{1,0:T(8,128)(2,1)}, bf16[512,2048]{1,0:T(8,128)(2,1)}, u32[]{:S(2)}, u32[]{:S(2)}) collective-permute-start(bf16[512,2048]{1,0:T(8,128)(2,1)} %constant_dynamic-slice_fusion), channel_id=1, source_target_pairs={{1,0},{3,2},{5,4},{7,6},{9,8},{11,10},{13,12},{15,14},{17,16},{19,... | collective-permute-start | bytes 6291464 | tf_op jit(solution)/shard_map/ppermute | solution.py:314
  50.2 42.3 %collective-permute-start.5 = (bf16[2,512,128]{2,1,0:T(8,128)(2,1)}, bf16[2,512,128]{2,1,0:T(8,128)(2,1)S(1)}, u32[]{:S(2)}, u32[]{:S(2)}) collective-permute-start(bf16[2,512,128]{2,1,0:T(8,128)(2,1)} %get-tuple-element.51), channel_id=1, source_target_pairs={{16,28},{18,30},{20,0},{22,2},{24,4},{26,6},{28,8},{30,10},{0,12},... | collective-permute-start | bytes 786440 | tf_op jit(solution)/shard_map/ppermute | solution.py:333
  54.7 39.7 %collective-permute-start.6 = (bf16[2,512,128]{2,1,0:T(8,128)(2,1)}, bf16[2,512,128]{2,1,0:T(8,128)(2,1)S(1)}, u32[]{:S(2)}, u32[]{:S(2)}) collective-permute-start(bf16[2,512,128]{2,1,0:T(8,128)(2,1)} %get-tuple-element.50), channel_id=1, source_target_pairs={{16,29},{18,31},{20,1},{22,3},{24,5},{26,7},{28,9},{30,11},{0,13},... | collective-permute-start | bytes 786440 | tf_op jit(solution)/shard_map/ppermute | solution.py:333
  57.1 38.8 %collective-permute-start.7 = (bf16[2,512,128]{2,1,0:T(8,128)(2,1)}, bf16[2,512,128]{2,1,0:T(8,128)(2,1)S(1)}, u32[]{:S(2)}, u32[]{:S(2)}) collective-permute-start(bf16[2,512,128]{2,1,0:T(8,128)(2,1)} %get-tuple-element.49), channel_id=1, source_target_pairs={{16,0},{18,2},{20,4},{22,6},{24,8},{26,10},{28,12},{30,14},{0,16},... | collective-permute-start | bytes 786440 | tf_op jit(solution)/shard_map/ppermute | solution.py:333
  60.2 37.6 %collective-permute-start.8 = (bf16[2,512,128]{2,1,0:T(8,128)(2,1)}, bf16[2,512,128]{2,1,0:T(8,128)(2,1)S(1)}, u32[]{:S(2)}, u32[]{:S(2)}) collective-permute-start(bf16[2,512,128]{2,1,0:T(8,128)(2,1)} %get-tuple-element.48), channel_id=1, source_target_pairs={{16,1},{18,3},{20,5},{22,7},{24,9},{26,11},{28,13},{30,15},{0,17},... | collective-permute-start | bytes 786440 | tf_op jit(solution)/shard_map/ppermute | solution.py:333
  94.4 34.2 %collective-permute-start.10 = (bf16[2,512,128]{2,1,0:T(8,128)(2,1)}, bf16[2,512,128]{2,1,0:T(8,128)(2,1)S(1)}, u32[]{:S(2)}, u32[]{:S(2)}) collective-permute-start(bf16[2,512,128]{2,1,0:T(8,128)(2,1)} %get-tuple-element.46), channel_id=1, source_target_pairs={{16,5},{18,7},{20,9},{22,11},{24,13},{26,15},{28,17},{30,19},{0,21... | collective-permute-start | bytes 786440 | tf_op jit(solution)/shard_map/ppermute | solution.py:333
  95.8 37.6 %collective-permute-start.11 = (bf16[2,512,128]{2,1,0:T(8,128)(2,1)}, bf16[2,512,128]{2,1,0:T(8,128)(2,1)S(1)}, u32[]{:S(2)}, u32[]{:S(2)}) collective-permute-start(bf16[2,512,128]{2,1,0:T(8,128)(2,1)} %get-tuple-element.45), channel_id=1, source_target_pairs={{16,8},{18,10},{20,12},{22,14},{24,16},{26,18},{28,20},{30,22},{0,... | collective-permute-start | bytes 786440 | tf_op jit(solution)/shard_map/ppermute | solution.py:333
  97.8 35.7 %collective-permute-start.12 = (bf16[2,512,128]{2,1,0:T(8,128)(2,1)}, bf16[2,512,128]{2,1,0:T(8,128)(2,1)S(1)}, u32[]{:S(2)}, u32[]{:S(2)}) collective-permute-start(bf16[2,512,128]{2,1,0:T(8,128)(2,1)} %get-tuple-element.44), channel_id=1, source_target_pairs={{16,9},{18,11},{20,13},{22,15},{24,17},{26,19},{28,21},{30,23},{0,... | collective-permute-start | bytes 786440 | tf_op jit(solution)/shard_map/ppermute | solution.py:333
  202.1 50.5 %collective-permute-start.24 = (bf16[512,2048]{1,0:T(8,128)(2,1)S(1)}, bf16[512,2048]{1,0:T(8,128)(2,1)}, u32[]{:S(2)}, u32[]{:S(2)}) collective-permute-start(bf16[512,2048]{1,0:T(8,128)(2,1)S(1)} %pad_maximum_fusion), channel_id=1, source_target_pairs={{0,1},{2,3},{4,5},{6,7},{8,9},{10,11},{12,13},{14,15},{16,17},{18,... | collective-permute-start | bytes 6291464 | tf_op jit(solution)/shard_map/ppermute | solution.py:352
  207.9 44.6 %collective-permute-start.28 = (f32[1,4096]{1,0:T(1,128)S(1)}, f32[1,4096]{1,0:T(1,128)S(1)}, u32[]{:S(2)}, u32[]{:S(2)}) collective-permute-start(f32[1,4096]{1,0:T(1,128)S(1)} %copy-done.15), channel_id=1, source_target_pairs={{0,1},{1,0},{2,3},{3,2},{4,5},{5,4},{6,7},{7,6},{8,9},{9,8},{10,11... | collective-permute-start | bytes 49160 | tf_op jit(solution)/shard_map/ppermute | solution.py:315
  252.5 70.4 %collective-permute-start.27 = (bf16[512,2048]{1,0:T(8,128)(2,1)}, bf16[512,2048]{1,0:T(8,128)(2,1)}, u32[]{:S(2)}, u32[]{:S(2)}) collective-permute-start(bf16[512,2048]{1,0:T(8,128)(2,1)} %collective-permute-done.26), channel_id=1, source_target_pairs={{16,18},{18,16},{20,22},{22,20},{24,26},{26,24},{28,30},{30,28},{0... | collective-permute-start | bytes 6291464 | tf_op jit(solution)/shard_map/ppermute | solution.py:355
  252.6 66.7 %collective-permute-start.25 = (bf16[512,2048]{1,0:T(8,128)(2,1)}, bf16[512,2048]{1,0:T(8,128)(2,1)}, u32[]{:S(2)}, u32[]{:S(2)}) collective-permute-start(bf16[512,2048]{1,0:T(8,128)(2,1)} %collective-permute-done.24), channel_id=1, source_target_pairs={{16,18},{18,16},{20,22},{22,20},{24,26},{26,24},{28,30},{30,28},{0... | collective-permute-start | bytes 6291464 | tf_op jit(solution)/shard_map/ppermute | solution.py:355
  258.6 33.0 %collective-permute-start.21 = (bf16[2,512,128]{2,1,0:T(8,128)(2,1)S(1)}, bf16[2,512,128]{2,1,0:T(8,128)(2,1)S(1)}, u32[]{:S(2)}, u32[]{:S(2)}) collective-permute-start(bf16[2,512,128]{2,1,0:T(8,128)(2,1)S(1)} %get-tuple-element.64), channel_id=1, source_target_pairs={{16,4},{18,6},{20,8},{22,10},{24,12},{26,14},{28,16},{30,18},{0,20... | collective-permute-start | bytes 786440 | tf_op jit(solution)/shard_map/ppermute | solution.py:430
  312.8 51.7 %collective-permute-start.35 = (bf16[1,512,1024]{2,1,0:T(8,128)(2,1)}, bf16[1,512,1024]{2,1,0:T(8,128)(2,1)}, u32[]{:S(2)}, u32[]{:S(2)}) collective-permute-start(bf16[1,512,1024]{2,1,0:T(8,128)(2,1)} %dynamic-slice_bitcast_fusion.2), channel_id=1, source_target_pairs={{0,2},{2,0},{4,6},{6,4},{8,10},{10,8},{12,14},{14,12},{16,18},{18,... | collective-permute-start | bytes 3145736 | tf_op jit(solution)/shard_map/ppermute | solution.py:387
  318.7 50.6 %collective-permute-start.48 = (bf16[1,512,1024]{2,1,0:T(8,128)(2,1)S(1)}, bf16[1,512,1024]{2,1,0:T(8,128)(2,1)S(1)}, u32[]{:S(2)}, u32[]{:S(2)}) collective-permute-start(bf16[1,512,1024]{2,1,0:T(8,128)(2,1)S(1)} %fusion.61), channel_id=1, source_target_pairs={{0,2},{2,0},{4,6},{6,4},{8,10},{10,8},{12,14},{14,12},{16,18},{18,... | collective-permute-start | bytes 3145736 | tf_op jit(solution)/shard_map/ppermute | solution.py:387
  361.7 47.6 %collective-permute-start.29 = (bf16[2,512,1024]{2,1,0:T(8,128)(2,1)S(1)}, bf16[2,512,1024]{2,1,0:T(8,128)(2,1)S(1)}, u32[]{:S(2)}, u32[]{:S(2)}) collective-permute-start(bf16[2,512,1024]{2,1,0:T(8,128)(2,1)S(1)} %pad_maximum_fusion.1), channel_id=1, source_target_pairs={{0,1},{1,0},{2,3},{3,2},{4,5},{5,4},{6,7},{7,6},{8,9},{9,8},{10,11... | collective-permute-start | bytes 6291464 | tf_op jit(solution)/shard_map/ppermute | solution.py:452
  364.4 51.1 %collective-permute-start.39 = (bf16[2,512,1024]{2,1,0:T(8,128)(2,1)S(1)}, bf16[2,512,1024]{2,1,0:T(8,128)(2,1)S(1)}, u32[]{:S(2)}, u32[]{:S(2)}) collective-permute-start(bf16[2,512,1024]{2,1,0:T(8,128)(2,1)S(1)} %fusion.47), channel_id=1, source_target_pairs={{0,2},{2,0},{4,6},{6,4},{8,10},{10,8},{12,14},{14,12},{16,18},{18,... | collective-permute-start | bytes 6291464 | tf_op jit(solution)/shard_map/ppermute | solution.py:387
  371.1 41.7 %collective-permute-start.52 = (bf16[2,512,1024]{2,1,0:T(8,128)(2,1)S(1)}, bf16[2,512,1024]{2,1,0:T(8,128)(2,1)S(1)}, u32[]{:S(2)}, u32[]{:S(2)}) collective-permute-start(bf16[2,512,1024]{2,1,0:T(8,128)(2,1)S(1)} %fusion.43), channel_id=1, source_target_pairs={{0,2},{2,0},{4,6},{6,4},{8,10},{10,8},{12,14},{14,12},{16,18},{18,... | collective-permute-start | bytes 6291464 | tf_op jit(solution)/shard_map/ppermute | solution.py:387
  381.4 36.7 %collective-permute-start.37 = (bf16[1,128,1024]{2,1,0:T(8,128)(2,1)S(1)}, bf16[1,128,1024]{2,1,0:T(8,128)(2,1)S(1)}, u32[]{:S(2)}, u32[]{:S(2)}) collective-permute-start(bf16[1,128,1024]{2,1,0:T(8,128)(2,1)S(1)} %dynamic-slice_bitcast_fusion.10), channel_id=1, source_target_pairs={{0,8},{2,10},{4,12},{6,14},{8,0},{10,2},{12,4},{14,6},{16,24},{18,... | collective-permute-start | bytes 786440 | tf_op jit(solution)/shard_map/ppermute | solution.py:387
  383.6 64.8 %collective-permute-start.50 = (bf16[1,128,1024]{2,1,0:T(8,128)(2,1)S(1)}, bf16[1,128,1024]{2,1,0:T(8,128)(2,1)S(1)}, u32[]{:S(2)}, u32[]{:S(2)}) collective-permute-start(bf16[1,128,1024]{2,1,0:T(8,128)(2,1)S(1)} %dynamic-slice_bitcast_fusion.8), channel_id=1, source_target_pairs={{0,16},{2,18},{4,20},{6,22},{8,24},{10,26},{12,28},{14,30},{16,0},... | collective-permute-start | bytes 786440 | tf_op jit(solution)/shard_map/ppermute | solution.py:387
  416.6 29.8 %collective-permute-start.40 = (bf16[2,256,1024]{2,1,0:T(8,128)(2,1)S(1)}, bf16[2,256,1024]{2,1,0:T(8,128)(2,1)S(1)}, u32[]{:S(2)}, u32[]{:S(2)}) collective-permute-start(bf16[2,256,1024]{2,1,0:T(8,128)(2,1)S(1)} %dynamic-slice_bitcast_fusion.1), channel_id=1, source_target_pairs={{0,4},{2,6},{4,0},{6,2},{8,12},{10,14},{12,8},{14,10},{16,20},{18,... | collective-permute-start | bytes 3145736 | tf_op jit(solution)/shard_map/ppermute | solution.py:387
  418.8 68.5 %collective-permute-start.38 = (bf16[1,64,1024]{2,1,0:T(8,128)(2,1)S(1)}, bf16[1,64,1024]{2,1,0:T(8,128)(2,1)S(1)}, u32[]{:S(2)}, u32[]{:S(2)}) collective-permute-start(bf16[1,64,1024]{2,1,0:T(8,128)(2,1)S(1)} %dynamic-slice_bitcast_fusion.34), channel_id=1, source_target_pairs={{0,16},{2,18},{4,20},{6,22},{8,24},{10,26},{12,28},{14,30},{16,0},... | collective-permute-start | bytes 393224 | tf_op jit(solution)/shard_map/ppermute | solution.py:387
  492.5 32.9 %collective-permute-start.44 = (bf16[2,64,1024]{2,1,0:T(8,128)(2,1)S(1)}, bf16[2,64,1024]{2,1,0:T(8,128)(2,1)S(1)}, u32[]{:S(2)}, u32[]{:S(2)}) collective-permute-start(bf16[2,64,1024]{2,1,0:T(8,128)(2,1)S(1)} %pad_maximum_fusion.2), channel_id=1, source_target_pairs={{0,16},{2,18},{4,20},{6,22},{8,24},{10,26},{12,28},{14,30},{16,0},... | collective-permute-start | bytes 786440 | tf_op jit(solution)/shard_map/ppermute | solution.py:394
  493.0 35.3 %collective-permute-start.61 = (bf16[1,64,1024]{2,1,0:T(8,128)(2,1)S(1)}, bf16[1,64,1024]{2,1,0:T(8,128)(2,1)S(1)}, u32[]{:S(2)}, u32[]{:S(2)}) collective-permute-start(bf16[1,64,1024]{2,1,0:T(8,128)(2,1)S(1)} %get-tuple-element.76), channel_id=1, source_target_pairs={{0,16},{2,18},{4,20},{6,22},{8,24},{10,26},{12,28},{14,30},{16,0},... | collective-permute-start | bytes 393224 | tf_op jit(solution)/shard_map/ppermute | solution.py:394
  496.8 42.8 %collective-permute-start.58 = (bf16[2,128,1024]{2,1,0:T(8,128)(2,1)S(1)}, bf16[2,128,1024]{2,1,0:T(8,128)(2,1)S(1)}, u32[]{:S(2)}, u32[]{:S(2)}) collective-permute-start(bf16[2,128,1024]{2,1,0:T(8,128)(2,1)S(1)} %maximum_select_fusion.18), channel_id=1, source_target_pairs={{0,16},{2,18},{4,20},{6,22},{8,24},{10,26},{12,28},{14,30},{16,0},... | collective-permute-start | bytes 1572872 | tf_op jit(solution)/shard_map/ppermute | solution.py:394
  498.1 46.9 %collective-permute-start.66 = (bf16[1,128,1024]{2,1,0:T(8,128)(2,1)S(1)}, bf16[1,128,1024]{2,1,0:T(8,128)(2,1)S(1)}, u32[]{:S(2)}, u32[]{:S(2)}) collective-permute-start(bf16[1,128,1024]{2,1,0:T(8,128)(2,1)S(1)} %maximum_select_fusion.26), channel_id=1, source_target_pairs={{0,16},{2,18},{4,20},{6,22},{8,24},{10,26},{12,28},{14,30},{16,0},... | collective-permute-start | bytes 786440 | tf_op jit(solution)/shard_map/ppermute | solution.py:394
  525.6 30.6 %collective-permute-start.45 = (bf16[2,128,1024]{2,1,0:T(8,128)(2,1)S(1)}, bf16[2,128,1024]{2,1,0:T(8,128)(2,1)S(1)}, u32[]{:S(2)}, u32[]{:S(2)}) collective-permute-start(bf16[2,128,1024]{2,1,0:T(8,128)(2,1)S(1)} %maximum_select_fusion.17), channel_id=1, source_target_pairs={{0,8},{2,10},{4,12},{6,14},{8,0},{10,2},{12,4},{14,6},{16,24},{18,... | collective-permute-start | bytes 1572872 | tf_op jit(solution)/shard_map/ppermute | solution.py:394
  528.3 33.4 %collective-permute-start.62 = (bf16[1,128,1024]{2,1,0:T(8,128)(2,1)S(1)}, bf16[1,128,1024]{2,1,0:T(8,128)(2,1)S(1)}, u32[]{:S(2)}, u32[]{:S(2)}) collective-permute-start(bf16[1,128,1024]{2,1,0:T(8,128)(2,1)S(1)} %maximum_select_fusion.24), channel_id=1, source_target_pairs={{0,8},{2,10},{4,12},{6,14},{8,0},{10,2},{12,4},{14,6},{16,24},{18,... | collective-permute-start | bytes 786440 | tf_op jit(solution)/shard_map/ppermute | solution.py:394
  540.1 56.9 %collective-permute-start.59 = (bf16[2,256,1024]{2,1,0:T(8,128)(2,1)S(1)}, bf16[2,256,1024]{2,1,0:T(8,128)(2,1)S(1)}, u32[]{:S(2)}, u32[]{:S(2)}) collective-permute-start(bf16[2,256,1024]{2,1,0:T(8,128)(2,1)S(1)} %maximum_select_fusion.12), channel_id=1, source_target_pairs={{0,8},{2,10},{4,12},{6,14},{8,0},{10,2},{12,4},{14,6},{16,24},{18,... | collective-permute-start | bytes 3145736 | tf_op jit(solution)/shard_map/ppermute | solution.py:394
  545.1 50.3 %collective-permute-start.67 = (bf16[1,256,1024]{2,1,0:T(8,128)(2,1)S(1)}, bf16[1,256,1024]{2,1,0:T(8,128)(2,1)S(1)}, u32[]{:S(2)}, u32[]{:S(2)}) collective-permute-start(bf16[1,256,1024]{2,1,0:T(8,128)(2,1)S(1)} %maximum_select_fusion.22), channel_id=1, source_target_pairs={{0,8},{2,10},{4,12},{6,14},{8,0},{10,2},{12,4},{14,6},{16,24},{18,... | collective-permute-start | bytes 1572872 | tf_op jit(solution)/shard_map/ppermute | solution.py:394
  556.6 41.5 %collective-permute-start.46 = (bf16[2,256,1024]{2,1,0:T(8,128)(2,1)S(1)}, bf16[2,256,1024]{2,1,0:T(8,128)(2,1)S(1)}, u32[]{:S(2)}, u32[]{:S(2)}) collective-permute-start(bf16[2,256,1024]{2,1,0:T(8,128)(2,1)S(1)} %maximum_select_fusion.11), channel_id=1, source_target_pairs={{0,4},{2,6},{4,0},{6,2},{8,12},{10,14},{12,8},{14,10},{16,20},{18,... | collective-permute-start | bytes 3145736 | tf_op jit(solution)/shard_map/ppermute | solution.py:394
  561.9 34.0 %collective-permute-start.63 = (bf16[1,256,1024]{2,1,0:T(8,128)(2,1)S(1)}, bf16[1,256,1024]{2,1,0:T(8,128)(2,1)S(1)}, u32[]{:S(2)}, u32[]{:S(2)}) collective-permute-start(bf16[1,256,1024]{2,1,0:T(8,128)(2,1)S(1)} %maximum_select_fusion.20), channel_id=1, source_target_pairs={{0,4},{2,6},{4,0},{6,2},{8,12},{10,14},{12,8},{14,10},{16,20},{18,... | collective-permute-start | bytes 1572872 | tf_op jit(solution)/shard_map/ppermute | solution.py:394
  (69 other events, 913.9 us)

commit v2 on v1

v2 whole, which is shorter than its diff:
```python
import functools

import jax
import jax.numpy as jnp
from jax import lax
from jax.experimental import pallas as pl
from jax.experimental.pallas import tpu as pltpu
from jax.sharding import PartitionSpec as P

HEADS = 16
HEAD_DIM = 64
D = 1024
FF = 4096
ROT = 16
SEQ_LEN = 8192
DOCS = 8
MOST_DOC = 4096

BQ = 512
BK = 512
epsilon = 1e-05
masked_fill = -1e30
bf16 = jnp.bfloat16
f32 = jnp.float32
VMEM_LIMIT = 60 * 1024 * 1024


def after(array, *others):
    return lax.optimization_barrier((array,) + others)[0]


def mm(left, right, dims):
    return lax.dot_general(left, right, (dims, ((), ())), preferred_element_type=f32)


def rotation_tables(positions, period):
    lane = lax.broadcasted_iota(jnp.int32, (positions.shape[0], 128), 1) % period
    inverse = 10000.0 ** (-2.0 * (lane % (ROT // 2)).astype(f32) / ROT)
    angle = positions.astype(f32)[:, None] * inverse
    cos_tab = jnp.where(lane < ROT, jnp.cos(angle), 1.0)
    sine = jnp.sin(angle)
    sine_tab = jnp.where(lane < ROT // 2, -sine, jnp.where(lane < ROT, sine, 0.0))
    return cos_tab, sine_tab


def turn(block, cos_tab, sine_tab, lane):
    from_left = pltpu.roll(block, 8, 1)
    from_right = pltpu.roll(block, 120, 1)
    return block * cos_tab + jnp.where(lane % 64 < 8, from_right, from_left) * sine_tab


def project_kernel(turned, x_ref, y_ref, wx, wy, bx, by, c_ref, s_ref, out):
    rows = x_ref.shape[0]
    lane = lax.broadcasted_iota(jnp.int32, (rows, 128), 1)
    low = lane < 64
    front_all = mm(x_ref[...], wx[...], ((1,), (0,))) + bx[...]
    back_all = mm(y_ref[...], wy[...], ((1,), (1 if turned else 0,))) + by[...]
    cos_tab = c_ref[...]
    sine_tab = s_ref[...]
    for pair in range(wx.shape[1] // 128):
        cut = slice(128 * pair, 128 * pair + 128)
        front = turn(front_all[:, cut], cos_tab, sine_tab, lane)
        back = back_all[:, cut]
        out[2 * pair] = jnp.where(low, front, pltpu.roll(back, 64, 1)).astype(bf16)
        out[2 * pair + 1] = jnp.where(low, pltpu.roll(front, 64, 1), back).astype(bf16)


def project(left, right, w_left, w_right, b_left, b_right, cos_tab, sine_tab, turned):
    rows = left.shape[0]
    heads = w_left.shape[1] // HEAD_DIM
    whole = lambda i: (0, 0)
    part = lambda i: (0, i)
    if turned:
        right_spec = pl.BlockSpec((256, D), lambda i: (i, 0))
    else:
        right_spec = pl.BlockSpec((D, 256), part)
    return pl.pallas_call(
        functools.partial(project_kernel, turned),
        grid=(heads // 4,),
        in_specs=[
            pl.BlockSpec((rows, D), whole),
            pl.BlockSpec((rows, D), whole),
            pl.BlockSpec((D, 256), part),
            right_spec,
            pl.BlockSpec((1, 256), part),
            pl.BlockSpec((1, 256), part),
            pl.BlockSpec((rows, 128), whole),
            pl.BlockSpec((rows, 128), whole),
        ],
        out_specs=pl.BlockSpec((4, rows, 128), lambda i: (i, 0, 0)),
        out_shape=jax.ShapeDtypeStruct((heads, rows, 128), bf16),
        compiler_params=pltpu.CompilerParams(vmem_limit_bytes=VMEM_LIMIT),
        name="project_q" if turned else "project_kv",
    )(left, right, w_left, w_right, b_left[None], b_right[None], cos_tab, sine_tab)


def feed_grad_kernel(orders, h_ref, u_ref, a_ref, g_ref, out):
    step = pl.program_id(0)
    size = out.shape[2]

    for part in range(4):
        @pl.when(step == part)
        def _():
            left, right = (h_ref, u_ref) if part < 2 else (a_ref, g_ref)
            total = mm(left[...], right[...], ((0,), (0,))).astype(bf16)
            order = orders[part] if part < 2 else range(out.shape[0])
            for i, block in enumerate(order):
                out[i, 0] = total[block * size : block * size + size]


def feed_grads(hidden, d_up, active, cotangent, orders):
    rows = hidden.shape[0]
    count = len(orders[0])
    whole = lambda i: (0, 0)
    return pl.pallas_call(
        functools.partial(feed_grad_kernel, orders),
        grid=(4,),
        in_specs=[
            pl.BlockSpec((rows, D), whole),
            pl.BlockSpec((rows, D), lambda i: (0, jnp.minimum(i, 1))),
            pl.BlockSpec((rows, D), lambda i: (0, jnp.maximum(i - 2, 0))),
            pl.BlockSpec((rows, D), whole),
        ],
        out_specs=pl.BlockSpec((count, 1, D // count, D), lambda i: (0, i, 0, 0)),
        out_shape=jax.ShapeDtypeStruct((count, 4, D // count, D), bf16),
        compiler_params=pltpu.CompilerParams(vmem_limit_bytes=VMEM_LIMIT),
        name="feed_grads",
    )(hidden, d_up, active, cotangent)


def attend_kernel(scal, lo_ref, qd_ref, kv_ref, kvp_ref, dq_ref, own_ref, send_ref,
                  kv_s, kvt_s, s_buf, p_buf, acc_s):
    members, rows, _ = qd_ref.shape
    parity = scal[0]
    scale = HEAD_DIM ** (-0.5)
    to_two = scale * 1.4426950408889634

    for m in range(members):
        at_own = pl.multiple_of((2 * m + parity) * rows, rows)
        at_other = pl.multiple_of((2 * m + 1 - parity) * rows, rows)
        kv_s[pl.ds(at_own, rows), :] = kv_ref[m]
        kv_s[pl.ds(at_other, rows), :] = kvp_ref[m]
    acc_s[...] = jnp.zeros_like(acc_s)

    def transpose_step(b, carry):
        at = pl.multiple_of(b * 256, 256)
        kvt_s[:, pl.ds(at, 256)] = kv_s[pl.ds(at, 256), :].astype(f32).T.astype(bf16)
        return carry

    lax.fori_loop(0, kv_s.shape[0] // 256, transpose_step, 0)

    per = rows // BQ
    lane = lax.broadcasted_iota(jnp.int32, (BQ, 128), 1)
    key_iota = lax.broadcasted_iota(jnp.int32, (BK, BQ), 0)
    query_iota = lax.broadcasted_iota(jnp.int32, (1, BQ), 1)

    def query_block(i, carry):
        m = i // per
        part = i % per
        off = pl.multiple_of(part * BQ, BQ)
        first = (2 * m + parity) * rows + off
        qd = qd_ref[m, pl.ds(off, BQ), :]
        zero = jnp.zeros_like(qd)
        qz = jnp.where(lane < 64, qd, zero)
        dz = jnp.where(lane < 64, zero, qd)
        both = jnp.concatenate([qz, dz], axis=0)
        kb0 = scal[1 + i] // BK
        kb1 = (first + BQ - 1) // BK + 1
        qpos = first + query_iota
        lo = lo_ref[pl.ds(i, 1), :]

        def scores_step(kb, mx):
            at = pl.multiple_of(kb * BK, BK)
            r = mm(kv_s[pl.ds(at, BK), :], both, ((1,), (1,)))
            kpos = at + key_iota
            s = jnp.where((kpos <= qpos) & (kpos >= lo), r[:, :BQ], masked_fill)
            to = pl.multiple_of((kb - kb0) * BK, BK)
            s_buf[pl.ds(to, BK), :] = s
            p_buf[pl.ds(to, BK), :] = r[:, BQ:]
            return jnp.maximum(mx, jnp.max(s.reshape(BK // 8, 8, BQ), axis=0))

        mx = lax.fori_loop(kb0, kb1, scores_step, jnp.full((8, BQ), masked_fill, f32))
        top = jnp.max(mx, axis=0, keepdims=True)

        def exp_step(kb, sums):
            total, dots = sums
            at = pl.multiple_of((kb - kb0) * BK, BK)
            e = jnp.exp2((s_buf[pl.ds(at, BK), :] - top) * to_two)
            s_buf[pl.ds(at, BK), :] = e
            w = e * p_buf[pl.ds(at, BK), :]
            return (total + jnp.sum(e.reshape(BK // 8, 8, BQ), axis=0),
                    dots + jnp.sum(w.reshape(BK // 8, 8, BQ), axis=0))

        zeros = jnp.zeros((8, BQ), f32)
        total, dots = lax.fori_loop(kb0, kb1, exp_step, (zeros, zeros))
        inv = 1.0 / jnp.sum(total, axis=0, keepdims=True)
        row_dot = jnp.sum(dots, axis=0, keepdims=True) * inv

        def grad_step(kb, outs):
            dq_t, at_t = outs
            at = pl.multiple_of(kb * BK, BK)
            to = pl.multiple_of((kb - kb0) * BK, BK)
            p = s_buf[pl.ds(to, BK), :] * inv
            ds = p * (p_buf[pl.ds(to, BK), :] - row_dot)
            p_low = p.astype(bf16)
            ds_low = ds.astype(bf16)
            joined = jnp.concatenate([ds_low, p_low], axis=1)
            acc_s[pl.ds(at, BK), :] += mm(joined, both, ((1,), (0,)))
            dq_t = dq_t + mm(kvt_s[0:64, pl.ds(at, BK)], ds_low, ((1,), (0,)))
            at_t = at_t + mm(kvt_s[64:128, pl.ds(at, BK)], p_low, ((1,), (0,)))
            return dq_t, at_t

        wide = jnp.zeros((64, BQ), f32)
        dq_t, at_t = lax.fori_loop(kb0, kb1, grad_step, (wide, wide))
        done = jnp.concatenate([dq_t * scale, at_t], axis=0).T
        dq_ref[m, pl.ds(off, BQ), :] = done.astype(bf16)
        return carry

    lax.fori_loop(0, members * per, query_block, 0)

    for m in range(members):
        at_own = pl.multiple_of((2 * m + parity) * rows, rows)
        at_other = pl.multiple_of((2 * m + 1 - parity) * rows, rows)
        own_ref[m] = acc_s[pl.ds(at_own, rows), :]
        send_ref[m] = acc_s[pl.ds(at_other, rows), :]


def attend(scal, lo, qd, kv, kv_other):
    members, rows, _ = qd.shape
    total = 2 * members * rows
    piece = jax.ShapeDtypeStruct((members, rows, 128), f32)
    vmem = pl.BlockSpec(memory_space=pltpu.VMEM)
    return pl.pallas_call(
        attend_kernel,
        in_specs=[pl.BlockSpec(memory_space=pltpu.SMEM)] + [vmem] * 4,
        out_specs=[vmem, vmem, vmem],
        out_shape=[jax.ShapeDtypeStruct((members, rows, 128), bf16), piece, piece],
        scratch_shapes=[
            pltpu.VMEM((total, 128), bf16),
            pltpu.VMEM((128, total), bf16),
            pltpu.VMEM((MOST_DOC + BQ + BK, BQ), f32),
            pltpu.VMEM((MOST_DOC + BQ + BK, BQ), f32),
            pltpu.VMEM((total, 128), f32),
        ],
        compiler_params=pltpu.CompilerParams(vmem_limit_bytes=VMEM_LIMIT),
        cost_estimate=pl.CostEstimate(
            flops=1_000_000_000_000, transcendentals=10_000_000, bytes_accessed=20_000_000
        ),
        name="attend",
    )(scal, lo, qd, kv, kv_other)


def join_kernel(own_ref, got_ref, out):
    lane = lax.broadcasted_iota(jnp.int32, own_ref.shape, 2)
    scale = jnp.where(lane < 64, HEAD_DIM ** (-0.5), 1.0)
    out[...] = ((own_ref[...] + got_ref[...]) * scale).astype(bf16)


def join(own, got):
    members, rows, _ = own.shape
    two = pl.BlockSpec((2, rows, 128), lambda m: (m, 0, 0))
    return pl.pallas_call(
        join_kernel,
        grid=(members // 2,),
        in_specs=[two] * 2,
        out_specs=two,
        out_shape=jax.ShapeDtypeStruct((members, rows, 128), bf16),
        name="join",
    )(own, got)


def side_by_side(x_ref, c_ref, s_ref, front_ref, back_ref):
    members, rows, _ = x_ref.shape
    lane = lax.broadcasted_iota(jnp.int32, (rows, 128), 1)
    low = lane < 64
    cos_tab = c_ref[...]
    sine_tab = -s_ref[...]
    for pair in range(members // 2):
        a = x_ref[2 * pair].astype(f32)
        b = x_ref[2 * pair + 1].astype(f32)
        cut = slice(128 * pair, 128 * pair + 128)
        front = jnp.where(low, a, pltpu.roll(b, 64, 1))
        front_ref[:, cut] = turn(front, cos_tab, sine_tab, lane).astype(bf16)
        back_ref[:, cut] = jnp.where(low, pltpu.roll(a, 64, 1), b).astype(bf16)


def query_grad_kernel(share, x_ref, c_ref, s_ref, h_ref, g_ref, dq_ref, att_ref, out):
    side_by_side(x_ref, c_ref, s_ref, dq_ref, att_ref)
    half = dq_ref.shape[1]
    out[:, :half] = mm(h_ref[...], dq_ref[...], ((0,), (0,))).astype(bf16)
    g_out = mm(att_ref[...], g_ref[...], ((0,), (0,))).astype(bf16)
    for i in range(half // share):
        rows = slice(i * share, (i + 1) * share)
        out[2 * i * share : (2 * i + 1) * share, half:] = g_out[rows, : D // 2]
        out[(2 * i + 1) * share : (2 * i + 2) * share, half:] = g_out[rows, D // 2 :]


def query_plain_kernel(x_ref, c_ref, s_ref, dq_ref, att_ref):
    side_by_side(x_ref, c_ref, s_ref, dq_ref, att_ref)


def query_grads(x, cos_tab, sine_tab, hidden, cotangent, share):
    members, rows, _ = x.shape
    half = members * HEAD_DIM
    vmem = pl.BlockSpec(memory_space=pltpu.VMEM)
    flat = jax.ShapeDtypeStruct((rows, half), bf16)
    params = pltpu.CompilerParams(vmem_limit_bytes=VMEM_LIMIT)
    if share % 32 == 0:
        return pl.pallas_call(
            functools.partial(query_grad_kernel, share),
            in_specs=[vmem] * 5,
            out_specs=[vmem] * 3,
            out_shape=[flat, flat, jax.ShapeDtypeStruct((D, D), bf16)],
            compiler_params=params,
            name="query_grads",
        )(x, cos_tab, sine_tab, hidden, cotangent)
    d_query, attended = pl.pallas_call(
        query_plain_kernel,
        in_specs=[vmem] * 3,
        out_specs=[vmem] * 2,
        out_shape=[flat, flat],
        compiler_params=params,
        name="query_plain",
    )(x, cos_tab, sine_tab)
    g_query = mm(hidden, d_query, ((0,), (0,))).astype(bf16)
    g_out = mm(attended, cotangent, ((0,), (0,))).astype(bf16)
    packed = g_out.reshape(half // share, share, 2, D // 2).transpose(0, 2, 1, 3)
    return d_query, attended, jnp.concatenate([g_query, packed.reshape(D, D // 2)], axis=1)


def key_grad_kernel(x_ref, c_ref, s_ref, h_ref, dkv_ref, out):
    half = dkv_ref.shape[1] // 2
    side_by_side(x_ref, c_ref, s_ref, dkv_ref.at[:, :half], dkv_ref.at[:, half:])
    out[...] = mm(h_ref[...], dkv_ref[...], ((0,), (0,))).astype(bf16)


def key_grads(x, cos_tab, sine_tab, hidden):
    members, rows, _ = x.shape
    vmem = pl.BlockSpec(memory_space=pltpu.VMEM)
    return pl.pallas_call(
        key_grad_kernel,
        in_specs=[vmem] * 4,
        out_specs=[vmem, vmem],
        out_shape=[
            jax.ShapeDtypeStruct((rows, 2 * members * HEAD_DIM), bf16),
            jax.ShapeDtypeStruct((D, D), bf16),
        ],
        compiler_params=pltpu.CompilerParams(vmem_limit_bytes=VMEM_LIMIT),
        name="key_grads",
    )(x, cos_tab, sine_tab, hidden)


def place_kernel(sel, near_one, far_one, near_two, far_two, near_out, far_out, out):
    step = pl.program_id(0)
    rows = out.shape[1]
    half = D // 2
    at = pl.multiple_of(step % 2 * rows, rows)
    take = pl.ds(at, rows)

    def attn_slot(ones, twos):
        for top in range(2):
            for part in range(2):
                first = part * half
                one = ones[top]
                two = twos[top]
                out[top, :, first : first + half] = one[0, part, take, :half].astype(f32)
                first = first + D
                out[top, :, first : first + half] = two[0, part, take, :half].astype(f32)
                first = first + D
                out[top, :, first : first + half] = two[0, part, take, half:].astype(f32)

    def feed_slot(ones, twos):
        for top in range(2):
            for part in range(2):
                first = 2 * part * D
                out[top, :, first : first + D] = ones[top][0, part, take, :].astype(f32)
                first = first + D
                out[top, :, first : first + D] = twos[top][0, part, take, :].astype(f32)

    def last_columns(source):
        for part in range(2):
            for side in range(2):
                first = 3 * D + side * half
                picked = source[0, part, side * rows : side * rows + rows, :]
                out[part, :, first : first + half] = picked.astype(f32)

    for slot, fill in enumerate((attn_slot, feed_slot)):
        for own in range(2):
            @pl.when((sel[0] == slot) & (sel[1] == own))
            def _():
                if own == 0:
                    fill((near_one, far_one), (near_two, far_two))
                else:
                    fill((far_one, near_one), (far_two, near_two))

    use_near = (step < pl.num_programs(0) // 2) == (sel[1] == 0)

    @pl.when((sel[0] == 0) & use_near)
    def _():
        last_columns(near_out)

    @pl.when((sel[0] == 0) & jnp.logical_not(use_near))
    def _():
        last_columns(far_out)


def place_slot(near_one, far_one, near_two, far_two, sel):
    half = near_one.shape[0]
    rows = near_one.shape[2]
    shape = (1, 2, rows, D)

    def by_pair(offset):
        return pl.BlockSpec(shape, lambda i, sel: ((i // 2) ^ sel[offset], 0, 0, 0))

    def out_spec(own):
        def index(i, sel):
            used = (sel[0] == 0) & ((i < half) == (sel[1] == own))
            return (jnp.where(used, (i % half) ^ sel[2], half - 1), 0, 0, 1)

        return pl.BlockSpec((1, 2, rows, D // 2), index)

    placed = pl.pallas_call(
        place_kernel,
        grid_spec=pltpu.PrefetchScalarGridSpec(
            num_scalar_prefetch=1,
            grid=(2 * half,),
            in_specs=[by_pair(2), by_pair(2), by_pair(3), by_pair(3), out_spec(0), out_spec(1)],
            out_specs=pl.BlockSpec((2, rows // 2, FF), lambda i, sel: (0, i, 0)),
        ),
        out_shape=jax.ShapeDtypeStruct((2, D // 2, FF), f32),
        compiler_params=pltpu.CompilerParams(vmem_limit_bytes=VMEM_LIMIT),
        name="place",
    )(sel, near_one, far_one, near_two, far_two, near_one, far_one)
    return placed.reshape(D, FF)


def body(inputs, cotangent, doc_lengths, pad_counts, ln_gain, ln_bias,
         w_first, b_first, w_second, b_second):
    rows = inputs.shape[0]
    count = lax.axis_size("seq")
    span = SEQ_LEN // rows
    lead = span // 2
    members = span // 2
    half = members * HEAD_DIM
    half_ff = FF // 2
    seq_at = lax.axis_index("seq")
    branch = lax.axis_index("pair")
    on_first = branch == 0
    block_at = (seq_at - lead) % count
    seq_no = block_at // span
    block_in = block_at % span
    place = block_in // 2
    parity = block_in % 2

    def device_of(block):
        return (block + lead) % count

    def seq_swap(bit):
        return [(i, i ^ bit) for i in range(count)]

    core_swap = [(device_of(b), device_of(b ^ 1)) for b in range(count)]

    weights = w_first[0]
    ids = jnp.arange(rows, dtype=jnp.int32)

    widened = inputs.astype(f32)
    centred = widened - jnp.mean(widened, axis=1, keepdims=True)
    rstd = lax.rsqrt(jnp.mean(centred * centred, axis=1, keepdims=True) + epsilon)
    hidden = (centred * rstd * ln_gain + ln_bias).astype(bf16)

    core = parity
    half_d = D // 2
    to_second = [(2 * i, 2 * i + 1) for i in range(count)]
    to_first = [(2 * i + 1, 2 * i) for i in range(count)]
    both_ways = [(0, 1), (1, 0)]

    def my_rows(at, width):
        return lax.dynamic_slice(weights, (core * half_d, at), (half_d, width))

    def columns(slot_part, index):
        at = slot_part * D + index * half
        return weights[:, at : at + half]

    def both_cores(got):
        other = lax.ppermute(got, "seq", core_swap)
        return (jnp.where(core == 0, got, other), jnp.where(core == 0, other, got))

    out_second = lax.dynamic_slice(weights, (half, 3 * D + core * half_d), (half, half_d))
    kv_sent = jnp.concatenate([my_rows(j * D + half, half) for j in (1, 2)], axis=1)
    kv_crossed = lax.ppermute(kv_sent, ("seq", "pair"), to_second)
    qo_sent = after(jnp.concatenate([my_rows(half, half), out_second], axis=1), kv_crossed)
    qo_crossed = lax.ppermute(qo_sent, ("seq", "pair"), to_second)
    up_crossed = lax.ppermute(my_rows(0, half_ff), ("seq", "pair"), to_first)
    b_other = lax.ppermute(b_first, "pair", both_ways)
    own_blocks = 2 * jnp.arange(members, dtype=jnp.int32) + parity
    own_pos = (own_blocks[:, None] * rows + ids[None, :]).reshape(-1)
    cos_q, sine_q = rotation_tables(block_in * rows + ids, 64)
    kv_low, kv_high = both_cores(kv_crossed)
    w_kv = jnp.where(
        on_first,
        jnp.concatenate([columns(1, 0), columns(2, 0)], axis=1),
        jnp.concatenate([kv_low, kv_high], axis=0),
    )
    b_attn = jnp.where(on_first, b_first[0], b_other[0])
    b_q, b_k, b_v = (
        lax.dynamic_slice(b_attn, (j * D + branch * half,), (half,)) for j in range(3)
    )
    kv_heads = project(
        hidden, hidden, w_kv[:, :half], w_kv[:, half:], b_k, b_v, cos_q, sine_q, False
    )
    qo_low, qo_high = both_cores(after(qo_crossed, kv_heads))
    w_q = jnp.where(
        on_first, columns(0, 0), jnp.concatenate([qo_low[:, :half], qo_high[:, :half]], axis=0)
    )
    w_out = jnp.where(
        on_first,
        weights[:half, 3 * D :],
        jnp.concatenate([qo_low[:, half:], qo_high[:, half:]], axis=1),
    )

    groups = [
        [device_of(n * span + 2 * m + k) for m in range(members)]
        for n in range(count // span)
        for k in range(2)
    ]

    def spread(blocks):
        return lax.all_to_all(blocks, "seq", 0, 0, axis_index_groups=groups)

    kv_own = spread(kv_heads)
    kv_other = lax.ppermute(kv_own, "seq", core_swap)
    qd_heads = project(
        hidden, cotangent, w_q, w_out, b_q, jnp.zeros_like(b_q), cos_q, sine_q, True
    )
    qd_own = spread(qd_heads)

    bits = list(range(count.bit_length() - 1))
    path_one = list(bits)
    path_two = [bits[0], bits[2], bits[1]] + bits[3:]

    def in_path(index, path):
        moved = [((index >> b) & 1) << (len(path) - 1 - i) for i, b in enumerate(path)]
        return functools.reduce(lambda x, y: x | y, moved)

    up_low, up_high = both_cores(up_crossed)
    w_up = jnp.where(on_first, jnp.concatenate([up_low, up_high], axis=0), weights[:, half_ff:])
    w_up = after(w_up, kv_other, qd_heads)
    b_up = jnp.where(on_first, b_other[0, :half_ff], b_first[0, half_ff:])
    w_down = lax.dynamic_slice(w_second, (branch * half_ff, 0), (half_ff, D))
    root_half = 0.7071067811865476
    up_proj = mm(hidden, w_up, ((1,), (0,))) + b_up
    cdf = 0.5 * (1.0 + lax.erf(up_proj * root_half))
    active = (up_proj * cdf).astype(bf16)
    slope = cdf + up_proj * jnp.exp(up_proj * up_proj * -0.5) * 0.3989422804014327
    d_active = mm(cotangent, w_down, ((1,), (1,)))
    d_up = (d_active * slope).astype(bf16)
    orders = [[in_path(i, path) for i in range(count)] for path in (path_one, path_two)]
    g_feed = feed_grads(hidden, d_up, active, cotangent, orders)
    up_bias = jnp.sum(d_up, axis=0, dtype=f32)
    feed_shard = lax.psum_scatter(g_feed, "seq", scatter_dimension=0, tiled=True)[0]

    def scatter_step(array, b):
        size, cols = array.shape
        bit = (seq_at >> b) & 1
        split = array.reshape(2, size // 2, cols)
        keep = lax.dynamic_index_in_dim(split, bit, 0, keepdims=False)
        send = lax.dynamic_index_in_dim(split, 1 - bit, 0, keepdims=False)
        got = lax.ppermute(send, "seq", seq_swap(1 << b))
        return (keep.astype(f32) + got.astype(f32)).astype(bf16)

    def gather_step(array, b):
        return jnp.concatenate([array, lax.ppermute(array, "seq", seq_swap(1 << b))], axis=0)

    doc_row = lax.dynamic_index_in_dim(doc_lengths, seq_no, 0, keepdims=False)
    pads = lax.dynamic_index_in_dim(pad_counts, seq_no, 0, keepdims=False)
    bounds = jnp.cumsum(doc_row)
    start = jnp.max(jnp.where(bounds[:, None] <= own_pos[None, :], bounds[:, None], 0), axis=0)
    lo = jnp.where(own_pos >= SEQ_LEN - pads, own_pos, start)
    lo = lo.reshape(-1, BQ)
    scal = jnp.concatenate([parity[None], lo[:, 0]]).astype(jnp.int32)
    qd_own = after(qd_own, g_feed)
    dq_att, dkv_own, dkv_send = attend(scal, lo, qd_own, kv_own, kv_other)
    dkv_got = lax.ppermute(dkv_send, "seq", core_swap)
    active = after(active, dq_att)
    d_up = after(d_up, dq_att)
    feed_out = mm(active, w_down, ((1,), (0,)))
    d_hidden_feed = mm(d_up, w_up, ((1,), (1,)))
    dq_att = spread(dq_att)
    d_kv = join(dkv_own, dkv_got)
    dq_att, d_kv, feed_out, d_hidden_feed = lax.optimization_barrier(
        (dq_att, d_kv, feed_out, d_hidden_feed)
    )
    d_kv = spread(d_kv)

    share = half // count
    d_query, attended, g_one = query_grads(dq_att, cos_q, sine_q, hidden, cotangent, share)
    attn_one = scatter_step(scatter_step(g_one, path_one[0]), path_one[1])
    d_hidden = mm(d_query, w_q, ((1,), (1,))) + d_hidden_feed
    out_part = mm(attended, w_out, ((1,), (0,))) + feed_out
    out_low = (out_part + jnp.where(on_first, b_first[0, 3 * D :], 0.0)).astype(bf16)
    d_kv, feed_shard, attn_one, d_hidden, out_low = lax.optimization_barrier(
        (d_kv, feed_shard, attn_one, d_hidden, out_low)
    )
    down_all = lax.all_gather(feed_shard[2:], "seq", axis=0)

    d_keys, g_two = key_grads(d_kv, cos_q, sine_q, hidden)
    d_hidden = d_hidden + mm(d_keys, w_kv, ((1,), (1,)))
    d_hidden_low = d_hidden.astype(bf16)

    def in_half(vector):
        zero = jnp.zeros_like(vector)
        return jnp.stack([jnp.where(on_first, vector, zero), jnp.where(on_first, zero, vector)])

    normal = centred * rstd
    q_bias = jnp.sum(d_query, axis=0, dtype=f32)
    kv_bias = jnp.sum(d_keys, axis=0, dtype=f32)
    qkv_bias = jnp.concatenate([q_bias, kv_bias]).reshape(3, half)
    cot_sum = jnp.where(on_first, jnp.sum(cotangent, axis=0, dtype=f32), 0.0)
    small = jnp.concatenate(
        [
            in_half(qkv_bias).transpose(1, 0, 2).reshape(-1),
            in_half(up_bias).reshape(-1),
            cot_sum,
            jnp.sum(d_hidden * normal, axis=0),
            jnp.sum(d_hidden, axis=0),
        ]
    ).reshape(-1, 128)

    attn_two = g_two
    ahead = list(path_one[2:])
    for i, b in enumerate(path_two):
        if ahead:
            attn_one = scatter_step(attn_one, ahead.pop(0))
        attn_two = scatter_step(attn_two, b)
        attn_one, attn_two = lax.optimization_barrier((attn_one, attn_two))
        if i == 1:
            attn_two, d_hidden_low, small = lax.optimization_barrier(
                (attn_two, d_hidden_low, small)
            )

    attn_both = jnp.stack([attn_one, attn_two])
    feed_both = feed_shard[:2]
    other = lax.ppermute(jnp.where(on_first, feed_both, attn_both), "pair", both_ways)
    zero_slot = jnp.where(on_first, attn_both, other)
    one_slot = jnp.where(on_first, other, feed_both)
    near_one = jnp.stack([zero_slot[0], one_slot[0]])[None]
    near_two = jnp.stack([zero_slot[1], one_slot[1]])[None]
    crossed = after(jnp.stack([out_low, d_hidden_low]), near_one, near_two)
    crossed = lax.ppermute(crossed, "pair", both_ways)
    small = small + lax.ppermute(small, "pair", both_ways)
    for i in range(len(bits) - 1, 0, -1):
        near_one = gather_step(near_one, path_one[i])
        near_two = gather_step(near_two, path_two[i])
        small = small + lax.ppermute(small, "seq", seq_swap(1 << path_two[i]))
        near_one, near_two, small = lax.optimization_barrier((near_one, near_two, small))
        if i == 2:
            crossed, down_all = lax.optimization_barrier((crossed, down_all, near_two))[:2]
    outputs = (widened + b_second + (out_low.astype(f32) + crossed[0].astype(f32))).astype(bf16)
    e = (d_hidden_low.astype(f32) + crossed[1].astype(f32)) * ln_gain
    d_norm = rstd * (
        e
        - jnp.mean(e, axis=1, keepdims=True)
        - normal * jnp.mean(e * normal, axis=1, keepdims=True)
    )
    d_inputs = (cotangent.astype(f32) + d_norm).astype(bf16)

    my_one = in_path(seq_at, path_one)
    my_two = in_path(seq_at, path_two)
    d_w_second = down_all.transpose(1, 0, 2, 3).reshape(half_ff, D).astype(f32)
    near_two, outputs, d_inputs, d_w_second = lax.optimization_barrier(
        (near_two, outputs, d_inputs, d_w_second)
    )
    far_two = lax.ppermute(near_two, "seq", seq_swap(1 << path_two[0]))
    small = small + lax.ppermute(small, "seq", seq_swap(1 << path_two[0]))
    far_one = lax.ppermute(near_one, "seq", seq_swap(1 << path_one[0]))
    small = small.reshape(-1)
    if share % 32 == 0:
        low_bits = count // 2 - 1
        sel = jnp.stack([branch, core, my_one & low_bits, my_two & low_bits]).astype(jnp.int32)
        d_w_first = place_slot(near_one, far_one, near_two, far_two, sel)
    else:
        order = jnp.arange(count, dtype=jnp.int32)
        full_one = jnp.take(jnp.concatenate([near_one, far_one]), order ^ my_one, axis=0)
        full_two = jnp.take(jnp.concatenate([near_two, far_two]), order ^ my_two, axis=0)
        full_one = full_one.transpose(1, 0, 2, 3).reshape(2, D, D)
        full_two = full_two.transpose(1, 0, 2, 3).reshape(2, D, D)
        unpacked = full_one[:, :, half:].reshape(2, count, 2, share, half)
        unpacked = unpacked.transpose(0, 1, 3, 2, 4).reshape(D, D)
        as_attn = jnp.concatenate(
            [
                full_one[0, :, :half], full_one[1, :, :half],
                full_two[0, :, :half], full_two[1, :, :half],
                full_two[0, :, half:], full_two[1, :, half:],
                unpacked,
            ],
            axis=1,
        )
        as_feed = jnp.concatenate([full_one[0], full_two[0], full_one[1], full_two[1]], axis=1)
        d_w_first = jnp.where(on_first, as_attn, as_feed).astype(f32)

    cot_total = small[3 * D + FF : 4 * D + FF]
    d_b_first = jnp.where(
        on_first, jnp.concatenate([small[: 3 * D], cot_total]), small[3 * D : 3 * D + FF]
    )
    return (
        outputs,
        d_inputs,
        small[4 * D + FF : 5 * D + FF],
        small[5 * D + FF :],
        d_w_first[None],
        d_b_first[None],
        d_w_second,
        cot_total,
    )


def solution(mesh):
    in_specs = (
        P("seq", None),
        P("seq", None),
        P(),
        P(),
        P(),
        P(),
        P("pair", None, None),
        P("pair", None),
        P(),
        P(),
    )
    out_specs = (
        P("seq", None),
        P("seq", None),
        P(),
        P(),
        P("pair", None, None),
        P("pair", None),
        P("pair", None),
        P(),
    )
    return jax.shard_map(body, mesh=mesh, in_specs=in_specs, out_specs=out_specs, check_vma=False)
```

time: 659 us -> 467 us (0.71)
  starting transfers between devices: 149 us -> 72.7 us
  waiting for transfers between devices: 246 us -> 178 us
  local copies, waits for them, and re-layouts: 69.2 us -> 26.5 us
  other arithmetic: 67.3 us -> 46.7 us
  Pallas kernels: 73.1 us -> 93.5 us
  matrix products: 38.5 us -> 26.1 us
  between operations: 3.45 us -> 15.7 us
    ppermute x66 -> x28, starting transfers between devices: 148 us -> 36.3 us  [the longest x8 7.97 us: scatter_step(): got = lax.ppermute(send, 'seq', seq_swap(1 << b))]
    ppermute x66 -> x28, waiting for transfers between devices: 246 us -> 147 us  [the longest x3 66.7 us: body(): small = small + lax.ppermute(small, 'seq', seq_swap(1 << path_two[i]))]
    all_to_all x0 -> x4, starting transfers between devices: none -> 36.2 us  [spread(): return lax.all_to_all(blocks, 'seq', 0, 0, axis_index_groups=groups)]
    all_to_all x0 -> x4, waiting for transfers between devices: none -> 31 us  [spread(): return lax.all_to_all(blocks, 'seq', 0, 0, axis_index_groups=groups)]
    pallas_call x3 -> x7, Pallas kernels: 22.5 us -> 52.2 us  [the longest x1 18.2 us: place_slot(): pl.pallas_call(place_kernel, grid_spec=pltpu.PrefetchScalarGridSpec(num_s...]
    slice x16 -> x7, local copies, waits for them, and re-layouts: 22.4 us -> 4.63 us  [the longest x1 1.7 us: columns(): return weights[:, at:at + half]]
    convert_element_type x16 -> x10, other arithmetic: 23.8 us -> 9.27 us  [the longest x8 4.53 us: scatter_step(): return (keep.astype(f32) + got.astype(f32)).astype(bf16)]
    dot_general x10 -> x7, matrix products: 38.5 us -> 26.1 us  [mm(): lax.dot_general(left, right, (dims, ((), ())), preferred_element_type=f32)]
  transfers between devices with their start and end apart: 69 -> 38, of which waited for: 24 -> 18; matrix products, arithmetic and copies ran while one was open for 20% -> 20% of each run, Pallas kernels for 10% -> 16%
where the time goes in v2:
time: 467 us; the launch traced here: 459 us
  waiting for transfers between devices  178 us (38%)
  Pallas kernels  93.5 us (20%)
  starting transfers between devices  72.7 us (16%)
  other arithmetic  46.7 us (10%)
  local copies, waits for them, and re-layouts  26.5 us (6%)
  matrix products  26.1 us (6%)
  between operations  15.7 us (3%)
    ppermute x3, waiting for transfers between devices, body(): small = small + lax.ppermute(small, 'seq', seq_swap(1 << path_two[i]))  66.7 us
    ppermute x8, waiting for transfers between devices, scatter_step(): got = lax.ppermute(send, 'seq', seq_swap(1 << b))  41.4 us
    pallas_call x1, Pallas kernels, attend(): pl.pallas_call(attend_kernel, in_specs=[pl.BlockSpec(memory_space=pltpu.S...  41.3 us
    all_to_all x4, starting transfers between devices, spread(): return lax.all_to_all(blocks, 'seq', 0, 0, axis_index_groups=groups)  36.2 us
    all_to_all x4, waiting for transfers between devices, spread(): return lax.all_to_all(blocks, 'seq', 0, 0, axis_index_groups=groups)  31 us
    dot_general x7, matrix products, mm(): lax.dot_general(left, right, (dims, ((), ())), preferred_element_type=f32)  26.1 us
    pallas_call x1, Pallas kernels, place_slot(): pl.pallas_call(place_kernel, grid_spec=pltpu.PrefetchScalarGridSpec(num_s...  18.2 us
    ppermute x1, waiting for transfers between devices, body(): qo_crossed = lax.ppermute(qo_sent, ('seq', 'pair'), to_second)  12.4 us
  transfers between devices with their start and end apart: 38, of which 18 were waited for; matrix products, arithmetic and copies ran while one was open for 20% of the time, Pallas kernels for 16%

profile of v2, /device:TPU:0, one launch (start us, length us, event | category | flops | bytes accessed | tf_op | source)
XLA Modules:
  0.0 459.1 jit_solution(6427436873264309949)
XLA Ops:
  26.4 11.4 %collective-permute-done = bf16[512,1024]{1,0:T(8,128)(2,1)S(1)} collective-permute-done((bf16[512,1024]{1,0:T(8,128)(2,1)}, bf16[512,1024]{1,0:T(8,128)(2,1)S(1)}, u32[]{:S(2)}, u32[]{:S(2)}) %collective-permute-start) | collective-permute-done | bytes 1048608 | tf_op jit(solution)/shard_map/ppermute | solution.py:490
  37.8 5.3 %collective-permute-start.1 = (bf16[512,1024]{1,0:T(8,128)(2,1)}, bf16[512,1024]{1,0:T(8,128)(2,1)}, u32[]{:S(2)}, u32[]{:S(2)}) collective-permute-start(bf16[512,1024]{1,0:T(8,128)(2,1)} %pad_maximum_fusion.3), channel_id=1, source_target_pairs={{0,1},{2,3},{4,5},{6,7},{8,9},{10,11},{12,13},{14,15},{16,17},{18,... | collective-permute-start | bytes 3145736 | tf_op jit(solution)/shard_map/ppermute | solution.py:492
  47.9 5.2 %project_kv.1 = bf16[8,512,128]{2,1,0:T(8,128)(2,1)} custom-call(bf16[512,1024]{1,0:T(8,128)(2,1)} %fusion.14.x_ref.y_ref.h_ref, bf16[512,1024]{1,0:T(8,128)(2,1)} %fusion.14.x_ref.y_ref.h_ref, bf16[1024,512]{1,0:T(8,128)(2,1)} %get-tuple-element.126.wx, bf16[1024,512]{1,0:T(8,128)(2,1)} %get-tuple-element.125.wy, f32[1,512]{1,0:T(1,128)} %get-tuple-element.146.bx, ...), custom_call_target="tpu_custom_call" | custom-call | tf_op jit(solution)/shard_map/project_kv/pallas_call | solution.py:77
  53.1 12.4 %collective-permute-done.1 = bf16[512,1024]{1,0:T(8,128)(2,1)} collective-permute-done((bf16[512,1024]{1,0:T(8,128)(2,1)}, bf16[512,1024]{1,0:T(8,128)(2,1)}, u32[]{:S(2)}, u32[]{:S(2)}) %collective-permute-start.1) | collective-permute-done | bytes 1048608 | tf_op jit(solution)/shard_map/ppermute | solution.py:492
  68.4 6.9 %all-to-all-start.1 = ((bf16[8,512,128]{2,1,0:T(8,128)(2,1)}), bf16[8,512,128]{2,1,0:T(8,128)(2,1)}, u32[]{:S(2)}, u32[]{:S(2)}) async-start(bf16[8,512,128]{2,1,0:T(8,128)(2,1)} %project_kv.1), calls=%async_computation.1 | async-start | bytes 2097152 | tf_op jit(solution)/shard_map/all_to_all | solution.py:528
  82.5 5.1 %project_q.1 = bf16[8,512,128]{2,1,0:T(8,128)(2,1)} custom-call(bf16[512,1024]{1,0:T(8,128)(2,1)} %fusion.14.x_ref.y_ref.h_ref, bf16[512,1024]{1,0:T(8,128)(2,1)} %g_ref.3, bf16[1024,512]{1,0:T(8,128)(2,1)} %slice_select_fusion.2.wx, bf16[512,1024]{1,0:T(8,128)(2,1)} %slice_select_fusion.1.wy, f32[1,512]{1,0:T(1,128)} %get-tuple-element.144.bx, ...), custom_call_target="tpu_custom_call" | custom-call | tf_op jit(solution)/shard_map/project_q/pallas_call | solution.py:77
  87.6 11.9 %all-to-all-done.1.kv_ref = bf16[8,512,128]{2,1,0:T(8,128)(2,1)} async-done(((bf16[8,512,128]{2,1,0:T(8,128)(2,1)}), bf16[8,512,128]{2,1,0:T(8,128)(2,1)}, u32[]{:S(2)}, u32[]{:S(2)}) %all-to-all-start.1) | async-done | bytes 1048608 | tf_op jit(solution)/shard_map/all_to_all | solution.py:528
  99.5 5.4 %all-to-all-start = ((bf16[8,512,128]{2,1,0:T(8,128)(2,1)}), bf16[8,512,128]{2,1,0:T(8,128)(2,1)S(1)}, u32[]{:S(2)}, u32[]{:S(2)}) async-start(bf16[8,512,128]{2,1,0:T(8,128)(2,1)} %project_q.1), calls=%async_computation | async-start | bytes 2097152 | tf_op jit(solution)/shard_map/all_to_all | solution.py:528
  107.1 4.0 slice_select_fusion
  112.2 4.0 multiply_convert_fusion
  116.2 5.5 %convert_reduce_fusion = (f32[2048]{0:T(1024)}, bf16[512,2048]{1,0:T(8,128)(2,1)}) fusion(f32[512,2048]{1,0:T(8,128)S(1)} %get-tuple-element.154, f32[2048]{0:T(1024)S(1)} %bitcast.174, bf16[512,1024]{1,0:T(8,128)(2,1)S(1)} %copy-done.1, bf16[4096,1024]{1,0:T(8,128)(2,1)S(1)} %bitcast.177, s32[]{:T(128)S(6)} %select_n.327), kind=kOutput, calls=%fused_computation.4 | convolution fusion | flops 2161113088 | bytes 11550724 | tf_op jit(solution)/shard_map/dot_general | solution.py:33
  121.6 9.4 %feed_grads.1 = bf16[16,4,64,1024]{3,2,1,0:T(8,128)(2,1)} custom-call(bf16[512,1024]{1,0:T(8,128)(2,1)} %fusion.14.x_ref.y_ref.h_ref, bf16[512,2048]{1,0:T(8,128)(2,1)} %get-tuple-element.66.u_ref, bf16[512,2048]{1,0:T(8,128)(2,1)} %get-tuple-element.65.a_ref, bf16[512,1024]{1,0:T(8,128)(2,1)} %g_ref.3), custom_call_target="tpu_custom_call" | custom-call | tf_op jit(solution)/shard_map/feed_grads/pallas_call | solution.py:115
  132.1 41.3 %attend.1 = (bf16[8,512,128]{2,1,0:T(8,128)(2,1)}, f32[8,512,128]{2,1,0:T(8,128)}, f32[8,512,128]{2,1,0:T(8,128)}) custom-call(s32[9]{0:T(128)} %pad_add_fusion.scal, s32[8,512]{1,0:T(8,128)} %copy-done.33, bf16[8,512,128]{2,1,0:T(8,128)(2,1)} %copy-done.24, bf16[8,512,128]{2,1,0:T(8,128)(2,1)} %all-to-all-done.1.kv_ref, bf16[8,512,128]{2,1,0:T(8,128)(2,1)} %copy-done.37), custom_call_target="tpu_custom_call" | custom-call | flops 999999995904 | bytes 20000000 | tf_op jit(solution)/shard_map/attend/pallas_call | solution.py:233
  173.4 18.8 %all-to-all-start.2 = ((bf16[8,512,128]{2,1,0:T(8,128)(2,1)}), bf16[8,512,128]{2,1,0:T(8,128)(2,1)S(1)}, u32[]{:S(2)}, u32[]{:S(2)}) async-start(bf16[8,512,128]{2,1,0:T(8,128)(2,1)} %get-tuple-element.62), calls=%async_computation.2 | async-start | bytes 2097152 | tf_op jit(solution)/shard_map/all_to_all | solution.py:528
  192.2 6.7 %fusion.1 = f32[512,1024]{1,0:T(8,128)} fusion(bf16[512,2048]{1,0:T(8,128)(2,1)} %get-tuple-element.65.a_ref, bf16[4096,1024]{1,0:T(8,128)(2,1)} %param.18, s32[]{:T(128)S(6)} %select_n.327), kind=kOutput, calls=%fused_computation.7 | convolution fusion | flops 2147483648 | bytes 8388612 | tf_op jit(solution)/shard_map/dot_general | solution.py:33
  198.9 3.7 fusion.54
  202.6 4.1 join.1
  206.7 14.4 %all-to-all-done.2.x_ref = bf16[8,512,128]{2,1,0:T(8,128)(2,1)S(1)} async-done(((bf16[8,512,128]{2,1,0:T(8,128)(2,1)}), bf16[8,512,128]{2,1,0:T(8,128)(2,1)S(1)}, u32[]{:S(2)}, u32[]{:S(2)}) %all-to-all-start.2) | async-done | bytes 1048608 | tf_op jit(solution)/shard_map/all_to_all | solution.py:528
  222.1 5.4 %query_grads.1 = (bf16[512,512]{1,0:T(8,128)(2,1)}, bf16[512,512]{1,0:T(8,128)(2,1)}, bf16[1024,1024]{1,0:T(8,128)(2,1)}) custom-call(bf16[8,512,128]{2,1,0:T(8,128)(2,1)} %copy-done.11, f32[512,128]{1,0:T(8,128)} %get-tuple-element.152.c_ref, f32[512,128]{1,0:T(8,128)} %get-tuple-element.151.s_ref, bf16[512,1024]{1,0:T(8,128)(2,1)} %fusion.14.x_ref.y_ref.h_ref, ...), custom_call_target="tpu_custom_call" | custom-call | tf_op jit(solution)/shard_map/query_grads/pallas_call | solution.py:309
  230.9 5.1 %all-to-all-start.3 = ((bf16[8,512,128]{2,1,0:T(8,128)(2,1)}), bf16[8,512,128]{2,1,0:T(8,128)(2,1)S(1)}, u32[]{:S(2)}, u32[]{:S(2)}) async-start(bf16[8,512,128]{2,1,0:T(8,128)(2,1)} %join.1), calls=%async_computation.3 | async-start | bytes 2097152 | tf_op jit(solution)/shard_map/all_to_all | solution.py:528
  246.2 15.3 %collective-permute-done.10 = bf16[256,1024]{1,0:T(8,128)(2,1)S(1)} collective-permute-done((bf16[256,1024]{1,0:T(8,128)(2,1)S(1)}, bf16[256,1024]{1,0:T(8,128)(2,1)S(1)}, u32[]{:S(2)}, u32[]{:S(2)}) %collective-permute-start.10) | collective-permute-done | bytes 524320 | tf_op jit(solution)/shard_map/ppermute | solution.py:568
  262.4 4.8 %all-to-all-done.3.x_ref = bf16[8,512,128]{2,1,0:T(8,128)(2,1)S(1)} async-done(((bf16[8,512,128]{2,1,0:T(8,128)(2,1)}), bf16[8,512,128]{2,1,0:T(8,128)(2,1)S(1)}, u32[]{:S(2)}, u32[]{:S(2)}) %all-to-all-start.3) | async-done | bytes 1048608 | tf_op jit(solution)/shard_map/all_to_all | solution.py:528
  268.4 4.9 %key_grads.1 = (bf16[512,1024]{1,0:T(8,128)(2,1)}, bf16[1024,1024]{1,0:T(8,128)(2,1)}) custom-call(bf16[8,512,128]{2,1,0:T(8,128)(2,1)} %copy-done.14, f32[512,128]{1,0:T(8,128)} %get-tuple-element.152.c_ref, f32[512,128]{1,0:T(8,128)} %get-tuple-element.151.s_ref, bf16[512,1024]{1,0:T(8,128)(2,1)} %fusion.14.x_ref.y_ref.h_ref), custom_call_target="tpu_custom_call" | custom-call | tf_op jit(solution)/shard_map/key_grads/pallas_call | solution.py:340
  284.1 14.1 %collective-permute-done.13 = bf16[64,1024]{1,0:T(8,128)(2,1)S(1)} collective-permute-done((bf16[64,1024]{1,0:T(8,128)(2,1)S(1)}, bf16[64,1024]{1,0:T(8,128)(2,1)S(1)}, u32[]{:S(2)}, u32[]{:S(2)}) %collective-permute-start.13) | collective-permute-done | bytes 131104 | tf_op jit(solution)/shard_map/ppermute | solution.py:568
  300.7 6.2 %collective-permute-done.15 = bf16[128,1024]{1,0:T(8,128)(2,1)S(1)} collective-permute-done((bf16[128,1024]{1,0:T(8,128)(2,1)S(1)}, bf16[128,1024]{1,0:T(8,128)(2,1)S(1)}, u32[]{:S(2)}, u32[]{:S(2)}) %collective-permute-start.15) | collective-permute-done | bytes 262176 | tf_op jit(solution)/shard_map/ppermute | solution.py:568
  309.5 5.2 %collective-permute-done.16 = bf16[64,1024]{1,0:T(8,128)(2,1)S(1)} collective-permute-done((bf16[64,1024]{1,0:T(8,128)(2,1)S(1)}, bf16[64,1024]{1,0:T(8,128)(2,1)S(1)}, u32[]{:S(2)}, u32[]{:S(2)}) %collective-permute-start.16) | collective-permute-done | bytes 131104 | tf_op jit(solution)/shard_map/ppermute | solution.py:568
  316.4 4.9 %collective-permute-done.17 = bf16[2,64,1024]{2,1,0:T(8,128)(2,1)S(1)} collective-permute-done((bf16[2,64,1024]{2,1,0:T(8,128)(2,1)S(1)}, bf16[2,64,1024]{2,1,0:T(8,128)(2,1)S(1)}, u32[]{:S(2)}, u32[]{:S(2)}) %collective-permute-start.17) | collective-permute-done | bytes 262176 | tf_op jit(solution)/shard_map/ppermute | solution.py:643
  331.1 23.4 %collective-permute-done.21 = f32[80,128]{1,0:T(8,128)S(1)} collective-permute-done((f32[80,128]{1,0:T(8,128)S(1)}, f32[80,128]{1,0:T(8,128)S(1)}, u32[]{:S(2)}, u32[]{:S(2)}) %collective-permute-start.21) | collective-permute-done | bytes 40992 | tf_op jit(solution)/shard_map/ppermute | solution.py:654
  358.7 19.4 %collective-permute-done.24 = f32[80,128]{1,0:T(8,128)S(1)} collective-permute-done((f32[80,128]{1,0:T(8,128)S(1)}, f32[80,128]{1,0:T(8,128)S(1)}, u32[]{:S(2)}, u32[]{:S(2)}) %collective-permute-start.24) | collective-permute-done | bytes 40992 | tf_op jit(solution)/shard_map/ppermute | solution.py:654
  386.7 23.8 %collective-permute-done.27 = f32[80,128]{1,0:T(8,128)S(1)} collective-permute-done((f32[80,128]{1,0:T(8,128)S(1)}, f32[80,128]{1,0:T(8,128)S(1)}, u32[]{:S(2)}, u32[]{:S(2)}) %collective-permute-start.27) | collective-permute-done | bytes 40992 | tf_op jit(solution)/shard_map/ppermute | solution.py:654
  418.9 4.3 copy.24
  433.9 18.2 %place.1 = f32[2,512,4096]{2,1,0:T(8,128)} custom-call(s32[4]{0:T(128)} %pad_add_fusion.1.sel, bf16[8,2,64,1024]{3,2,1,0:T(8,128)(2,1)} %pad_maximum_fusion.near_one.near_out, bf16[8,2,64,1024]{3,2,1,0:T(8,128)(2,1)} %collective-permute-done.30.far_one.far_out, bf16[8,2,64,1024]{3,2,1,0:T(8,128)(2,1)} %pad_maximum_fusion.1.near_two, ...), custom_call_target="tpu_custom_call" | custom-call | tf_op jit(solution)/shard_map/place/pallas_call | solution.py:422
  (246 shorter events, 113.2 us)
Async XLA Ops:
  7.2 35.9 %collective-permute-start.3 = (f32[1,4096]{1,0:T(1,128)}, f32[1,4096]{1,0:T(1,128)S(1)}, u32[]{:S(2)}, u32[]{:S(2)}) collective-permute-start(f32[1,4096]{1,0:T(1,128)} %param.17), channel_id=1, source_target_pairs={{0,1},{1,0},{2,3},{3,2},{4,5},{5,4},{6,7},{7,6},{8,9},{9,8},{10,11... | collective-permute-start | bytes 49160 | tf_op jit(solution)/shard_map/ppermute | solution.py:494
  13.0 24.8 %collective-permute-start = (bf16[512,1024]{1,0:T(8,128)(2,1)}, bf16[512,1024]{1,0:T(8,128)(2,1)S(1)}, u32[]{:S(2)}, u32[]{:S(2)}) collective-permute-start(bf16[512,1024]{1,0:T(8,128)(2,1)} %pad_maximum_fusion.4), channel_id=1, source_target_pairs={{0,1},{2,3},{4,5},{6,7},{8,9},{10,11},{12,13},{14,15},{16,17},{18,... | collective-permute-start | bytes 3145736 | tf_op jit(solution)/shard_map/ppermute | solution.py:490
  18.3 49.3 %collective-permute-start.5 = (bf16[512,2048]{1,0:T(8,128)(2,1)}, bf16[512,2048]{1,0:T(8,128)(2,1)}, u32[]{:S(2)}, u32[]{:S(2)}) collective-permute-start(bf16[512,2048]{1,0:T(8,128)(2,1)} %dynamic-slice_bitcast_fusion), channel_id=1, source_target_pairs={{1,0},{3,2},{5,4},{7,6},{9,8},{11,10},{13,12},{15,14},{17,16},{19,... | collective-permute-start | bytes 6291464 | tf_op jit(solution)/shard_map/ppermute | solution.py:493
  37.8 27.7 %collective-permute-start.1 = (bf16[512,1024]{1,0:T(8,128)(2,1)}, bf16[512,1024]{1,0:T(8,128)(2,1)}, u32[]{:S(2)}, u32[]{:S(2)}) collective-permute-start(bf16[512,1024]{1,0:T(8,128)(2,1)} %pad_maximum_fusion.3), channel_id=1, source_target_pairs={{0,1},{2,3},{4,5},{6,7},{8,9},{10,11},{12,13},{14,15},{16,17},{18,... | collective-permute-start | bytes 3145736 | tf_op jit(solution)/shard_map/ppermute | solution.py:492
  65.5 9.8 %collective-permute-start.4 = (bf16[512,1024]{1,0:T(8,128)(2,1)}, bf16[512,1024]{1,0:T(8,128)(2,1)S(1)}, u32[]{:S(2)}, u32[]{:S(2)}) collective-permute-start(bf16[512,1024]{1,0:T(8,128)(2,1)} %collective-permute-done.1), channel_id=1, source_target_pairs={{16,18},{18,16},{20,22},{22,20},{24,26},{26,24},{28,30},{30,28},{0... | collective-permute-start | bytes 3145736 | tf_op jit(solution)/shard_map/ppermute | solution.py:485
  67.6 37.6 %collective-permute-start.6 = (bf16[512,2048]{1,0:T(8,128)(2,1)}, bf16[512,2048]{1,0:T(8,128)(2,1)S(1)}, u32[]{:S(2)}, u32[]{:S(2)}) collective-permute-start(bf16[512,2048]{1,0:T(8,128)(2,1)} %collective-permute-done.5), channel_id=1, source_target_pairs={{16,18},{18,16},{20,22},{22,20},{24,26},{26,24},{28,30},{30,28},{0... | collective-permute-start | bytes 6291464 | tf_op jit(solution)/shard_map/ppermute | solution.py:485
  68.4 31.1 %all-to-all-start.1 = ((bf16[8,512,128]{2,1,0:T(8,128)(2,1)}), bf16[8,512,128]{2,1,0:T(8,128)(2,1)}, u32[]{:S(2)}, u32[]{:S(2)}) async-start(bf16[8,512,128]{2,1,0:T(8,128)(2,1)} %project_kv.1), calls=%async_computation.1 | async-start | bytes 2097152 | tf_op jit(solution)/shard_map/all_to_all | solution.py:528
  99.5 31.6 %all-to-all-start = ((bf16[8,512,128]{2,1,0:T(8,128)(2,1)}), bf16[8,512,128]{2,1,0:T(8,128)(2,1)S(1)}, u32[]{:S(2)}, u32[]{:S(2)}) async-start(bf16[8,512,128]{2,1,0:T(8,128)(2,1)} %project_q.1), calls=%async_computation | async-start | bytes 2097152 | tf_op jit(solution)/shard_map/all_to_all | solution.py:528
  104.9 162.3 %reduce-scatter.2.cloned.1.call-start = ((), (), s32[]{:S(2)}) async-start(), calls=%async_computation.5 | async-start | bytes 8912896 | tf_op jit(solution)/shard_map/reduce_scatter | solution.py:560
  173.4 29.2 %collective-permute-start.8 = (f32[8,512,128]{2,1,0:T(8,128)}, f32[8,512,128]{2,1,0:T(8,128)}, u32[]{:S(2)}, u32[]{:S(2)}) collective-permute-start(f32[8,512,128]{2,1,0:T(8,128)} %get-tuple-element.64), channel_id=1, source_target_pairs={{16,18},{18,16},{20,22},{22,20},{24,26},{26,24},{28,30},{30,28},{0... | collective-permute-start | bytes 6291464 | tf_op jit(solution)/shard_map/ppermute | solution.py:583
  173.4 47.7 %all-to-all-start.2 = ((bf16[8,512,128]{2,1,0:T(8,128)(2,1)}), bf16[8,512,128]{2,1,0:T(8,128)(2,1)S(1)}, u32[]{:S(2)}, u32[]{:S(2)}) async-start(bf16[8,512,128]{2,1,0:T(8,128)(2,1)} %get-tuple-element.62), calls=%async_computation.2 | async-start | bytes 2097152 | tf_op jit(solution)/shard_map/all_to_all | solution.py:528
  229.8 8.1 %collective-permute-start.9 = (bf16[512,1024]{1,0:T(8,128)(2,1)}, bf16[512,1024]{1,0:T(8,128)(2,1)}, u32[]{:S(2)}, u32[]{:S(2)}) collective-permute-start(bf16[512,1024]{1,0:T(8,128)(2,1)} %dynamic-slice_bitcast_fusion.2), channel_id=1, source_target_pairs={{0,2},{2,0},{4,6},{6,4},{8,10},{10,8},{12,14},{14,12},{16,18},{18,... | collective-permute-start | bytes 3145736 | tf_op jit(solution)/shard_map/ppermute | solution.py:568
  230.9 36.3 %all-to-all-start.3 = ((bf16[8,512,128]{2,1,0:T(8,128)(2,1)}), bf16[8,512,128]{2,1,0:T(8,128)(2,1)S(1)}, u32[]{:S(2)}, u32[]{:S(2)}) async-start(bf16[8,512,128]{2,1,0:T(8,128)(2,1)} %join.1), calls=%async_computation.3 | async-start | bytes 2097152 | tf_op jit(solution)/shard_map/all_to_all | solution.py:528
  236.0 177.6 %all-gather.3.cloned.1.call-start = ((), (), s32[]{:S(2)}) async-start(), calls=%async_computation.6 | async-start | bytes 4456448 | tf_op jit(solution)/shard_map/all_gather | solution.py:604
  239.8 21.6 %collective-permute-start.10 = (bf16[256,1024]{1,0:T(8,128)(2,1)S(1)}, bf16[256,1024]{1,0:T(8,128)(2,1)S(1)}, u32[]{:S(2)}, u32[]{:S(2)}) collective-permute-start(bf16[256,1024]{1,0:T(8,128)(2,1)S(1)} %dynamic-slice_bitcast_fusion.4), channel_id=1, source_target_pairs={{0,4},{2,6},{4,0},{6,2},{8,12},{10,14},{12,8},{14,10},{16,20},{18,... | collective-permute-start | bytes 1572872 | tf_op jit(solution)/shard_map/ppermute | solution.py:568
  268.3 12.1 %collective-permute-start.11 = (bf16[128,1024]{1,0:T(8,128)(2,1)S(1)}, bf16[128,1024]{1,0:T(8,128)(2,1)}, u32[]{:S(2)}, u32[]{:S(2)}) collective-permute-start(bf16[128,1024]{1,0:T(8,128)(2,1)S(1)} %dynamic-slice_bitcast_fusion.10), channel_id=1, source_target_pairs={{0,8},{2,10},{4,12},{6,14},{8,0},{10,2},{12,4},{14,6},{16,24},{18,... | collective-permute-start | bytes 786440 | tf_op jit(solution)/shard_map/ppermute | solution.py:568
  281.9 17.0 %collective-permute-start.14 = (bf16[256,1024]{1,0:T(8,128)(2,1)S(1)}, bf16[256,1024]{1,0:T(8,128)(2,1)S(1)}, u32[]{:S(2)}, u32[]{:S(2)}) collective-permute-start(bf16[256,1024]{1,0:T(8,128)(2,1)S(1)} %dynamic-slice_bitcast_fusion.3), channel_id=1, source_target_pairs={{0,8},{2,10},{4,12},{6,14},{8,0},{10,2},{12,4},{14,6},{16,24},{18,... | collective-permute-start | bytes 1572872 | tf_op jit(solution)/shard_map/ppermute | solution.py:568
  284.0 14.2 %collective-permute-start.13 = (bf16[64,1024]{1,0:T(8,128)(2,1)S(1)}, bf16[64,1024]{1,0:T(8,128)(2,1)S(1)}, u32[]{:S(2)}, u32[]{:S(2)}) collective-permute-start(bf16[64,1024]{1,0:T(8,128)(2,1)S(1)} %dynamic-slice_bitcast_fusion.12), channel_id=1, source_target_pairs={{0,16},{2,18},{4,20},{6,22},{8,24},{10,26},{12,28},{14,30},{16,0},... | collective-permute-start | bytes 393224 | tf_op jit(solution)/shard_map/ppermute | solution.py:568
  299.2 7.7 %collective-permute-start.15 = (bf16[128,1024]{1,0:T(8,128)(2,1)S(1)}, bf16[128,1024]{1,0:T(8,128)(2,1)S(1)}, u32[]{:S(2)}, u32[]{:S(2)}) collective-permute-start(bf16[128,1024]{1,0:T(8,128)(2,1)S(1)} %dynamic-slice_bitcast_fusion.9), channel_id=1, source_target_pairs={{0,4},{2,6},{4,0},{6,2},{8,12},{10,14},{12,8},{14,10},{16,20},{18,... | collective-permute-start | bytes 786440 | tf_op jit(solution)/shard_map/ppermute | solution.py:568
  307.0 7.7 %collective-permute-start.16 = (bf16[64,1024]{1,0:T(8,128)(2,1)S(1)}, bf16[64,1024]{1,0:T(8,128)(2,1)S(1)}, u32[]{:S(2)}, u32[]{:S(2)}) collective-permute-start(bf16[64,1024]{1,0:T(8,128)(2,1)S(1)} %dynamic-slice_bitcast_fusion.11), channel_id=1, source_target_pairs={{0,16},{2,18},{4,20},{6,22},{8,24},{10,26},{12,28},{14,30},{16,0},... | collective-permute-start | bytes 393224 | tf_op jit(solution)/shard_map/ppermute | solution.py:568
  314.8 6.4 %collective-permute-start.17 = (bf16[2,64,1024]{2,1,0:T(8,128)(2,1)S(1)}, bf16[2,64,1024]{2,1,0:T(8,128)(2,1)S(1)}, u32[]{:S(2)}, u32[]{:S(2)}) collective-permute-start(bf16[2,64,1024]{2,1,0:T(8,128)(2,1)S(1)} %broadcast_select_fusion.8), channel_id=1, source_target_pairs={{0,1},{1,0},{2,3},{3,2},{4,5},{5,4},{6,7},{7,6},{8,9},{9,8},{10,11... | collective-permute-start | bytes 786440 | tf_op jit(solution)/shard_map/ppermute | solution.py:643
  323.3 31.2 %collective-permute-start.18 = (bf16[1,2,64,1024]{3,2,1,0:T(8,128)(2,1)S(1)}, bf16[1,2,64,1024]{3,2,1,0:T(8,128)(2,1)S(1)}, u32[]{:S(2)}, u32[]{:S(2)}) collective-permute-start(bf16[1,2,64,1024]{3,2,1,0:T(8,128)(2,1)S(1)} %maximum_bitcast_fusion), channel_id=1, source_target_pairs={{0,16},{2,18},{4,20},{6,22},{8,24},{10,26},{12,28},{14,30},{16,0},... | collective-permute-start | bytes 786440 | tf_op jit(solution)/shard_map/ppermute | solution.py:572
  324.1 30.5 %collective-permute-start.19 = (bf16[1,2,64,1024]{3,2,1,0:T(8,128)(2,1)S(1)}, bf16[1,2,64,1024]{3,2,1,0:T(8,128)(2,1)S(1)}, u32[]{:S(2)}, u32[]{:S(2)}) collective-permute-start(bf16[1,2,64,1024]{3,2,1,0:T(8,128)(2,1)S(1)} %maximum_bitcast_fusion.1), channel_id=1, source_target_pairs={{0,16},{2,18},{4,20},{6,22},{8,24},{10,26},{12,28},{14,30},{16,0},... | collective-permute-start | bytes 786440 | tf_op jit(solution)/shard_map/ppermute | solution.py:572
  330.4 24.1 %collective-permute-start.21 = (f32[80,128]{1,0:T(8,128)S(1)}, f32[80,128]{1,0:T(8,128)S(1)}, u32[]{:S(2)}, u32[]{:S(2)}) collective-permute-start(f32[80,128]{1,0:T(8,128)S(1)} %add.319), channel_id=1, source_target_pairs={{0,16},{2,18},{4,20},{6,22},{8,24},{10,26},{12,28},{14,30},{16,0},... | collective-permute-start | bytes 122888 | tf_op jit(solution)/shard_map/ppermute | solution.py:654
  354.6 26.6 %collective-permute-start.22 = (bf16[2,2,64,1024]{3,2,1,0:T(8,128)(2,1)S(1)}, bf16[2,2,64,1024]{3,2,1,0:T(8,128)(2,1)S(1)}, u32[]{:S(2)}, u32[]{:S(2)}) collective-permute-start(bf16[2,2,64,1024]{3,2,1,0:T(8,128)(2,1)S(1)} %pad_maximum_fusion.7), channel_id=1, source_target_pairs={{0,8},{2,10},{4,12},{6,14},{8,0},{10,2},{12,4},{14,6},{16,24},{18,... | collective-permute-start | bytes 1572872 | tf_op jit(solution)/shard_map/ppermute | solution.py:572
  354.9 58.6 %collective-permute-start.28 = (bf16[2,512,1024]{2,1,0:T(8,128)(2,1)S(1)}, bf16[2,512,1024]{2,1,0:T(8,128)(2,1)}, u32[]{:S(2)}, u32[]{:S(2)}) collective-permute-start(bf16[2,512,1024]{2,1,0:T(8,128)(2,1)S(1)} %pad_maximum_fusion.2), channel_id=1, source_target_pairs={{0,1},{1,0},{2,3},{3,2},{4,5},{5,4},{6,7},{7,6},{8,9},{9,8},{10,11... | collective-permute-start | bytes 6291464 | tf_op jit(solution)/shard_map/ppermute | solution.py:649
  356.7 24.6 %collective-permute-start.23 = (bf16[2,2,64,1024]{3,2,1,0:T(8,128)(2,1)S(1)}, bf16[2,2,64,1024]{3,2,1,0:T(8,128)(2,1)S(1)}, u32[]{:S(2)}, u32[]{:S(2)}) collective-permute-start(bf16[2,2,64,1024]{3,2,1,0:T(8,128)(2,1)S(1)} %pad_maximum_fusion.8), channel_id=1, source_target_pairs={{0,4},{2,6},{4,0},{6,2},{8,12},{10,14},{12,8},{14,10},{16,20},{18,... | collective-permute-start | bytes 1572872 | tf_op jit(solution)/shard_map/ppermute | solution.py:572
  358.1 20.0 %collective-permute-start.24 = (f32[80,128]{1,0:T(8,128)S(1)}, f32[80,128]{1,0:T(8,128)S(1)}, u32[]{:S(2)}, u32[]{:S(2)}) collective-permute-start(f32[80,128]{1,0:T(8,128)S(1)} %add.320), channel_id=1, source_target_pairs={{0,4},{2,6},{4,0},{6,2},{8,12},{10,14},{12,8},{14,10},{16,20},{18,... | collective-permute-start | bytes 122888 | tf_op jit(solution)/shard_map/ppermute | solution.py:654
  381.4 29.1 %collective-permute-start.25 = (bf16[4,2,64,1024]{3,2,1,0:T(8,128)(2,1)S(1)}, bf16[4,2,64,1024]{3,2,1,0:T(8,128)(2,1)S(1)}, u32[]{:S(2)}, u32[]{:S(2)}) collective-permute-start(bf16[4,2,64,1024]{3,2,1,0:T(8,128)(2,1)S(1)} %pad_maximum_fusion.5), channel_id=1, source_target_pairs={{0,4},{2,6},{4,0},{6,2},{8,12},{10,14},{12,8},{14,10},{16,20},{18,... | collective-permute-start | bytes 3145736 | tf_op jit(solution)/shard_map/ppermute | solution.py:572
  384.6 27.4 %collective-permute-start.26 = (bf16[4,2,64,1024]{3,2,1,0:T(8,128)(2,1)S(1)}, bf16[4,2,64,1024]{3,2,1,0:T(8,128)(2,1)S(1)}, u32[]{:S(2)}, u32[]{:S(2)}) collective-permute-start(bf16[4,2,64,1024]{3,2,1,0:T(8,128)(2,1)S(1)} %pad_maximum_fusion.6), channel_id=1, source_target_pairs={{0,8},{2,10},{4,12},{6,14},{8,0},{10,2},{12,4},{14,6},{16,24},{18,... | collective-permute-start | bytes 3145736 | tf_op jit(solution)/shard_map/ppermute | solution.py:572
  384.6 25.9 %collective-permute-start.27 = (f32[80,128]{1,0:T(8,128)S(1)}, f32[80,128]{1,0:T(8,128)S(1)}, u32[]{:S(2)}, u32[]{:S(2)}) collective-permute-start(f32[80,128]{1,0:T(8,128)S(1)} %add.321), channel_id=1, source_target_pairs={{0,8},{2,10},{4,12},{6,14},{8,0},{10,2},{12,4},{14,6},{16,24},{18,... | collective-permute-start | bytes 122888 | tf_op jit(solution)/shard_map/ppermute | solution.py:654
  413.5 19.0 %collective-permute-start.30 = (bf16[8,2,64,1024]{3,2,1,0:T(8,128)(2,1)}, bf16[8,2,64,1024]{3,2,1,0:T(8,128)(2,1)}, u32[]{:S(2)}, u32[]{:S(2)}) collective-permute-start(bf16[8,2,64,1024]{3,2,1,0:T(8,128)(2,1)} %pad_maximum_fusion.near_one.near_out), channel_id=1, source_target_pairs={{0,2},{2,0},{4,6},{6,4},{8,10},{10,8},{12,14},{14,12},{16,18},{18,... | collective-permute-start | bytes 6291464 | tf_op jit(solution)/shard_map/ppermute | solution.py:675
  (47 other events, 290.3 us)
Sparse Core Ops, SparseCore 0:
  131.2 120.8 reduce-scatter.1
  322.2 62.5 all-gather.2

commit v3 on v2

--- a/solution.py
+++ b/solution.py
@@ -129,7 +129,7 @@
 
 
 def attend_kernel(scal, lo_ref, qd_ref, kv_ref, kvp_ref, dq_ref, own_ref, send_ref,
-                  kv_s, kvt_s, s_buf, p_buf, acc_s):
+                  kv_s, kvt_s, s_buf, p_buf, acc_s, m_s):
     members, rows, _ = qd_ref.shape
     parity = scal[0]
     scale = HEAD_DIM ** (-0.5)
@@ -169,30 +169,28 @@
         qpos = first + query_iota
         lo = lo_ref[pl.ds(i, 1), :]
 
-        def scores_step(kb, mx):
+        def scores_step(kb, sums):
+            top, total, dots = sums
             at = pl.multiple_of(kb * BK, BK)
             r = mm(kv_s[pl.ds(at, BK), :], both, ((1,), (1,)))
             kpos = at + key_iota
             s = jnp.where((kpos <= qpos) & (kpos >= lo), r[:, :BQ], masked_fill)
+            eights = jnp.max(s.reshape(BK // 8, 8, BQ), axis=0)
+            new_top = jnp.maximum(top, jnp.max(eights, axis=0, keepdims=True))
+            e = jnp.exp2((s - new_top) * to_two)
+            w = e * r[:, BQ:]
             to = pl.multiple_of((kb - kb0) * BK, BK)
-            s_buf[pl.ds(to, BK), :] = s
+            s_buf[pl.ds(to, BK), :] = e
             p_buf[pl.ds(to, BK), :] = r[:, BQ:]
-            return jnp.maximum(mx, jnp.max(s.reshape(BK // 8, 8, BQ), axis=0))
-
-        mx = lax.fori_loop(kb0, kb1, scores_step, jnp.full((8, BQ), masked_fill, f32))
-        top = jnp.max(mx, axis=0, keepdims=True)
-
-        def exp_step(kb, sums):
-            total, dots = sums
-            at = pl.multiple_of((kb - kb0) * BK, BK)
-            e = jnp.exp2((s_buf[pl.ds(at, BK), :] - top) * to_two)
-            s_buf[pl.ds(at, BK), :] = e
-            w = e * p_buf[pl.ds(at, BK), :]
-            return (total + jnp.sum(e.reshape(BK // 8, 8, BQ), axis=0),
-                    dots + jnp.sum(w.reshape(BK // 8, 8, BQ), axis=0))
+            m_s[pl.ds(kb - kb0, 1), :] = new_top
+            shrink = jnp.exp2((top - new_top) * to_two)
+            return (new_top,
+                    total * shrink + jnp.sum(e.reshape(BK // 8, 8, BQ), axis=0),
+                    dots * shrink + jnp.sum(w.reshape(BK // 8, 8, BQ), axis=0))
 
         zeros = jnp.zeros((8, BQ), f32)
-        total, dots = lax.fori_loop(kb0, kb1, exp_step, (zeros, zeros))
+        lowest = jnp.full((1, BQ), masked_fill, f32)
+        top, total, dots = lax.fori_loop(kb0, kb1, scores_step, (lowest, zeros, zeros))
         inv = 1.0 / jnp.sum(total, axis=0, keepdims=True)
         row_dot = jnp.sum(dots, axis=0, keepdims=True) * inv
 
@@ -200,7 +198,8 @@
             dq_t, at_t = outs
             at = pl.multiple_of(kb * BK, BK)
             to = pl.multiple_of((kb - kb0) * BK, BK)
-            p = s_buf[pl.ds(to, BK), :] * inv
+            share = jnp.exp2((m_s[pl.ds(kb - kb0, 1), :] - top) * to_two) * inv
+            p = s_buf[pl.ds(to, BK), :] * share
             ds = p * (p_buf[pl.ds(to, BK), :] - row_dot)
             p_low = p.astype(bf16)
             ds_low = ds.astype(bf16)
@@ -241,6 +240,7 @@
             pltpu.VMEM((MOST_DOC + BQ + BK, BQ), f32),
             pltpu.VMEM((MOST_DOC + BQ + BK, BQ), f32),
             pltpu.VMEM((total, 128), f32),
+            pltpu.VMEM((32, BQ), f32),
         ],
         compiler_params=pltpu.CompilerParams(vmem_limit_bytes=VMEM_LIMIT),
         cost_estimate=pl.CostEstimate(
@@ -350,12 +350,11 @@
     )(x, cos_tab, sine_tab, hidden)
 
 
-def place_kernel(sel, near_one, far_one, near_two, far_two, near_out, far_out, out):
+def place_kernel(sel, near_one, far_one, near_two, far_two, near_a, far_a, near_b, far_b, out):
     step = pl.program_id(0)
     rows = out.shape[1]
     half = D // 2
-    at = pl.multiple_of(step % 2 * rows, rows)
-    take = pl.ds(at, rows)
+    share = rows // 2
 
     def attn_slot(ones, twos):
         for top in range(2):
@@ -363,26 +362,28 @@
                 first = part * half
                 one = ones[top]
                 two = twos[top]
-                out[top, :, first : first + half] = one[0, part, take, :half].astype(f32)
+                out[top, :, first : first + half] = one[0, part, :, :half].astype(f32)
                 first = first + D
-                out[top, :, first : first + half] = two[0, part, take, :half].astype(f32)
+                out[top, :, first : first + half] = two[0, part, :, :half].astype(f32)
                 first = first + D
-                out[top, :, first : first + half] = two[0, part, take, half:].astype(f32)
+                out[top, :, first : first + half] = two[0, part, :, half:].astype(f32)
 
     def feed_slot(ones, twos):
         for top in range(2):
             for part in range(2):
                 first = 2 * part * D
-                out[top, :, first : first + D] = ones[top][0, part, take, :].astype(f32)
+                out[top, :, first : first + D] = ones[top][0, part, :, :].astype(f32)
                 first = first + D
-                out[top, :, first : first + D] = twos[top][0, part, take, :].astype(f32)
-
-    def last_columns(source):
-        for part in range(2):
-            for side in range(2):
-                first = 3 * D + side * half
-                picked = source[0, part, side * rows : side * rows + rows, :]
-                out[part, :, first : first + half] = picked.astype(f32)
+                out[top, :, first : first + D] = twos[top][0, part, :, :].astype(f32)
+
+    def last_columns(sources):
+        for which, source in enumerate(sources):
+            for part in range(2):
+                for side in range(2):
+                    first = 3 * D + side * half
+                    picked = source[0, part, side * share : side * share + share, :]
+                    to = slice(which * share, which * share + share)
+                    out[part, to, first : first + half] = picked.astype(f32)
 
     for slot, fill in enumerate((attn_slot, feed_slot)):
         for own in range(2):
@@ -397,11 +398,11 @@
 
     @pl.when((sel[0] == 0) & use_near)
     def _():
-        last_columns(near_out)
+        last_columns((near_a, near_b))
 
     @pl.when((sel[0] == 0) & jnp.logical_not(use_near))
     def _():
-        last_columns(far_out)
+        last_columns((far_a, far_b))
 
 
 def place_slot(near_one, far_one, near_two, far_two, sel):
@@ -410,12 +411,13 @@
     shape = (1, 2, rows, D)
 
     def by_pair(offset):
-        return pl.BlockSpec(shape, lambda i, sel: ((i // 2) ^ sel[offset], 0, 0, 0))
-
-    def out_spec(own):
+        return pl.BlockSpec(shape, lambda i, sel: (i ^ sel[offset], 0, 0, 0))
+
+    def out_spec(own, which):
         def index(i, sel):
-            used = (sel[0] == 0) & ((i < half) == (sel[1] == own))
-            return (jnp.where(used, (i % half) ^ sel[2], half - 1), 0, 0, 1)
+            block = 2 * i + which
+            used = (sel[0] == 0) & ((block < half) == (sel[1] == own))
+            return (jnp.where(used, (block % half) ^ sel[2], half - 1), 0, 0, 1)
 
         return pl.BlockSpec((1, 2, rows, D // 2), index)
 
@@ -423,14 +425,15 @@
         place_kernel,
         grid_spec=pltpu.PrefetchScalarGridSpec(
             num_scalar_prefetch=1,
-            grid=(2 * half,),
-            in_specs=[by_pair(2), by_pair(2), by_pair(3), by_pair(3), out_spec(0), out_spec(1)],
-            out_specs=pl.BlockSpec((2, rows // 2, FF), lambda i, sel: (0, i, 0)),
+            grid=(half,),
+            in_specs=[by_pair(2), by_pair(2), by_pair(3), by_pair(3)]
+            + [out_spec(own, which) for which in range(2) for own in range(2)],
+            out_specs=pl.BlockSpec((2, rows, FF), lambda i, sel: (0, i, 0)),
         ),
         out_shape=jax.ShapeDtypeStruct((2, D // 2, FF), f32),
         compiler_params=pltpu.CompilerParams(vmem_limit_bytes=VMEM_LIMIT),
         name="place",
-    )(sel, near_one, far_one, near_two, far_two, near_one, far_one)
+    )(sel, near_one, far_one, near_two, far_two, near_one, far_one, near_one, far_one)
     return placed.reshape(D, FF)
 
 
@@ -601,7 +604,7 @@
     d_kv, feed_shard, attn_one, d_hidden, out_low = lax.optimization_barrier(
         (d_kv, feed_shard, attn_one, d_hidden, out_low)
     )
-    down_all = lax.all_gather(feed_shard[2:], "seq", axis=0)
+    down_all = lax.all_gather(feed_shard[2:], "seq", axis=1, tiled=True)
 
     d_keys, g_two = key_grads(d_kv, cos_q, sine_q, hidden)
     d_hidden = d_hidden + mm(d_keys, w_kv, ((1,), (1,)))
@@ -627,16 +630,23 @@
     ).reshape(-1, 128)
 
     attn_two = g_two
+    out_other = lax.ppermute(out_low, "pair", both_ways)
     ahead = list(path_one[2:])
     for i, b in enumerate(path_two):
         if ahead:
             attn_one = scatter_step(attn_one, ahead.pop(0))
         attn_two = scatter_step(attn_two, b)
         attn_one, attn_two = lax.optimization_barrier((attn_one, attn_two))
+        if i == len(path_two) - 1:
+            attn_one, attn_two, down_all = lax.optimization_barrier(
+                (attn_one, attn_two, down_all)
+            )
         if i == 1:
             attn_two, d_hidden_low, small = lax.optimization_barrier(
                 (attn_two, d_hidden_low, small)
             )
+        if i == 2:
+            attn_two, out_other = lax.optimization_barrier((attn_two, out_other))
 
     attn_both = jnp.stack([attn_one, attn_two])
     feed_both = feed_shard[:2]
@@ -645,7 +655,7 @@
     one_slot = jnp.where(on_first, other, feed_both)
     near_one = jnp.stack([zero_slot[0], one_slot[0]])[None]
     near_two = jnp.stack([zero_slot[1], one_slot[1]])[None]
-    crossed = after(jnp.stack([out_low, d_hidden_low]), near_one, near_two)
+    crossed = after(d_hidden_low, near_one, near_two)
     crossed = lax.ppermute(crossed, "pair", both_ways)
     small = small + lax.ppermute(small, "pair", both_ways)
     for i in range(len(bits) - 1, 0, -1):
@@ -655,8 +665,8 @@
         near_one, near_two, small = lax.optimization_barrier((near_one, near_two, small))
         if i == 2:
             crossed, down_all = lax.optimization_barrier((crossed, down_all, near_two))[:2]
-    outputs = (widened + b_second + (out_low.astype(f32) + crossed[0].astype(f32))).astype(bf16)
-    e = (d_hidden_low.astype(f32) + crossed[1].astype(f32)) * ln_gain
+    outputs = (widened + b_second + (out_low.astype(f32) + out_other.astype(f32))).astype(bf16)
+    e = (d_hidden_low.astype(f32) + crossed.astype(f32)) * ln_gain
     d_norm = rstd * (
         e
         - jnp.mean(e, axis=1, keepdims=True)
@@ -666,7 +676,7 @@
 
     my_one = in_path(seq_at, path_one)
     my_two = in_path(seq_at, path_two)
-    d_w_second = down_all.transpose(1, 0, 2, 3).reshape(half_ff, D).astype(f32)
+    d_w_second = down_all.reshape(half_ff, D).astype(f32)
     near_two, outputs, d_inputs, d_w_second = lax.optimization_barrier(
         (near_two, outputs, d_inputs, d_w_second)
     )

time: 467 us -> 444 us (0.951)
  starting transfers between devices: 72.7 us -> 61.1 us
  Pallas kernels: 93.5 us -> 87.3 us
  local copies, waits for them, and re-layouts: 26.5 us -> 20.4 us
  waiting for transfers between devices: 178 us -> 183 us
    ppermute x3, waiting for transfers between devices: 66.7 us -> 33.4 us  [body(): small = small + lax.ppermute(small, 'seq', seq_swap(1 << path_two[i]))]
    all_to_all x4, starting transfers between devices: 36.2 us -> 22.7 us  [spread(): return lax.all_to_all(blocks, 'seq', 0, 0, axis_index_groups=groups)]
    ppermute x8, waiting for transfers between devices: 41.4 us -> 54.7 us  [scatter_step(): got = lax.ppermute(send, 'seq', seq_swap(1 << b))]
    all_to_all x4, waiting for transfers between devices: 31 us -> 43.4 us  [spread(): return lax.all_to_all(blocks, 'seq', 0, 0, axis_index_groups=groups)]
    ppermute x1, starting transfers between devices: 0.01 us -> 7.66 us  [body(): dkv_got = lax.ppermute(dkv_send, 'seq', core_swap)]
    pallas_call x1, Pallas kernels: 18.2 us -> 12.4 us  [place_slot(): pl.pallas_call(place_kernel, grid_spec=pltpu.PrefetchScalarGridSpec(num_s...]
  transfers between devices with their start and end apart: 38 -> 39, of which waited for: 18 -> 20; matrix products, arithmetic and copies ran while one was open for 20% -> 19% of each run, Pallas kernels for 16% -> 17%
where the time goes in v3:
time: 444 us; the launch traced here: 438 us
  waiting for transfers between devices  183 us (41%)
  Pallas kernels  87.3 us (20%)
  starting transfers between devices  61.1 us (14%)
  other arithmetic  46.5 us (10%)
  matrix products  24.1 us (5%)
  local copies, waits for them, and re-layouts  20.4 us (5%)
  between operations  16 us (4%)
    ppermute x8, waiting for transfers between devices, scatter_step(): got = lax.ppermute(send, 'seq', seq_swap(1 << b))  54.7 us
    all_to_all x4, waiting for transfers between devices, spread(): return lax.all_to_all(blocks, 'seq', 0, 0, axis_index_groups=groups)  43.4 us
    pallas_call x1, Pallas kernels, attend(): pl.pallas_call(attend_kernel, in_specs=[pl.BlockSpec(memory_space=pltpu.S...  40.8 us
    ppermute x3, waiting for transfers between devices, body(): small = small + lax.ppermute(small, 'seq', seq_swap(1 << path_two[i]))  33.4 us
    dot_general x7, matrix products, mm(): lax.dot_general(left, right, (dims, ((), ())), preferred_element_type=f32)  24.1 us
    all_to_all x4, starting transfers between devices, spread(): return lax.all_to_all(blocks, 'seq', 0, 0, axis_index_groups=groups)  22.7 us
    pallas_call x1, Pallas kernels, place_slot(): pl.pallas_call(place_kernel, grid_spec=pltpu.PrefetchScalarGridSpec(num_s...  12.4 us
    ppermute x1, waiting for transfers between devices, body(): qo_crossed = lax.ppermute(qo_sent, ('seq', 'pair'), to_second)  12.3 us
  transfers between devices with their start and end apart: 39, of which 20 were waited for; matrix products, arithmetic and copies ran while one was open for 19% of the time, Pallas kernels for 17%

profile of v3, /device:TPU:0, one launch (start us, length us, event | category | flops | bytes accessed | tf_op | source)
XLA Modules:
  0.0 438.4 jit_solution(17175699366453350054)
XLA Ops:
  26.4 11.4 %collective-permute-done = bf16[512,1024]{1,0:T(8,128)(2,1)S(1)} collective-permute-done((bf16[512,1024]{1,0:T(8,128)(2,1)}, bf16[512,1024]{1,0:T(8,128)(2,1)S(1)}, u32[]{:S(2)}, u32[]{:S(2)}) %collective-permute-start) | collective-permute-done | bytes 1048608 | tf_op jit(solution)/shard_map/ppermute | solution.py:493
  37.8 5.3 %collective-permute-start.1 = (bf16[512,1024]{1,0:T(8,128)(2,1)}, bf16[512,1024]{1,0:T(8,128)(2,1)}, u32[]{:S(2)}, u32[]{:S(2)}) collective-permute-start(bf16[512,1024]{1,0:T(8,128)(2,1)} %pad_maximum_fusion.2), channel_id=1, source_target_pairs={{0,1},{2,3},{4,5},{6,7},{8,9},{10,11},{12,13},{14,15},{16,17},{18,... | collective-permute-start | bytes 3145736 | tf_op jit(solution)/shard_map/ppermute | solution.py:495
  47.9 5.3 %project_kv.1 = bf16[8,512,128]{2,1,0:T(8,128)(2,1)} custom-call(bf16[512,1024]{1,0:T(8,128)(2,1)} %fusion.14.x_ref.y_ref.h_ref, bf16[512,1024]{1,0:T(8,128)(2,1)} %fusion.14.x_ref.y_ref.h_ref, bf16[1024,512]{1,0:T(8,128)(2,1)} %get-tuple-element.134.wx, bf16[1024,512]{1,0:T(8,128)(2,1)} %get-tuple-element.133.wy, f32[1,512]{1,0:T(1,128)} %get-tuple-element.155.bx, ...), custom_call_target="tpu_custom_call" | custom-call | tf_op jit(solution)/shard_map/project_kv/pallas_call | solution.py:77
  53.2 12.3 %collective-permute-done.1 = bf16[512,1024]{1,0:T(8,128)(2,1)} collective-permute-done((bf16[512,1024]{1,0:T(8,128)(2,1)}, bf16[512,1024]{1,0:T(8,128)(2,1)}, u32[]{:S(2)}, u32[]{:S(2)}) %collective-permute-start.1) | collective-permute-done | bytes 1048608 | tf_op jit(solution)/shard_map/ppermute | solution.py:495
  68.4 6.9 %all-to-all-start.1 = ((bf16[8,512,128]{2,1,0:T(8,128)(2,1)}), bf16[8,512,128]{2,1,0:T(8,128)(2,1)}, u32[]{:S(2)}, u32[]{:S(2)}) async-start(bf16[8,512,128]{2,1,0:T(8,128)(2,1)} %project_kv.1), calls=%async_computation.1 | async-start | bytes 2097152 | tf_op jit(solution)/shard_map/all_to_all | solution.py:531
  82.5 5.2 %project_q.1 = bf16[8,512,128]{2,1,0:T(8,128)(2,1)} custom-call(bf16[512,1024]{1,0:T(8,128)(2,1)} %fusion.14.x_ref.y_ref.h_ref, bf16[512,1024]{1,0:T(8,128)(2,1)} %g_ref.3, bf16[1024,512]{1,0:T(8,128)(2,1)} %slice_select_fusion.2.wx, bf16[512,1024]{1,0:T(8,128)(2,1)} %slice_select_fusion.1.wy, f32[1,512]{1,0:T(1,128)} %get-tuple-element.153.bx, ...), custom_call_target="tpu_custom_call" | custom-call | tf_op jit(solution)/shard_map/project_q/pallas_call | solution.py:77
  87.6 11.9 %all-to-all-done.1.kv_ref = bf16[8,512,128]{2,1,0:T(8,128)(2,1)} async-done(((bf16[8,512,128]{2,1,0:T(8,128)(2,1)}), bf16[8,512,128]{2,1,0:T(8,128)(2,1)}, u32[]{:S(2)}, u32[]{:S(2)}) %all-to-all-start.1) | async-done | bytes 1048608 | tf_op jit(solution)/shard_map/all_to_all | solution.py:531
  99.5 5.4 %all-to-all-start = ((bf16[8,512,128]{2,1,0:T(8,128)(2,1)}), bf16[8,512,128]{2,1,0:T(8,128)(2,1)S(1)}, u32[]{:S(2)}, u32[]{:S(2)}) async-start(bf16[8,512,128]{2,1,0:T(8,128)(2,1)} %project_q.1), calls=%async_computation | async-start | bytes 2097152 | tf_op jit(solution)/shard_map/all_to_all | solution.py:531
  107.0 4.0 slice_select_fusion
  116.2 5.4 %convert_reduce_fusion = (f32[2048]{0:T(1024)}, bf16[512,2048]{1,0:T(8,128)(2,1)}) fusion(f32[512,2048]{1,0:T(8,128)S(1)} %get-tuple-element.163, f32[2048]{0:T(1024)S(1)} %bitcast.160, bf16[512,1024]{1,0:T(8,128)(2,1)S(1)} %copy-done.2, bf16[4096,1024]{1,0:T(8,128)(2,1)S(1)} %bitcast.163, s32[]{:T(128)S(6)} %select_n.327), kind=kOutput, calls=%fused_computation.4 | convolution fusion | flops 2161113088 | bytes 11550724 | tf_op jit(solution)/shard_map/dot_general | solution.py:33
  121.6 9.4 %feed_grads.1 = bf16[16,4,64,1024]{3,2,1,0:T(8,128)(2,1)} custom-call(bf16[512,1024]{1,0:T(8,128)(2,1)} %fusion.14.x_ref.y_ref.h_ref, bf16[512,2048]{1,0:T(8,128)(2,1)} %get-tuple-element.71.u_ref, bf16[512,2048]{1,0:T(8,128)(2,1)} %get-tuple-element.70.a_ref, bf16[512,1024]{1,0:T(8,128)(2,1)} %g_ref.3), custom_call_target="tpu_custom_call" | custom-call | tf_op jit(solution)/shard_map/feed_grads/pallas_call | solution.py:115
  132.0 40.8 %attend.1 = (bf16[8,512,128]{2,1,0:T(8,128)(2,1)}, f32[8,512,128]{2,1,0:T(8,128)}, f32[8,512,128]{2,1,0:T(8,128)}) custom-call(s32[9]{0:T(128)} %pad_add_fusion.scal, s32[8,512]{1,0:T(8,128)} %copy-done.33, bf16[8,512,128]{2,1,0:T(8,128)(2,1)} %copy-done.24, bf16[8,512,128]{2,1,0:T(8,128)(2,1)} %all-to-all-done.1.kv_ref, bf16[8,512,128]{2,1,0:T(8,128)(2,1)} %copy-done.37), custom_call_target="tpu_custom_call" | custom-call | flops 999999995904 | bytes 20000000 | tf_op jit(solution)/shard_map/attend/pallas_call | solution.py:232
  172.9 7.7 %collective-permute-start.8 = (f32[8,512,128]{2,1,0:T(8,128)}, f32[8,512,128]{2,1,0:T(8,128)}, u32[]{:S(2)}, u32[]{:S(2)}) collective-permute-start(f32[8,512,128]{2,1,0:T(8,128)} %get-tuple-element.69), channel_id=1, source_target_pairs={{16,18},{18,16},{20,22},{22,20},{24,26},{26,24},{28,30},{30,28},{0... | collective-permute-start | bytes 6291464 | tf_op jit(solution)/shard_map/ppermute | solution.py:586
  180.5 5.3 %all-to-all-start.2 = ((bf16[8,512,128]{2,1,0:T(8,128)(2,1)}), bf16[8,512,128]{2,1,0:T(8,128)(2,1)S(1)}, u32[]{:S(2)}, u32[]{:S(2)}) async-start(bf16[8,512,128]{2,1,0:T(8,128)(2,1)} %get-tuple-element.67), calls=%async_computation.2 | async-start | bytes 2097152 | tf_op jit(solution)/shard_map/all_to_all | solution.py:531
  185.9 6.0 %fusion.1 = f32[512,1024]{1,0:T(8,128)} fusion(bf16[512,2048]{1,0:T(8,128)(2,1)S(1)} %copy-done.17, bf16[4096,1024]{1,0:T(8,128)(2,1)} %param.18, s32[]{:T(128)S(6)} %select_n.327), kind=kOutput, calls=%fused_computation.7 | convolution fusion | flops 2147483648 | bytes 8388612 | tf_op jit(solution)/shard_map/dot_general | solution.py:33
  199.6 21.4 %all-to-all-done.2.x_ref = bf16[8,512,128]{2,1,0:T(8,128)(2,1)S(1)} async-done(((bf16[8,512,128]{2,1,0:T(8,128)(2,1)}), bf16[8,512,128]{2,1,0:T(8,128)(2,1)S(1)}, u32[]{:S(2)}, u32[]{:S(2)}) %all-to-all-start.2) | async-done | bytes 1048608 | tf_op jit(solution)/shard_map/all_to_all | solution.py:531
  222.0 5.4 %query_grads.1 = (bf16[512,512]{1,0:T(8,128)(2,1)}, bf16[512,512]{1,0:T(8,128)(2,1)}, bf16[1024,1024]{1,0:T(8,128)(2,1)}) custom-call(bf16[8,512,128]{2,1,0:T(8,128)(2,1)} %copy-done.11, f32[512,128]{1,0:T(8,128)} %get-tuple-element.161.c_ref, f32[512,128]{1,0:T(8,128)} %get-tuple-element.160.s_ref, bf16[512,1024]{1,0:T(8,128)(2,1)} %fusion.14.x_ref.y_ref.h_ref, ...), custom_call_target="tpu_custom_call" | custom-call | tf_op jit(solution)/shard_map/query_grads/pallas_call | solution.py:309
  229.8 5.1 %all-to-all-start.3 = ((bf16[8,512,128]{2,1,0:T(8,128)(2,1)}), bf16[8,512,128]{2,1,0:T(8,128)(2,1)S(1)}, u32[]{:S(2)}, u32[]{:S(2)}) async-start(bf16[8,512,128]{2,1,0:T(8,128)(2,1)} %join.1), calls=%async_computation.3 | async-start | bytes 2097152 | tf_op jit(solution)/shard_map/all_to_all | solution.py:531
  244.3 14.9 %collective-permute-done.10 = bf16[256,1024]{1,0:T(8,128)(2,1)S(1)} collective-permute-done((bf16[256,1024]{1,0:T(8,128)(2,1)S(1)}, bf16[256,1024]{1,0:T(8,128)(2,1)S(1)}, u32[]{:S(2)}, u32[]{:S(2)}) %collective-permute-start.10) | collective-permute-done | bytes 524320 | tf_op jit(solution)/shard_map/ppermute | solution.py:571
  259.5 10.2 %all-to-all-done.3.x_ref = bf16[8,512,128]{2,1,0:T(8,128)(2,1)S(1)} async-done(((bf16[8,512,128]{2,1,0:T(8,128)(2,1)}), bf16[8,512,128]{2,1,0:T(8,128)(2,1)S(1)}, u32[]{:S(2)}, u32[]{:S(2)}) %all-to-all-start.3) | async-done | bytes 1048608 | tf_op jit(solution)/shard_map/all_to_all | solution.py:531
  273.5 4.9 %key_grads.1 = (bf16[512,1024]{1,0:T(8,128)(2,1)}, bf16[1024,1024]{1,0:T(8,128)(2,1)}) custom-call(bf16[8,512,128]{2,1,0:T(8,128)(2,1)} %copy-done.14, f32[512,128]{1,0:T(8,128)} %get-tuple-element.161.c_ref, f32[512,128]{1,0:T(8,128)} %get-tuple-element.160.s_ref, bf16[512,1024]{1,0:T(8,128)(2,1)} %fusion.14.x_ref.y_ref.h_ref), custom_call_target="tpu_custom_call" | custom-call | tf_op jit(solution)/shard_map/key_grads/pallas_call | solution.py:340
  289.2 19.4 %collective-permute-done.13 = bf16[64,1024]{1,0:T(8,128)(2,1)S(1)} collective-permute-done((bf16[64,1024]{1,0:T(8,128)(2,1)S(1)}, bf16[64,1024]{1,0:T(8,128)(2,1)S(1)}, u32[]{:S(2)}, u32[]{:S(2)}) %collective-permute-start.13) | collective-permute-done | bytes 131104 | tf_op jit(solution)/shard_map/ppermute | solution.py:571
  308.6 4.1 collective-permute-done.14
  313.1 8.2 %collective-permute-done.15 = bf16[128,1024]{1,0:T(8,128)(2,1)S(1)} collective-permute-done((bf16[128,1024]{1,0:T(8,128)(2,1)S(1)}, bf16[128,1024]{1,0:T(8,128)(2,1)S(1)}, u32[]{:S(2)}, u32[]{:S(2)}) %collective-permute-start.15) | collective-permute-done | bytes 262176 | tf_op jit(solution)/shard_map/ppermute | solution.py:571
  322.0 8.0 %collective-permute-done.17 = bf16[64,1024]{1,0:T(8,128)(2,1)S(1)} collective-permute-done((bf16[64,1024]{1,0:T(8,128)(2,1)S(1)}, bf16[64,1024]{1,0:T(8,128)(2,1)S(1)}, u32[]{:S(2)}, u32[]{:S(2)}) %collective-permute-start.17) | collective-permute-done | bytes 131104 | tf_op jit(solution)/shard_map/ppermute | solution.py:571
  332.4 6.7 %collective-permute-done.18 = bf16[2,64,1024]{2,1,0:T(8,128)(2,1)S(1)} collective-permute-done((bf16[2,64,1024]{2,1,0:T(8,128)(2,1)S(1)}, bf16[2,64,1024]{2,1,0:T(8,128)(2,1)S(1)}, u32[]{:S(2)}, u32[]{:S(2)}) %collective-permute-start.18) | collective-permute-done | bytes 262176 | tf_op jit(solution)/shard_map/ppermute | solution.py:653
  347.4 18.8 %collective-permute-done.22 = f32[80,128]{1,0:T(8,128)S(1)} collective-permute-done((f32[80,128]{1,0:T(8,128)S(1)}, f32[80,128]{1,0:T(8,128)S(1)}, u32[]{:S(2)}, u32[]{:S(2)}) %collective-permute-start.22) | collective-permute-done | bytes 40992 | tf_op jit(solution)/shard_map/ppermute | solution.py:664
  370.2 12.4 %collective-permute-done.25 = f32[80,128]{1,0:T(8,128)S(1)} collective-permute-done((f32[80,128]{1,0:T(8,128)S(1)}, f32[80,128]{1,0:T(8,128)S(1)}, u32[]{:S(2)}, u32[]{:S(2)}) %collective-permute-start.25) | collective-permute-done | bytes 40992 | tf_op jit(solution)/shard_map/ppermute | solution.py:664
  396.1 4.7 %bitcast_convert_fusion = f32[2048,1024]{1,0:T(8,128)} fusion(bf16[2,1024,1024]{2,1,0:T(8,128)(2,1)S(1)} %copy-done.10), kind=kLoop, calls=%fused_computation.1 | loop fusion | flops 2097152 | bytes 12582912 | tf_op jit(solution)/shard_map/convert_element_type | solution.py:679
  400.9 7.2 %collective-permute-done.26 = bf16[4,2,64,1024]{3,2,1,0:T(8,128)(2,1)S(1)} collective-permute-done((bf16[4,2,64,1024]{3,2,1,0:T(8,128)(2,1)S(1)}, bf16[4,2,64,1024]{3,2,1,0:T(8,128)(2,1)S(1)}, u32[]{:S(2)}, u32[]{:S(2)}) %collective-permute-start.26) | collective-permute-done | bytes 1048608 | tf_op jit(solution)/shard_map/ppermute | solution.py:575
  411.3 6.2 %collective-permute-done.30 = f32[80,128]{1,0:T(8,128)S(1)} collective-permute-done((f32[80,128]{1,0:T(8,128)S(1)}, f32[80,128]{1,0:T(8,128)S(1)}, u32[]{:S(2)}, u32[]{:S(2)}) %collective-permute-start.30) | collective-permute-done | bytes 40992 | tf_op jit(solution)/shard_map/ppermute | solution.py:684
  418.7 12.4 %place.1 = f32[2,512,4096]{2,1,0:T(8,128)} custom-call(s32[4]{0:T(128)} %pad_add_fusion.1.sel, bf16[8,2,64,1024]{3,2,1,0:T(8,128)(2,1)} %copy-done.1, bf16[8,2,64,1024]{3,2,1,0:T(8,128)(2,1)} %collective-permute-done.31.far_one.far_a.far_b, bf16[8,2,64,1024]{3,2,1,0:T(8,128)(2,1)} %pad_maximum_fusion.1.near_two, ...), custom_call_target="tpu_custom_call" | custom-call | tf_op jit(solution)/shard_map/place/pallas_call | solution.py:424
  (247 shorter events, 110.2 us)
Async XLA Ops:
  7.2 35.9 %collective-permute-start.3 = (f32[1,4096]{1,0:T(1,128)}, f32[1,4096]{1,0:T(1,128)S(1)}, u32[]{:S(2)}, u32[]{:S(2)}) collective-permute-start(f32[1,4096]{1,0:T(1,128)} %param.17), channel_id=1, source_target_pairs={{0,1},{1,0},{2,3},{3,2},{4,5},{5,4},{6,7},{7,6},{8,9},{9,8},{10,11... | collective-permute-start | bytes 49160 | tf_op jit(solution)/shard_map/ppermute | solution.py:497
  13.0 24.8 %collective-permute-start = (bf16[512,1024]{1,0:T(8,128)(2,1)}, bf16[512,1024]{1,0:T(8,128)(2,1)S(1)}, u32[]{:S(2)}, u32[]{:S(2)}) collective-permute-start(bf16[512,1024]{1,0:T(8,128)(2,1)} %pad_maximum_fusion.3), channel_id=1, source_target_pairs={{0,1},{2,3},{4,5},{6,7},{8,9},{10,11},{12,13},{14,15},{16,17},{18,... | collective-permute-start | bytes 3145736 | tf_op jit(solution)/shard_map/ppermute | solution.py:493
  18.3 49.3 %collective-permute-start.5 = (bf16[512,2048]{1,0:T(8,128)(2,1)}, bf16[512,2048]{1,0:T(8,128)(2,1)}, u32[]{:S(2)}, u32[]{:S(2)}) collective-permute-start(bf16[512,2048]{1,0:T(8,128)(2,1)} %dynamic-slice_bitcast_fusion), channel_id=1, source_target_pairs={{1,0},{3,2},{5,4},{7,6},{9,8},{11,10},{13,12},{15,14},{17,16},{19,... | collective-permute-start | bytes 6291464 | tf_op jit(solution)/shard_map/ppermute | solution.py:496
  37.8 27.7 %collective-permute-start.1 = (bf16[512,1024]{1,0:T(8,128)(2,1)}, bf16[512,1024]{1,0:T(8,128)(2,1)}, u32[]{:S(2)}, u32[]{:S(2)}) collective-permute-start(bf16[512,1024]{1,0:T(8,128)(2,1)} %pad_maximum_fusion.2), channel_id=1, source_target_pairs={{0,1},{2,3},{4,5},{6,7},{8,9},{10,11},{12,13},{14,15},{16,17},{18,... | collective-permute-start | bytes 3145736 | tf_op jit(solution)/shard_map/ppermute | solution.py:495
  65.5 9.8 %collective-permute-start.4 = (bf16[512,1024]{1,0:T(8,128)(2,1)}, bf16[512,1024]{1,0:T(8,128)(2,1)S(1)}, u32[]{:S(2)}, u32[]{:S(2)}) collective-permute-start(bf16[512,1024]{1,0:T(8,128)(2,1)} %collective-permute-done.1), channel_id=1, source_target_pairs={{16,18},{18,16},{20,22},{22,20},{24,26},{26,24},{28,30},{30,28},{0... | collective-permute-start | bytes 3145736 | tf_op jit(solution)/shard_map/ppermute | solution.py:488
  67.6 37.5 %collective-permute-start.6 = (bf16[512,2048]{1,0:T(8,128)(2,1)}, bf16[512,2048]{1,0:T(8,128)(2,1)S(1)}, u32[]{:S(2)}, u32[]{:S(2)}) collective-permute-start(bf16[512,2048]{1,0:T(8,128)(2,1)} %collective-permute-done.5), channel_id=1, source_target_pairs={{16,18},{18,16},{20,22},{22,20},{24,26},{26,24},{28,30},{30,28},{0... | collective-permute-start | bytes 6291464 | tf_op jit(solution)/shard_map/ppermute | solution.py:488
  68.4 31.1 %all-to-all-start.1 = ((bf16[8,512,128]{2,1,0:T(8,128)(2,1)}), bf16[8,512,128]{2,1,0:T(8,128)(2,1)}, u32[]{:S(2)}, u32[]{:S(2)}) async-start(bf16[8,512,128]{2,1,0:T(8,128)(2,1)} %project_kv.1), calls=%async_computation.1 | async-start | bytes 2097152 | tf_op jit(solution)/shard_map/all_to_all | solution.py:531
  99.5 31.6 %all-to-all-start = ((bf16[8,512,128]{2,1,0:T(8,128)(2,1)}), bf16[8,512,128]{2,1,0:T(8,128)(2,1)S(1)}, u32[]{:S(2)}, u32[]{:S(2)}) async-start(bf16[8,512,128]{2,1,0:T(8,128)(2,1)} %project_q.1), calls=%async_computation | async-start | bytes 2097152 | tf_op jit(solution)/shard_map/all_to_all | solution.py:531
  104.9 164.8 %reduce-scatter.2.cloned.1.call-start = ((), (), s32[]{:S(2)}) async-start(), calls=%async_computation.5 | async-start | bytes 8912896 | tf_op jit(solution)/shard_map/reduce_scatter | solution.py:563
  172.9 22.8 %collective-permute-start.8 = (f32[8,512,128]{2,1,0:T(8,128)}, f32[8,512,128]{2,1,0:T(8,128)}, u32[]{:S(2)}, u32[]{:S(2)}) collective-permute-start(f32[8,512,128]{2,1,0:T(8,128)} %get-tuple-element.69), channel_id=1, source_target_pairs={{16,18},{18,16},{20,22},{22,20},{24,26},{26,24},{28,30},{30,28},{0... | collective-permute-start | bytes 6291464 | tf_op jit(solution)/shard_map/ppermute | solution.py:586
  180.5 40.5 %all-to-all-start.2 = ((bf16[8,512,128]{2,1,0:T(8,128)(2,1)}), bf16[8,512,128]{2,1,0:T(8,128)(2,1)S(1)}, u32[]{:S(2)}, u32[]{:S(2)}) async-start(bf16[8,512,128]{2,1,0:T(8,128)(2,1)} %get-tuple-element.67), calls=%async_computation.2 | async-start | bytes 2097152 | tf_op jit(solution)/shard_map/all_to_all | solution.py:531
  229.8 8.5 %collective-permute-start.9 = (bf16[512,1024]{1,0:T(8,128)(2,1)}, bf16[512,1024]{1,0:T(8,128)(2,1)}, u32[]{:S(2)}, u32[]{:S(2)}) collective-permute-start(bf16[512,1024]{1,0:T(8,128)(2,1)} %dynamic-slice_bitcast_fusion.2), channel_id=1, source_target_pairs={{0,2},{2,0},{4,6},{6,4},{8,10},{10,8},{12,14},{14,12},{16,18},{18,... | collective-permute-start | bytes 3145736 | tf_op jit(solution)/shard_map/ppermute | solution.py:571
  229.8 39.8 %all-to-all-start.3 = ((bf16[8,512,128]{2,1,0:T(8,128)(2,1)}), bf16[8,512,128]{2,1,0:T(8,128)(2,1)S(1)}, u32[]{:S(2)}, u32[]{:S(2)}) async-start(bf16[8,512,128]{2,1,0:T(8,128)(2,1)} %join.1), calls=%async_computation.3 | async-start | bytes 2097152 | tf_op jit(solution)/shard_map/all_to_all | solution.py:531
  234.9 95.1 %all-gather.2.cloned.1.call-start = ((), (), s32[]{:S(2)}) async-start(), calls=%async_computation.6 | async-start | bytes 4456448 | tf_op jit(solution)/shard_map/all_gather | solution.py:607
  240.6 18.7 %collective-permute-start.10 = (bf16[256,1024]{1,0:T(8,128)(2,1)S(1)}, bf16[256,1024]{1,0:T(8,128)(2,1)S(1)}, u32[]{:S(2)}, u32[]{:S(2)}) collective-permute-start(bf16[256,1024]{1,0:T(8,128)(2,1)S(1)} %dynamic-slice_bitcast_fusion.4), channel_id=1, source_target_pairs={{0,4},{2,6},{4,0},{6,2},{8,12},{10,14},{12,8},{14,10},{16,20},{18,... | collective-permute-start | bytes 1572872 | tf_op jit(solution)/shard_map/ppermute | solution.py:571
  271.9 13.6 %collective-permute-start.11 = (bf16[128,1024]{1,0:T(8,128)(2,1)S(1)}, bf16[128,1024]{1,0:T(8,128)(2,1)}, u32[]{:S(2)}, u32[]{:S(2)}) collective-permute-start(bf16[128,1024]{1,0:T(8,128)(2,1)S(1)} %dynamic-slice_bitcast_fusion.10), channel_id=1, source_target_pairs={{0,8},{2,10},{4,12},{6,14},{8,0},{10,2},{12,4},{14,6},{16,24},{18,... | collective-permute-start | bytes 786440 | tf_op jit(solution)/shard_map/ppermute | solution.py:571
  272.0 49.4 %collective-permute-start.16 = (bf16[512,1024]{1,0:T(8,128)(2,1)}, bf16[512,1024]{1,0:T(8,128)(2,1)}, u32[]{:S(2)}, u32[]{:S(2)}) collective-permute-start(bf16[512,1024]{1,0:T(8,128)(2,1)} %add_convert_fusion), channel_id=1, source_target_pairs={{0,1},{1,0},{2,3},{3,2},{4,5},{5,4},{6,7},{7,6},{8,9},{9,8},{10,11... | collective-permute-start | bytes 3145736 | tf_op jit(solution)/shard_map/ppermute | solution.py:633
  287.0 25.7 %collective-permute-start.14 = (bf16[256,1024]{1,0:T(8,128)(2,1)S(1)}, bf16[256,1024]{1,0:T(8,128)(2,1)S(1)}, u32[]{:S(2)}, u32[]{:S(2)}) collective-permute-start(bf16[256,1024]{1,0:T(8,128)(2,1)S(1)} %dynamic-slice_bitcast_fusion.3), channel_id=1, source_target_pairs={{0,8},{2,10},{4,12},{6,14},{8,0},{10,2},{12,4},{14,6},{16,24},{18,... | collective-permute-start | bytes 1572872 | tf_op jit(solution)/shard_map/ppermute | solution.py:571
  289.1 19.5 %collective-permute-start.13 = (bf16[64,1024]{1,0:T(8,128)(2,1)S(1)}, bf16[64,1024]{1,0:T(8,128)(2,1)S(1)}, u32[]{:S(2)}, u32[]{:S(2)}) collective-permute-start(bf16[64,1024]{1,0:T(8,128)(2,1)S(1)} %dynamic-slice_bitcast_fusion.12), channel_id=1, source_target_pairs={{0,16},{2,18},{4,20},{6,22},{8,24},{10,26},{12,28},{14,30},{16,0},... | collective-permute-start | bytes 393224 | tf_op jit(solution)/shard_map/ppermute | solution.py:571
  313.0 8.3 %collective-permute-start.15 = (bf16[128,1024]{1,0:T(8,128)(2,1)S(1)}, bf16[128,1024]{1,0:T(8,128)(2,1)S(1)}, u32[]{:S(2)}, u32[]{:S(2)}) collective-permute-start(bf16[128,1024]{1,0:T(8,128)(2,1)S(1)} %dynamic-slice_bitcast_fusion.9), channel_id=1, source_target_pairs={{0,4},{2,6},{4,0},{6,2},{8,12},{10,14},{12,8},{14,10},{16,20},{18,... | collective-permute-start | bytes 786440 | tf_op jit(solution)/shard_map/ppermute | solution.py:571
  321.4 8.6 %collective-permute-start.17 = (bf16[64,1024]{1,0:T(8,128)(2,1)S(1)}, bf16[64,1024]{1,0:T(8,128)(2,1)S(1)}, u32[]{:S(2)}, u32[]{:S(2)}) collective-permute-start(bf16[64,1024]{1,0:T(8,128)(2,1)S(1)} %dynamic-slice_bitcast_fusion.11), channel_id=1, source_target_pairs={{0,16},{2,18},{4,20},{6,22},{8,24},{10,26},{12,28},{14,30},{16,0},... | collective-permute-start | bytes 393224 | tf_op jit(solution)/shard_map/ppermute | solution.py:571
  340.2 27.7 %collective-permute-start.19 = (bf16[1,2,64,1024]{3,2,1,0:T(8,128)(2,1)S(1)}, bf16[1,2,64,1024]{3,2,1,0:T(8,128)(2,1)S(1)}, u32[]{:S(2)}, u32[]{:S(2)}) collective-permute-start(bf16[1,2,64,1024]{3,2,1,0:T(8,128)(2,1)S(1)} %maximum_bitcast_fusion), channel_id=1, source_target_pairs={{0,16},{2,18},{4,20},{6,22},{8,24},{10,26},{12,28},{14,30},{16,0},... | collective-permute-start | bytes 786440 | tf_op jit(solution)/shard_map/ppermute | solution.py:575
  340.3 27.7 %collective-permute-start.20 = (bf16[1,2,64,1024]{3,2,1,0:T(8,128)(2,1)S(1)}, bf16[1,2,64,1024]{3,2,1,0:T(8,128)(2,1)S(1)}, u32[]{:S(2)}, u32[]{:S(2)}) collective-permute-start(bf16[1,2,64,1024]{3,2,1,0:T(8,128)(2,1)S(1)} %maximum_bitcast_fusion.1), channel_id=1, source_target_pairs={{0,16},{2,18},{4,20},{6,22},{8,24},{10,26},{12,28},{14,30},{16,0},... | collective-permute-start | bytes 786440 | tf_op jit(solution)/shard_map/ppermute | solution.py:575
  347.3 18.9 %collective-permute-start.22 = (f32[80,128]{1,0:T(8,128)S(1)}, f32[80,128]{1,0:T(8,128)S(1)}, u32[]{:S(2)}, u32[]{:S(2)}) collective-permute-start(f32[80,128]{1,0:T(8,128)S(1)} %add.319), channel_id=1, source_target_pairs={{0,16},{2,18},{4,20},{6,22},{8,24},{10,26},{12,28},{14,30},{16,0},... | collective-permute-start | bytes 122888 | tf_op jit(solution)/shard_map/ppermute | solution.py:664
  366.2 25.1 %collective-permute-start.29 = (bf16[512,1024]{1,0:T(8,128)(2,1)S(1)}, bf16[512,1024]{1,0:T(8,128)(2,1)S(1)}, u32[]{:S(2)}, u32[]{:S(2)}) collective-permute-start(bf16[512,1024]{1,0:T(8,128)(2,1)S(1)} %get-tuple-element.108), channel_id=1, source_target_pairs={{0,1},{1,0},{2,3},{3,2},{4,5},{5,4},{6,7},{7,6},{8,9},{9,8},{10,11... | collective-permute-start | bytes 3145736 | tf_op jit(solution)/shard_map/ppermute | solution.py:659
  368.1 14.6 %collective-permute-start.23 = (bf16[2,2,64,1024]{3,2,1,0:T(8,128)(2,1)S(1)}, bf16[2,2,64,1024]{3,2,1,0:T(8,128)(2,1)S(1)}, u32[]{:S(2)}, u32[]{:S(2)}) collective-permute-start(bf16[2,2,64,1024]{3,2,1,0:T(8,128)(2,1)S(1)} %pad_maximum_fusion.6), channel_id=1, source_target_pairs={{0,8},{2,10},{4,12},{6,14},{8,0},{10,2},{12,4},{14,6},{16,24},{18,... | collective-permute-start | bytes 1572872 | tf_op jit(solution)/shard_map/ppermute | solution.py:575
  368.1 14.6 %collective-permute-start.24 = (bf16[2,2,64,1024]{3,2,1,0:T(8,128)(2,1)S(1)}, bf16[2,2,64,1024]{3,2,1,0:T(8,128)(2,1)S(1)}, u32[]{:S(2)}, u32[]{:S(2)}) collective-permute-start(bf16[2,2,64,1024]{3,2,1,0:T(8,128)(2,1)S(1)} %pad_maximum_fusion.7), channel_id=1, source_target_pairs={{0,4},{2,6},{4,0},{6,2},{8,12},{10,14},{12,8},{14,10},{16,20},{18,... | collective-permute-start | bytes 1572872 | tf_op jit(solution)/shard_map/ppermute | solution.py:575
  368.5 14.1 %collective-permute-start.25 = (f32[80,128]{1,0:T(8,128)S(1)}, f32[80,128]{1,0:T(8,128)S(1)}, u32[]{:S(2)}, u32[]{:S(2)}) collective-permute-start(f32[80,128]{1,0:T(8,128)S(1)} %add.320), channel_id=1, source_target_pairs={{0,4},{2,6},{4,0},{6,2},{8,12},{10,14},{12,8},{14,10},{16,20},{18,... | collective-permute-start | bytes 122888 | tf_op jit(solution)/shard_map/ppermute | solution.py:664
  384.6 23.4 %collective-permute-start.26 = (bf16[4,2,64,1024]{3,2,1,0:T(8,128)(2,1)S(1)}, bf16[4,2,64,1024]{3,2,1,0:T(8,128)(2,1)S(1)}, u32[]{:S(2)}, u32[]{:S(2)}) collective-permute-start(bf16[4,2,64,1024]{3,2,1,0:T(8,128)(2,1)S(1)} %pad_maximum_fusion.4), channel_id=1, source_target_pairs={{0,4},{2,6},{4,0},{6,2},{8,12},{10,14},{12,8},{14,10},{16,20},{18,... | collective-permute-start | bytes 3145736 | tf_op jit(solution)/shard_map/ppermute | solution.py:575
  384.9 23.5 %collective-permute-start.27 = (bf16[4,2,64,1024]{3,2,1,0:T(8,128)(2,1)S(1)}, bf16[4,2,64,1024]{3,2,1,0:T(8,128)(2,1)S(1)}, u32[]{:S(2)}, u32[]{:S(2)}) collective-permute-start(bf16[4,2,64,1024]{3,2,1,0:T(8,128)(2,1)S(1)} %pad_maximum_fusion.5), channel_id=1, source_target_pairs={{0,8},{2,10},{4,12},{6,14},{8,0},{10,2},{12,4},{14,6},{16,24},{18,... | collective-permute-start | bytes 3145736 | tf_op jit(solution)/shard_map/ppermute | solution.py:575
  410.2 8.6 %collective-permute-start.31 = (bf16[8,2,64,1024]{3,2,1,0:T(8,128)(2,1)S(1)}, bf16[8,2,64,1024]{3,2,1,0:T(8,128)(2,1)}, u32[]{:S(2)}, u32[]{:S(2)}) collective-permute-start(bf16[8,2,64,1024]{3,2,1,0:T(8,128)(2,1)S(1)} %pad_maximum_fusion.near_one.near_a.near_b), channel_id=1, source_target_pairs={{0,2},{2,0},{4,6},{6,4},{8,10},{10,8},{12,14},{14,12},{16,18},{18,... | collective-permute-start | bytes 6291464 | tf_op jit(solution)/shard_map/ppermute | solution.py:685
  410.2 8.5 %collective-permute-start.32 = (bf16[8,2,64,1024]{3,2,1,0:T(8,128)(2,1)}, bf16[8,2,64,1024]{3,2,1,0:T(8,128)(2,1)}, u32[]{:S(2)}, u32[]{:S(2)}) collective-permute-start(bf16[8,2,64,1024]{3,2,1,0:T(8,128)(2,1)} %pad_maximum_fusion.1.near_two), channel_id=1, source_target_pairs={{0,2},{2,0},{4,6},{6,4},{8,10},{10,8},{12,14},{14,12},{16,18},{18,... | collective-permute-start | bytes 6291464 | tf_op jit(solution)/shard_map/ppermute | solution.py:683
  (48 other events, 318.2 us)
Sparse Core Ops, SparseCore 0:
  131.2 124.6 reduce-scatter.1
  271.6 53.2 all-gather.1

commit v4 on v3

--- a/solution.py
+++ b/solution.py
@@ -531,6 +531,9 @@
         return lax.all_to_all(blocks, "seq", 0, 0, axis_index_groups=groups)
 
     kv_own = spread(kv_heads)
+    w_down = lax.dynamic_slice(w_second, (branch * half_ff, 0), (half_ff, D))
+    d_active = mm(cotangent, w_down, ((1,), (1,)))
+    kv_own, d_active = lax.optimization_barrier((kv_own, d_active))
     kv_other = lax.ppermute(kv_own, "seq", core_swap)
     qd_heads = project(
         hidden, cotangent, w_q, w_out, b_q, jnp.zeros_like(b_q), cos_q, sine_q, True
@@ -549,13 +552,11 @@
     w_up = jnp.where(on_first, jnp.concatenate([up_low, up_high], axis=0), weights[:, half_ff:])
     w_up = after(w_up, kv_other, qd_heads)
     b_up = jnp.where(on_first, b_other[0, :half_ff], b_first[0, half_ff:])
-    w_down = lax.dynamic_slice(w_second, (branch * half_ff, 0), (half_ff, D))
     root_half = 0.7071067811865476
     up_proj = mm(hidden, w_up, ((1,), (0,))) + b_up
     cdf = 0.5 * (1.0 + lax.erf(up_proj * root_half))
     active = (up_proj * cdf).astype(bf16)
     slope = cdf + up_proj * jnp.exp(up_proj * up_proj * -0.5) * 0.3989422804014327
-    d_active = mm(cotangent, w_down, ((1,), (1,)))
     d_up = (d_active * slope).astype(bf16)
     orders = [[in_path(i, path) for i in range(count)] for path in (path_one, path_two)]
     g_feed = feed_grads(hidden, d_up, active, cotangent, orders)

time: 444 us -> 450 us (1.014)
  starting transfers between devices: 61.1 us -> 70.6 us
  waiting for transfers between devices: 183 us -> 175 us
    reduce_scatter x1, starting transfers between devices: 0.17 us -> 10.4 us  [body(): lax.psum_scatter(g_feed, 'seq', scatter_dimension=0, tiled=True)[0]]
    ppermute x1, waiting for transfers between devices: 11.4 us -> 4.56 us  [body(): kv_crossed = lax.ppermute(kv_sent, ('seq', 'pair'), to_second)]
where the time goes in v4:
time: 450 us; the launch traced here: 445 us
  waiting for transfers between devices  175 us (39%)
  Pallas kernels  89.7 us (20%)
  starting transfers between devices  70.6 us (16%)
  other arithmetic  46.4 us (10%)
  matrix products  27.6 us (6%)
  local copies, waits for them, and re-layouts  19.5 us (4%)
  between operations  16 us (4%)
    ppermute x8, waiting for transfers between devices, scatter_step(): got = lax.ppermute(send, 'seq', seq_swap(1 << b))  54.7 us
    pallas_call x1, Pallas kernels, attend(): pl.pallas_call(attend_kernel, in_specs=[pl.BlockSpec(memory_space=pltpu.S...  43.2 us
    all_to_all x4, waiting for transfers between devices, spread(): return lax.all_to_all(blocks, 'seq', 0, 0, axis_index_groups=groups)  42.8 us
    ppermute x3, waiting for transfers between devices, body(): small = small + lax.ppermute(small, 'seq', seq_swap(1 << path_two[i]))  32.9 us
    dot_general x7, matrix products, mm(): lax.dot_general(left, right, (dims, ((), ())), preferred_element_type=f32)  27.6 us
    all_to_all x4, starting transfers between devices, spread(): return lax.all_to_all(blocks, 'seq', 0, 0, axis_index_groups=groups)  22.5 us
    pallas_call x1, Pallas kernels, place_slot(): pl.pallas_call(place_kernel, grid_spec=pltpu.PrefetchScalarGridSpec(num_s...  12.4 us
    ppermute x1, waiting for transfers between devices, body(): qo_crossed = lax.ppermute(qo_sent, ('seq', 'pair'), to_second)  12.3 us
  transfers between devices with their start and end apart: 39, of which 20 were waited for; matrix products, arithmetic and copies ran while one was open for 19% of the time, Pallas kernels for 17%

profile of v4, /device:TPU:0, one launch (start us, length us, event | category | flops | bytes accessed | tf_op | source)
XLA Modules:
  0.0 445.1 jit_solution(16868178568316037900)
XLA Ops:
  26.6 6.6 %fusion.4 = f32[512,2048]{1,0:T(8,128)} fusion(bf16[512,1024]{1,0:T(8,128)(2,1)S(1)} %copy-done.2, bf16[4096,1024]{1,0:T(8,128)(2,1)} %param.18, s32[]{:T(128)S(6)} %select_n.327), kind=kOutput, calls=%fused_computation.10 | convolution fusion | flops 2147483648 | bytes 9437188 | tf_op jit(solution)/shard_map/dot_general | solution.py:33
  33.2 4.6 %collective-permute-done = bf16[512,1024]{1,0:T(8,128)(2,1)S(1)} collective-permute-done((bf16[512,1024]{1,0:T(8,128)(2,1)}, bf16[512,1024]{1,0:T(8,128)(2,1)S(1)}, u32[]{:S(2)}, u32[]{:S(2)}) %collective-permute-start) | collective-permute-done | bytes 1048608 | tf_op jit(solution)/shard_map/ppermute | solution.py:493
  37.8 5.3 %collective-permute-start.1 = (bf16[512,1024]{1,0:T(8,128)(2,1)}, bf16[512,1024]{1,0:T(8,128)(2,1)}, u32[]{:S(2)}, u32[]{:S(2)}) collective-permute-start(bf16[512,1024]{1,0:T(8,128)(2,1)} %pad_maximum_fusion.2), channel_id=1, source_target_pairs={{0,1},{2,3},{4,5},{6,7},{8,9},{10,11},{12,13},{14,15},{16,17},{18,... | collective-permute-start | bytes 3145736 | tf_op jit(solution)/shard_map/ppermute | solution.py:495
  47.9 5.3 %project_kv.1 = bf16[8,512,128]{2,1,0:T(8,128)(2,1)} custom-call(bf16[512,1024]{1,0:T(8,128)(2,1)} %fusion.14.x_ref.y_ref.h_ref, bf16[512,1024]{1,0:T(8,128)(2,1)} %fusion.14.x_ref.y_ref.h_ref, bf16[1024,512]{1,0:T(8,128)(2,1)} %get-tuple-element.141.wx, bf16[1024,512]{1,0:T(8,128)(2,1)} %get-tuple-element.140.wy, f32[1,512]{1,0:T(1,128)} %get-tuple-element.162.bx, ...), custom_call_target="tpu_custom_call" | custom-call | tf_op jit(solution)/shard_map/project_kv/pallas_call | solution.py:77
  53.2 12.3 %collective-permute-done.1 = bf16[512,1024]{1,0:T(8,128)(2,1)} collective-permute-done((bf16[512,1024]{1,0:T(8,128)(2,1)}, bf16[512,1024]{1,0:T(8,128)(2,1)}, u32[]{:S(2)}, u32[]{:S(2)}) %collective-permute-start.1) | collective-permute-done | bytes 1048608 | tf_op jit(solution)/shard_map/ppermute | solution.py:495
  68.4 6.9 %all-to-all-start.1 = ((bf16[8,512,128]{2,1,0:T(8,128)(2,1)}), bf16[8,512,128]{2,1,0:T(8,128)(2,1)}, u32[]{:S(2)}, u32[]{:S(2)}) async-start(bf16[8,512,128]{2,1,0:T(8,128)(2,1)} %project_kv.1), calls=%async_computation.1 | async-start | bytes 2097152 | tf_op jit(solution)/shard_map/all_to_all | solution.py:531
  82.5 5.2 %project_q.1 = bf16[8,512,128]{2,1,0:T(8,128)(2,1)} custom-call(bf16[512,1024]{1,0:T(8,128)(2,1)} %fusion.14.x_ref.y_ref.h_ref, bf16[512,1024]{1,0:T(8,128)(2,1)} %g_ref.3, bf16[1024,512]{1,0:T(8,128)(2,1)} %slice_select_fusion.2.wx, bf16[512,1024]{1,0:T(8,128)(2,1)} %slice_select_fusion.1.wy, f32[1,512]{1,0:T(1,128)} %get-tuple-element.160.bx, ...), custom_call_target="tpu_custom_call" | custom-call | tf_op jit(solution)/shard_map/project_q/pallas_call | solution.py:77
  87.7 11.9 %all-to-all-done.1.kv_ref = bf16[8,512,128]{2,1,0:T(8,128)(2,1)} async-done(((bf16[8,512,128]{2,1,0:T(8,128)(2,1)}), bf16[8,512,128]{2,1,0:T(8,128)(2,1)}, u32[]{:S(2)}, u32[]{:S(2)}) %all-to-all-start.1) | async-done | bytes 1048608 | tf_op jit(solution)/shard_map/all_to_all | solution.py:531
  99.6 5.4 %all-to-all-start = ((bf16[8,512,128]{2,1,0:T(8,128)(2,1)}), bf16[8,512,128]{2,1,0:T(8,128)(2,1)S(1)}, u32[]{:S(2)}, u32[]{:S(2)}) async-start(bf16[8,512,128]{2,1,0:T(8,128)(2,1)} %project_q.1), calls=%async_computation | async-start | bytes 2097152 | tf_op jit(solution)/shard_map/all_to_all | solution.py:531
  104.9 10.4 %reduce-scatter.2.cloned.1.call-start = ((), (), s32[]{:S(2)}) async-start(), calls=%async_computation.5 | async-start | bytes 8912896 | tf_op jit(solution)/shard_map/reduce_scatter | solution.py:564
  121.4 6.3 %convert_reduce_fusion = (f32[2048]{0:T(1024)}, bf16[512,2048]{1,0:T(8,128)(2,1)}, bf16[512,2048]{1,0:T(8,128)(2,1)}) fusion(f32[512,2048]{1,0:T(8,128)S(1)} %copy-done.39, f32[2048]{0:T(1024)S(1)} %bitcast.157, bf16[512,1024]{1,0:T(8,128)(2,1)S(1)} %copy-done, bf16[1024,2048]{1,0:T(8,128)(2,1)S(1)} %slice_select_fusion), kind=kOutput, calls=%fused_computation.2 | convolution fusion | flops 2163210240 | bytes 13647872 | tf_op jit(solution)/shard_map/dot_general | solution.py:33
  127.7 9.5 %feed_grads.1 = bf16[16,4,64,1024]{3,2,1,0:T(8,128)(2,1)} custom-call(bf16[512,1024]{1,0:T(8,128)(2,1)} %fusion.14.x_ref.y_ref.h_ref, bf16[512,2048]{1,0:T(8,128)(2,1)} %get-tuple-element.75.u_ref, bf16[512,2048]{1,0:T(8,128)(2,1)} %get-tuple-element.74.a_ref, bf16[512,1024]{1,0:T(8,128)(2,1)} %g_ref.3), custom_call_target="tpu_custom_call" | custom-call | tf_op jit(solution)/shard_map/feed_grads/pallas_call | solution.py:115
  138.2 43.2 %attend.1 = (bf16[8,512,128]{2,1,0:T(8,128)(2,1)}, f32[8,512,128]{2,1,0:T(8,128)}, f32[8,512,128]{2,1,0:T(8,128)}) custom-call(s32[9]{0:T(128)} %pad_add_fusion.scal, s32[8,512]{1,0:T(8,128)} %copy-done.33, bf16[8,512,128]{2,1,0:T(8,128)(2,1)} %copy-done.24, bf16[8,512,128]{2,1,0:T(8,128)(2,1)} %all-to-all-done.1.kv_ref, bf16[8,512,128]{2,1,0:T(8,128)(2,1)} %copy-done.37), custom_call_target="tpu_custom_call" | custom-call | flops 999999995904 | bytes 20000000 | tf_op jit(solution)/shard_map/attend/pallas_call | solution.py:232
  181.3 6.5 %collective-permute-start.8 = (f32[8,512,128]{2,1,0:T(8,128)}, f32[8,512,128]{2,1,0:T(8,128)}, u32[]{:S(2)}, u32[]{:S(2)}) collective-permute-start(f32[8,512,128]{2,1,0:T(8,128)} %get-tuple-element.73), channel_id=1, source_target_pairs={{16,18},{18,16},{20,22},{22,20},{24,26},{26,24},{28,30},{30,28},{0... | collective-permute-start | bytes 6291464 | tf_op jit(solution)/shard_map/ppermute | solution.py:587
  187.8 5.1 %all-to-all-start.2 = ((bf16[8,512,128]{2,1,0:T(8,128)(2,1)}), bf16[8,512,128]{2,1,0:T(8,128)(2,1)S(1)}, u32[]{:S(2)}, u32[]{:S(2)}) async-start(bf16[8,512,128]{2,1,0:T(8,128)(2,1)} %get-tuple-element.71), calls=%async_computation.2 | async-start | bytes 2097152 | tf_op jit(solution)/shard_map/all_to_all | solution.py:531
  192.9 6.0 %fusion = f32[512,1024]{1,0:T(8,128)} fusion(bf16[512,2048]{1,0:T(8,128)(2,1)S(1)} %copy-done.17, bf16[4096,1024]{1,0:T(8,128)(2,1)} %param.18, s32[]{:T(128)S(6)} %select_n.327), kind=kOutput, calls=%fused_computation.6 | convolution fusion | flops 2147483648 | bytes 8388612 | tf_op jit(solution)/shard_map/dot_general | solution.py:33
  206.6 20.4 %all-to-all-done.2.x_ref = bf16[8,512,128]{2,1,0:T(8,128)(2,1)S(1)} async-done(((bf16[8,512,128]{2,1,0:T(8,128)(2,1)}), bf16[8,512,128]{2,1,0:T(8,128)(2,1)S(1)}, u32[]{:S(2)}, u32[]{:S(2)}) %all-to-all-start.2) | async-done | bytes 1048608 | tf_op jit(solution)/shard_map/all_to_all | solution.py:531
  228.1 5.4 %query_grads.1 = (bf16[512,512]{1,0:T(8,128)(2,1)}, bf16[512,512]{1,0:T(8,128)(2,1)}, bf16[1024,1024]{1,0:T(8,128)(2,1)}) custom-call(bf16[8,512,128]{2,1,0:T(8,128)(2,1)} %copy-done.11, f32[512,128]{1,0:T(8,128)} %get-tuple-element.168.c_ref, f32[512,128]{1,0:T(8,128)} %get-tuple-element.167.s_ref, bf16[512,1024]{1,0:T(8,128)(2,1)} %fusion.14.x_ref.y_ref.h_ref, ...), custom_call_target="tpu_custom_call" | custom-call | tf_op jit(solution)/shard_map/query_grads/pallas_call | solution.py:309
  236.1 5.2 %all-to-all-start.3 = ((bf16[8,512,128]{2,1,0:T(8,128)(2,1)}), bf16[8,512,128]{2,1,0:T(8,128)(2,1)S(1)}, u32[]{:S(2)}, u32[]{:S(2)}) async-start(bf16[8,512,128]{2,1,0:T(8,128)(2,1)} %join.1), calls=%async_computation.3 | async-start | bytes 2097152 | tf_op jit(solution)/shard_map/all_to_all | solution.py:531
  250.6 14.9 %collective-permute-done.10 = bf16[256,1024]{1,0:T(8,128)(2,1)S(1)} collective-permute-done((bf16[256,1024]{1,0:T(8,128)(2,1)S(1)}, bf16[256,1024]{1,0:T(8,128)(2,1)S(1)}, u32[]{:S(2)}, u32[]{:S(2)}) %collective-permute-start.10) | collective-permute-done | bytes 524320 | tf_op jit(solution)/shard_map/ppermute | solution.py:572
  265.7 10.5 %all-to-all-done.3.x_ref = bf16[8,512,128]{2,1,0:T(8,128)(2,1)S(1)} async-done(((bf16[8,512,128]{2,1,0:T(8,128)(2,1)}), bf16[8,512,128]{2,1,0:T(8,128)(2,1)S(1)}, u32[]{:S(2)}, u32[]{:S(2)}) %all-to-all-start.3) | async-done | bytes 1048608 | tf_op jit(solution)/shard_map/all_to_all | solution.py:531
  280.1 4.9 %key_grads.1 = (bf16[512,1024]{1,0:T(8,128)(2,1)}, bf16[1024,1024]{1,0:T(8,128)(2,1)}) custom-call(bf16[8,512,128]{2,1,0:T(8,128)(2,1)} %copy-done.14, f32[512,128]{1,0:T(8,128)} %get-tuple-element.168.c_ref, f32[512,128]{1,0:T(8,128)} %get-tuple-element.167.s_ref, bf16[512,1024]{1,0:T(8,128)(2,1)} %fusion.14.x_ref.y_ref.h_ref), custom_call_target="tpu_custom_call" | custom-call | tf_op jit(solution)/shard_map/key_grads/pallas_call | solution.py:340
  295.8 19.4 %collective-permute-done.13 = bf16[64,1024]{1,0:T(8,128)(2,1)S(1)} collective-permute-done((bf16[64,1024]{1,0:T(8,128)(2,1)S(1)}, bf16[64,1024]{1,0:T(8,128)(2,1)S(1)}, u32[]{:S(2)}, u32[]{:S(2)}) %collective-permute-start.13) | collective-permute-done | bytes 131104 | tf_op jit(solution)/shard_map/ppermute | solution.py:572
  319.6 8.2 %collective-permute-done.15 = bf16[128,1024]{1,0:T(8,128)(2,1)S(1)} collective-permute-done((bf16[128,1024]{1,0:T(8,128)(2,1)S(1)}, bf16[128,1024]{1,0:T(8,128)(2,1)S(1)}, u32[]{:S(2)}, u32[]{:S(2)}) %collective-permute-start.15) | collective-permute-done | bytes 262176 | tf_op jit(solution)/shard_map/ppermute | solution.py:572
  328.5 8.1 %collective-permute-done.17 = bf16[64,1024]{1,0:T(8,128)(2,1)S(1)} collective-permute-done((bf16[64,1024]{1,0:T(8,128)(2,1)S(1)}, bf16[64,1024]{1,0:T(8,128)(2,1)S(1)}, u32[]{:S(2)}, u32[]{:S(2)}) %collective-permute-start.17) | collective-permute-done | bytes 131104 | tf_op jit(solution)/shard_map/ppermute | solution.py:572
  339.0 6.7 %collective-permute-done.18 = bf16[2,64,1024]{2,1,0:T(8,128)(2,1)S(1)} collective-permute-done((bf16[2,64,1024]{2,1,0:T(8,128)(2,1)S(1)}, bf16[2,64,1024]{2,1,0:T(8,128)(2,1)S(1)}, u32[]{:S(2)}, u32[]{:S(2)}) %collective-permute-start.18) | collective-permute-done | bytes 262176 | tf_op jit(solution)/shard_map/ppermute | solution.py:654
  354.0 18.7 %collective-permute-done.22 = f32[80,128]{1,0:T(8,128)S(1)} collective-permute-done((f32[80,128]{1,0:T(8,128)S(1)}, f32[80,128]{1,0:T(8,128)S(1)}, u32[]{:S(2)}, u32[]{:S(2)}) %collective-permute-start.22) | collective-permute-done | bytes 40992 | tf_op jit(solution)/shard_map/ppermute | solution.py:665
  376.8 12.4 %collective-permute-done.25 = f32[80,128]{1,0:T(8,128)S(1)} collective-permute-done((f32[80,128]{1,0:T(8,128)S(1)}, f32[80,128]{1,0:T(8,128)S(1)}, u32[]{:S(2)}, u32[]{:S(2)}) %collective-permute-start.25) | collective-permute-done | bytes 40992 | tf_op jit(solution)/shard_map/ppermute | solution.py:665
  402.7 4.7 %bitcast_convert_fusion = f32[2048,1024]{1,0:T(8,128)} fusion(bf16[2,1024,1024]{2,1,0:T(8,128)(2,1)S(1)} %copy-done.10), kind=kLoop, calls=%fused_computation.1 | loop fusion | flops 2097152 | bytes 12582912 | tf_op jit(solution)/shard_map/convert_element_type | solution.py:680
  407.4 7.2 %collective-permute-done.26 = bf16[4,2,64,1024]{3,2,1,0:T(8,128)(2,1)S(1)} collective-permute-done((bf16[4,2,64,1024]{3,2,1,0:T(8,128)(2,1)S(1)}, bf16[4,2,64,1024]{3,2,1,0:T(8,128)(2,1)S(1)}, u32[]{:S(2)}, u32[]{:S(2)}) %collective-permute-start.26) | collective-permute-done | bytes 1048608 | tf_op jit(solution)/shard_map/ppermute | solution.py:576
  418.0 6.2 %collective-permute-done.30 = f32[80,128]{1,0:T(8,128)S(1)} collective-permute-done((f32[80,128]{1,0:T(8,128)S(1)}, f32[80,128]{1,0:T(8,128)S(1)}, u32[]{:S(2)}, u32[]{:S(2)}) %collective-permute-start.30) | collective-permute-done | bytes 40992 | tf_op jit(solution)/shard_map/ppermute | solution.py:685
  425.5 12.4 %place.1 = f32[2,512,4096]{2,1,0:T(8,128)} custom-call(s32[4]{0:T(128)} %pad_add_fusion.1.sel, bf16[8,2,64,1024]{3,2,1,0:T(8,128)(2,1)} %copy-done.1, bf16[8,2,64,1024]{3,2,1,0:T(8,128)(2,1)} %collective-permute-done.31.far_one.far_a.far_b, bf16[8,2,64,1024]{3,2,1,0:T(8,128)(2,1)} %pad_maximum_fusion.1.near_two, ...), custom_call_target="tpu_custom_call" | custom-call | tf_op jit(solution)/shard_map/place/pallas_call | solution.py:424
  (244 shorter events, 113.7 us)
Async XLA Ops:
  7.2 35.9 %collective-permute-start.3 = (f32[1,4096]{1,0:T(1,128)}, f32[1,4096]{1,0:T(1,128)S(1)}, u32[]{:S(2)}, u32[]{:S(2)}) collective-permute-start(f32[1,4096]{1,0:T(1,128)} %param.17), channel_id=1, source_target_pairs={{0,1},{1,0},{2,3},{3,2},{4,5},{5,4},{6,7},{7,6},{8,9},{9,8},{10,11... | collective-permute-start | bytes 49160 | tf_op jit(solution)/shard_map/ppermute | solution.py:497
  13.0 24.8 %collective-permute-start = (bf16[512,1024]{1,0:T(8,128)(2,1)}, bf16[512,1024]{1,0:T(8,128)(2,1)S(1)}, u32[]{:S(2)}, u32[]{:S(2)}) collective-permute-start(bf16[512,1024]{1,0:T(8,128)(2,1)} %pad_maximum_fusion.3), channel_id=1, source_target_pairs={{0,1},{2,3},{4,5},{6,7},{8,9},{10,11},{12,13},{14,15},{16,17},{18,... | collective-permute-start | bytes 3145736 | tf_op jit(solution)/shard_map/ppermute | solution.py:493
  18.3 49.3 %collective-permute-start.5 = (bf16[512,2048]{1,0:T(8,128)(2,1)}, bf16[512,2048]{1,0:T(8,128)(2,1)}, u32[]{:S(2)}, u32[]{:S(2)}) collective-permute-start(bf16[512,2048]{1,0:T(8,128)(2,1)} %dynamic-slice_bitcast_fusion), channel_id=1, source_target_pairs={{1,0},{3,2},{5,4},{7,6},{9,8},{11,10},{13,12},{15,14},{17,16},{19,... | collective-permute-start | bytes 6291464 | tf_op jit(solution)/shard_map/ppermute | solution.py:496
  37.8 27.7 %collective-permute-start.1 = (bf16[512,1024]{1,0:T(8,128)(2,1)}, bf16[512,1024]{1,0:T(8,128)(2,1)}, u32[]{:S(2)}, u32[]{:S(2)}) collective-permute-start(bf16[512,1024]{1,0:T(8,128)(2,1)} %pad_maximum_fusion.2), channel_id=1, source_target_pairs={{0,1},{2,3},{4,5},{6,7},{8,9},{10,11},{12,13},{14,15},{16,17},{18,... | collective-permute-start | bytes 3145736 | tf_op jit(solution)/shard_map/ppermute | solution.py:495
  65.5 9.9 %collective-permute-start.4 = (bf16[512,1024]{1,0:T(8,128)(2,1)}, bf16[512,1024]{1,0:T(8,128)(2,1)S(1)}, u32[]{:S(2)}, u32[]{:S(2)}) collective-permute-start(bf16[512,1024]{1,0:T(8,128)(2,1)} %collective-permute-done.1), channel_id=1, source_target_pairs={{16,18},{18,16},{20,22},{22,20},{24,26},{26,24},{28,30},{30,28},{0... | collective-permute-start | bytes 3145736 | tf_op jit(solution)/shard_map/ppermute | solution.py:488
  67.6 47.8 %collective-permute-start.6 = (bf16[512,2048]{1,0:T(8,128)(2,1)}, bf16[512,2048]{1,0:T(8,128)(2,1)S(1)}, u32[]{:S(2)}, u32[]{:S(2)}) collective-permute-start(bf16[512,2048]{1,0:T(8,128)(2,1)} %collective-permute-done.5), channel_id=1, source_target_pairs={{16,18},{18,16},{20,22},{22,20},{24,26},{26,24},{28,30},{30,28},{0... | collective-permute-start | bytes 6291464 | tf_op jit(solution)/shard_map/ppermute | solution.py:488
  68.4 31.1 %all-to-all-start.1 = ((bf16[8,512,128]{2,1,0:T(8,128)(2,1)}), bf16[8,512,128]{2,1,0:T(8,128)(2,1)}, u32[]{:S(2)}, u32[]{:S(2)}) async-start(bf16[8,512,128]{2,1,0:T(8,128)(2,1)} %project_kv.1), calls=%async_computation.1 | async-start | bytes 2097152 | tf_op jit(solution)/shard_map/all_to_all | solution.py:531
  99.6 37.6 %all-to-all-start = ((bf16[8,512,128]{2,1,0:T(8,128)(2,1)}), bf16[8,512,128]{2,1,0:T(8,128)(2,1)S(1)}, u32[]{:S(2)}, u32[]{:S(2)}) async-start(bf16[8,512,128]{2,1,0:T(8,128)(2,1)} %project_q.1), calls=%async_computation | async-start | bytes 2097152 | tf_op jit(solution)/shard_map/all_to_all | solution.py:531
  104.9 171.3 %reduce-scatter.2.cloned.1.call-start = ((), (), s32[]{:S(2)}) async-start(), calls=%async_computation.5 | async-start | bytes 8912896 | tf_op jit(solution)/shard_map/reduce_scatter | solution.py:564
  181.3 21.3 %collective-permute-start.8 = (f32[8,512,128]{2,1,0:T(8,128)}, f32[8,512,128]{2,1,0:T(8,128)}, u32[]{:S(2)}, u32[]{:S(2)}) collective-permute-start(f32[8,512,128]{2,1,0:T(8,128)} %get-tuple-element.73), channel_id=1, source_target_pairs={{16,18},{18,16},{20,22},{22,20},{24,26},{26,24},{28,30},{30,28},{0... | collective-permute-start | bytes 6291464 | tf_op jit(solution)/shard_map/ppermute | solution.py:587
  187.8 39.3 %all-to-all-start.2 = ((bf16[8,512,128]{2,1,0:T(8,128)(2,1)}), bf16[8,512,128]{2,1,0:T(8,128)(2,1)S(1)}, u32[]{:S(2)}, u32[]{:S(2)}) async-start(bf16[8,512,128]{2,1,0:T(8,128)(2,1)} %get-tuple-element.71), calls=%async_computation.2 | async-start | bytes 2097152 | tf_op jit(solution)/shard_map/all_to_all | solution.py:531
  235.9 8.8 %collective-permute-start.9 = (bf16[512,1024]{1,0:T(8,128)(2,1)}, bf16[512,1024]{1,0:T(8,128)(2,1)}, u32[]{:S(2)}, u32[]{:S(2)}) collective-permute-start(bf16[512,1024]{1,0:T(8,128)(2,1)} %dynamic-slice_bitcast_fusion.2), channel_id=1, source_target_pairs={{0,2},{2,0},{4,6},{6,4},{8,10},{10,8},{12,14},{14,12},{16,18},{18,... | collective-permute-start | bytes 3145736 | tf_op jit(solution)/shard_map/ppermute | solution.py:572
  236.1 40.1 %all-to-all-start.3 = ((bf16[8,512,128]{2,1,0:T(8,128)(2,1)}), bf16[8,512,128]{2,1,0:T(8,128)(2,1)S(1)}, u32[]{:S(2)}, u32[]{:S(2)}) async-start(bf16[8,512,128]{2,1,0:T(8,128)(2,1)} %join.1), calls=%async_computation.3 | async-start | bytes 2097152 | tf_op jit(solution)/shard_map/all_to_all | solution.py:531
  241.3 95.4 %all-gather.2.cloned.1.call-start = ((), (), s32[]{:S(2)}) async-start(), calls=%async_computation.6 | async-start | bytes 4456448 | tf_op jit(solution)/shard_map/all_gather | solution.py:608
  246.9 18.6 %collective-permute-start.10 = (bf16[256,1024]{1,0:T(8,128)(2,1)S(1)}, bf16[256,1024]{1,0:T(8,128)(2,1)S(1)}, u32[]{:S(2)}, u32[]{:S(2)}) collective-permute-start(bf16[256,1024]{1,0:T(8,128)(2,1)S(1)} %dynamic-slice_bitcast_fusion.4), channel_id=1, source_target_pairs={{0,4},{2,6},{4,0},{6,2},{8,12},{10,14},{12,8},{14,10},{16,20},{18,... | collective-permute-start | bytes 1572872 | tf_op jit(solution)/shard_map/ppermute | solution.py:572
  278.5 13.6 %collective-permute-start.11 = (bf16[128,1024]{1,0:T(8,128)(2,1)S(1)}, bf16[128,1024]{1,0:T(8,128)(2,1)}, u32[]{:S(2)}, u32[]{:S(2)}) collective-permute-start(bf16[128,1024]{1,0:T(8,128)(2,1)S(1)} %dynamic-slice_bitcast_fusion.10), channel_id=1, source_target_pairs={{0,8},{2,10},{4,12},{6,14},{8,0},{10,2},{12,4},{14,6},{16,24},{18,... | collective-permute-start | bytes 786440 | tf_op jit(solution)/shard_map/ppermute | solution.py:572
  278.5 49.4 %collective-permute-start.16 = (bf16[512,1024]{1,0:T(8,128)(2,1)}, bf16[512,1024]{1,0:T(8,128)(2,1)}, u32[]{:S(2)}, u32[]{:S(2)}) collective-permute-start(bf16[512,1024]{1,0:T(8,128)(2,1)} %add_convert_fusion), channel_id=1, source_target_pairs={{0,1},{1,0},{2,3},{3,2},{4,5},{5,4},{6,7},{7,6},{8,9},{9,8},{10,11... | collective-permute-start | bytes 3145736 | tf_op jit(solution)/shard_map/ppermute | solution.py:634
  293.6 25.7 %collective-permute-start.14 = (bf16[256,1024]{1,0:T(8,128)(2,1)S(1)}, bf16[256,1024]{1,0:T(8,128)(2,1)S(1)}, u32[]{:S(2)}, u32[]{:S(2)}) collective-permute-start(bf16[256,1024]{1,0:T(8,128)(2,1)S(1)} %dynamic-slice_bitcast_fusion.3), channel_id=1, source_target_pairs={{0,8},{2,10},{4,12},{6,14},{8,0},{10,2},{12,4},{14,6},{16,24},{18,... | collective-permute-start | bytes 1572872 | tf_op jit(solution)/shard_map/ppermute | solution.py:572
  295.7 19.5 %collective-permute-start.13 = (bf16[64,1024]{1,0:T(8,128)(2,1)S(1)}, bf16[64,1024]{1,0:T(8,128)(2,1)S(1)}, u32[]{:S(2)}, u32[]{:S(2)}) collective-permute-start(bf16[64,1024]{1,0:T(8,128)(2,1)S(1)} %dynamic-slice_bitcast_fusion.12), channel_id=1, source_target_pairs={{0,16},{2,18},{4,20},{6,22},{8,24},{10,26},{12,28},{14,30},{16,0},... | collective-permute-start | bytes 393224 | tf_op jit(solution)/shard_map/ppermute | solution.py:572
  319.6 8.3 %collective-permute-start.15 = (bf16[128,1024]{1,0:T(8,128)(2,1)S(1)}, bf16[128,1024]{1,0:T(8,128)(2,1)S(1)}, u32[]{:S(2)}, u32[]{:S(2)}) collective-permute-start(bf16[128,1024]{1,0:T(8,128)(2,1)S(1)} %dynamic-slice_bitcast_fusion.9), channel_id=1, source_target_pairs={{0,4},{2,6},{4,0},{6,2},{8,12},{10,14},{12,8},{14,10},{16,20},{18,... | collective-permute-start | bytes 786440 | tf_op jit(solution)/shard_map/ppermute | solution.py:572
  328.0 8.6 %collective-permute-start.17 = (bf16[64,1024]{1,0:T(8,128)(2,1)S(1)}, bf16[64,1024]{1,0:T(8,128)(2,1)S(1)}, u32[]{:S(2)}, u32[]{:S(2)}) collective-permute-start(bf16[64,1024]{1,0:T(8,128)(2,1)S(1)} %dynamic-slice_bitcast_fusion.11), channel_id=1, source_target_pairs={{0,16},{2,18},{4,20},{6,22},{8,24},{10,26},{12,28},{14,30},{16,0},... | collective-permute-start | bytes 393224 | tf_op jit(solution)/shard_map/ppermute | solution.py:572
  346.8 27.6 %collective-permute-start.19 = (bf16[1,2,64,1024]{3,2,1,0:T(8,128)(2,1)S(1)}, bf16[1,2,64,1024]{3,2,1,0:T(8,128)(2,1)S(1)}, u32[]{:S(2)}, u32[]{:S(2)}) collective-permute-start(bf16[1,2,64,1024]{3,2,1,0:T(8,128)(2,1)S(1)} %maximum_bitcast_fusion), channel_id=1, source_target_pairs={{0,16},{2,18},{4,20},{6,22},{8,24},{10,26},{12,28},{14,30},{16,0},... | collective-permute-start | bytes 786440 | tf_op jit(solution)/shard_map/ppermute | solution.py:576
  346.9 27.6 %collective-permute-start.20 = (bf16[1,2,64,1024]{3,2,1,0:T(8,128)(2,1)S(1)}, bf16[1,2,64,1024]{3,2,1,0:T(8,128)(2,1)S(1)}, u32[]{:S(2)}, u32[]{:S(2)}) collective-permute-start(bf16[1,2,64,1024]{3,2,1,0:T(8,128)(2,1)S(1)} %maximum_bitcast_fusion.1), channel_id=1, source_target_pairs={{0,16},{2,18},{4,20},{6,22},{8,24},{10,26},{12,28},{14,30},{16,0},... | collective-permute-start | bytes 786440 | tf_op jit(solution)/shard_map/ppermute | solution.py:576
  353.9 18.8 %collective-permute-start.22 = (f32[80,128]{1,0:T(8,128)S(1)}, f32[80,128]{1,0:T(8,128)S(1)}, u32[]{:S(2)}, u32[]{:S(2)}) collective-permute-start(f32[80,128]{1,0:T(8,128)S(1)} %add.319), channel_id=1, source_target_pairs={{0,16},{2,18},{4,20},{6,22},{8,24},{10,26},{12,28},{14,30},{16,0},... | collective-permute-start | bytes 122888 | tf_op jit(solution)/shard_map/ppermute | solution.py:665
  372.7 25.1 %collective-permute-start.29 = (bf16[512,1024]{1,0:T(8,128)(2,1)S(1)}, bf16[512,1024]{1,0:T(8,128)(2,1)S(1)}, u32[]{:S(2)}, u32[]{:S(2)}) collective-permute-start(bf16[512,1024]{1,0:T(8,128)(2,1)S(1)} %get-tuple-element.112), channel_id=1, source_target_pairs={{0,1},{1,0},{2,3},{3,2},{4,5},{5,4},{6,7},{7,6},{8,9},{9,8},{10,11... | collective-permute-start | bytes 3145736 | tf_op jit(solution)/shard_map/ppermute | solution.py:660
  374.6 14.6 %collective-permute-start.23 = (bf16[2,2,64,1024]{3,2,1,0:T(8,128)(2,1)S(1)}, bf16[2,2,64,1024]{3,2,1,0:T(8,128)(2,1)S(1)}, u32[]{:S(2)}, u32[]{:S(2)}) collective-permute-start(bf16[2,2,64,1024]{3,2,1,0:T(8,128)(2,1)S(1)} %pad_maximum_fusion.6), channel_id=1, source_target_pairs={{0,8},{2,10},{4,12},{6,14},{8,0},{10,2},{12,4},{14,6},{16,24},{18,... | collective-permute-start | bytes 1572872 | tf_op jit(solution)/shard_map/ppermute | solution.py:576
  374.7 14.6 %collective-permute-start.24 = (bf16[2,2,64,1024]{3,2,1,0:T(8,128)(2,1)S(1)}, bf16[2,2,64,1024]{3,2,1,0:T(8,128)(2,1)S(1)}, u32[]{:S(2)}, u32[]{:S(2)}) collective-permute-start(bf16[2,2,64,1024]{3,2,1,0:T(8,128)(2,1)S(1)} %pad_maximum_fusion.7), channel_id=1, source_target_pairs={{0,4},{2,6},{4,0},{6,2},{8,12},{10,14},{12,8},{14,10},{16,20},{18,... | collective-permute-start | bytes 1572872 | tf_op jit(solution)/shard_map/ppermute | solution.py:576
  375.4 13.8 %collective-permute-start.25 = (f32[80,128]{1,0:T(8,128)S(1)}, f32[80,128]{1,0:T(8,128)S(1)}, u32[]{:S(2)}, u32[]{:S(2)}) collective-permute-start(f32[80,128]{1,0:T(8,128)S(1)} %add.320), channel_id=1, source_target_pairs={{0,4},{2,6},{4,0},{6,2},{8,12},{10,14},{12,8},{14,10},{16,20},{18,... | collective-permute-start | bytes 122888 | tf_op jit(solution)/shard_map/ppermute | solution.py:665
  391.2 23.4 %collective-permute-start.26 = (bf16[4,2,64,1024]{3,2,1,0:T(8,128)(2,1)S(1)}, bf16[4,2,64,1024]{3,2,1,0:T(8,128)(2,1)S(1)}, u32[]{:S(2)}, u32[]{:S(2)}) collective-permute-start(bf16[4,2,64,1024]{3,2,1,0:T(8,128)(2,1)S(1)} %pad_maximum_fusion.4), channel_id=1, source_target_pairs={{0,4},{2,6},{4,0},{6,2},{8,12},{10,14},{12,8},{14,10},{16,20},{18,... | collective-permute-start | bytes 3145736 | tf_op jit(solution)/shard_map/ppermute | solution.py:576
  391.8 23.5 %collective-permute-start.27 = (bf16[4,2,64,1024]{3,2,1,0:T(8,128)(2,1)S(1)}, bf16[4,2,64,1024]{3,2,1,0:T(8,128)(2,1)S(1)}, u32[]{:S(2)}, u32[]{:S(2)}) collective-permute-start(bf16[4,2,64,1024]{3,2,1,0:T(8,128)(2,1)S(1)} %pad_maximum_fusion.5), channel_id=1, source_target_pairs={{0,8},{2,10},{4,12},{6,14},{8,0},{10,2},{12,4},{14,6},{16,24},{18,... | collective-permute-start | bytes 3145736 | tf_op jit(solution)/shard_map/ppermute | solution.py:576
  416.9 8.6 %collective-permute-start.31 = (bf16[8,2,64,1024]{3,2,1,0:T(8,128)(2,1)S(1)}, bf16[8,2,64,1024]{3,2,1,0:T(8,128)(2,1)}, u32[]{:S(2)}, u32[]{:S(2)}) collective-permute-start(bf16[8,2,64,1024]{3,2,1,0:T(8,128)(2,1)S(1)} %pad_maximum_fusion.near_one.near_a.near_b), channel_id=1, source_target_pairs={{0,2},{2,0},{4,6},{6,4},{8,10},{10,8},{12,14},{14,12},{16,18},{18,... | collective-permute-start | bytes 6291464 | tf_op jit(solution)/shard_map/ppermute | solution.py:686
  416.9 8.5 %collective-permute-start.32 = (bf16[8,2,64,1024]{3,2,1,0:T(8,128)(2,1)}, bf16[8,2,64,1024]{3,2,1,0:T(8,128)(2,1)}, u32[]{:S(2)}, u32[]{:S(2)}) collective-permute-start(bf16[8,2,64,1024]{3,2,1,0:T(8,128)(2,1)} %pad_maximum_fusion.1.near_two), channel_id=1, source_target_pairs={{0,2},{2,0},{4,6},{6,4},{8,10},{10,8},{12,14},{14,12},{16,18},{18,... | collective-permute-start | bytes 6291464 | tf_op jit(solution)/shard_map/ppermute | solution.py:684
  (47 other events, 303.1 us)
Sparse Core Ops, SparseCore 0:
  137.3 125.5 reduce-scatter.1
  278.2 53.2 all-gather.1
